TPU v7x, 32 devices: a whole 2x2x4 slice. The times are simulated.
32 devices in a mesh: row: 2 (over x), col: 16 (over z, y, core).
Axes of the slice: x: 2, y: 2, z: 4, core: 2. Of those that a mesh axis runs over, the one named last changes fastest.
Arguments:
- tokens: bfloat16 [4096, 1024], P(('row', 'col')), may hold values from -6 to 6
- variate_ids: int32 [4096], P(('row', 'col')), may hold values from 0 to 3
- time_ids: int32 [4096], P(('row', 'col')), may hold values from 0 to 1023
- lengths: int32 [2, 6], P('row'), may hold values from 1 to 8, 16 in all within a row
- deal: int32 [2, 16, 16], P('row', 'col'), may hold values from 0 to 15, each once within a row
- w_qkv: bfloat16 [1024, 3072], P(('row', 'col')), may hold values from -0.1875 to 0.1875
- w_out: bfloat16 [1024, 1024], P(('row', 'col')), may hold values from -3 to 3
- w_gate_up: bfloat16 [1024, 8192], P(('row', 'col')), may hold values from -0.1875 to 0.1875
- w_down: bfloat16 [4096, 1024], P(('row', 'col')), may hold values from -0.09375 to 0.09375
- gain_attn: bfloat16 [1024], P(('row', 'col')), may hold values from 0.5 to 1.5
- gain_ffn: bfloat16 [1024], P(('row', 'col')), may hold values from 0.5 to 1.5
- var_bias: float32 [2, 16], replicated, may hold values from -3 to 3
- cotangent: bfloat16 [4096, 1024], P(('row', 'col')), may hold values from -6 to 6
Outputs:
- output: bfloat16 [4096, 1024], P(('row', 'col'))
- grad_tokens: bfloat16 [4096, 1024], P(('row', 'col'))
- grad_w_qkv: float32 [1024, 3072], P(('row', 'col'))
- grad_w_out: float32 [1024, 1024], P(('row', 'col'))
- grad_w_gate_up: float32 [1024, 8192], P(('row', 'col'))
- grad_w_down: float32 [4096, 1024], P(('row', 'col'))
- grad_gain_attn: float32 [1024], P(('row', 'col'))
- grad_gain_ffn: float32 [1024], P(('row', 'col'))
- grad_var_bias: float32 [2, 16], replicated
All inputs are finite; a program needn't handle non-finite values.
Results may differ from a plain program's by a relative error of at most 0.018.
The roundings to bfloat16 on the way count: a program that leaves them out, or rounds other values in their place, can miss the bound.
Values may be sent and summed in bfloat16 or wider, within the bound.
A program may use at most 320 MiB of HBM per device.

v0:
```python
import math

import jax
import jax.numpy as jnp
from jax import lax
from jax.sharding import PartitionSpec as P

HEAD_DIM = 64
UNIT = 128
KEY_BLOCK = 1024


epsilon = 1e-05


def contract_rows(operand, factor):
    return lax.dot_general(
        operand, factor, (((0,), (0,)), ((), ())), preferred_element_type=jnp.float32
    )


def contract_cols(operand, factor):
    return lax.dot_general(
        operand, factor, (((1,), (1,)), ((), ())), preferred_element_type=jnp.float32
    )


def angles(time_ids):
    half_dim = HEAD_DIM // 2
    inverse_freq = jnp.exp(-math.log(10000.0) * jnp.arange(half_dim, dtype=jnp.float32) / half_dim)
    phases = time_ids.astype(jnp.float32)[:, None] * inverse_freq[None, :]
    return (jnp.cos(phases)[:, None, :], jnp.sin(phases)[:, None, :])


def rotate(tensor, cos_part, sin_part):
    half_dim = tensor.shape[-1] // 2
    former = tensor[..., :half_dim]
    latter = tensor[..., half_dim:]
    return jnp.concatenate(
        [former * cos_part - latter * sin_part, latter * cos_part + former * sin_part], axis=-1
    )


def unrotate(tensor, cos_part, sin_part):
    half_dim = tensor.shape[-1] // 2
    former = tensor[..., :half_dim]
    latter = tensor[..., half_dim:]
    return jnp.concatenate(
        [former * cos_part + latter * sin_part, latter * cos_part - former * sin_part], axis=-1
    )


def norm_scale(values):
    return lax.rsqrt(jnp.mean(values * values, axis=-1, keepdims=True) + epsilon)


def norm_back(d_normed, normed, scale):
    return scale * (d_normed - normed * jnp.mean(d_normed * normed, axis=-1, keepdims=True))


def score_weights(queries, query_seq, query_var, key_block, seq_block, var_block, var_bias):
    scores = (
        jnp.einsum("qhd,khd->hqk", queries, key_block, preferred_element_type=jnp.float32) * 0.125
    )
    matched = query_var[:, None] == var_block[None, :]
    scores = scores + jnp.where(
        matched[None], var_bias[0][:, None, None], var_bias[1][:, None, None]
    )
    within = query_seq[:, None] == seq_block[None, :]
    return (jnp.where(within[None], jnp.exp(scores), 0.0), matched)


def shards(
    tokens,
    variate_ids,
    time_ids,
    lengths,
    deal,
    w_qkv,
    w_out,
    w_gate_up,
    w_down,
    gain_attn,
    gain_ffn,
    var_bias,
    cotangent,
):
    tok_rows, model_width = tokens.shape
    n_col = lax.axis_size("col")
    col_index = lax.axis_index("col")
    piece_len = tok_rows // n_col
    head_count = model_width // HEAD_DIM
    bounds = jnp.cumsum(lengths[0]) * UNIT
    position = col_index * tok_rows + jnp.arange(tok_rows, dtype=jnp.int32)
    seq_own = jnp.sum((position[:, None] >= bounds[None, :]).astype(jnp.int32), axis=1)
    target = deal[0, 0]
    slots = jnp.arange(n_col, dtype=jnp.int32)
    inverse = jnp.sum(
        slots[:, None] * (target[:, None] == slots[None, :]).astype(jnp.int32), axis=0
    )
    send_rows = jnp.take(tokens.reshape(n_col, piece_len, model_width), inverse, axis=0)
    labels = jnp.stack(
        [
            seq_own.reshape(n_col, piece_len),
            variate_ids.reshape(n_col, piece_len),
            time_ids.reshape(n_col, piece_len),
        ],
        axis=1,
    )
    send_labels = jnp.take(labels, inverse, axis=0)
    got_rows, got_labels = (
        lax.all_to_all(send_rows, "col", split_axis=0, concat_axis=0, tiled=True),
        lax.all_to_all(send_labels, "col", split_axis=0, concat_axis=0, tiled=True),
    )
    inputs = got_rows.reshape(tok_rows, model_width).astype(jnp.float32)
    seq_q = got_labels[:, 0, :].reshape(tok_rows)
    var_q = got_labels[:, 1, :].reshape(tok_rows)
    cos_part, sin_part = angles(got_labels[:, 2, :].reshape(tok_rows))
    qkv_full, out_full, gate_up_full, down_full, gain_one, gain_two = (
        lax.all_gather(w_qkv, ("row", "col"), axis=0, tiled=True),
        lax.all_gather(w_out, ("row", "col"), axis=0, tiled=True),
        lax.all_gather(w_gate_up, ("row", "col"), axis=0, tiled=True),
        lax.all_gather(w_down, ("row", "col"), axis=0, tiled=True),
        lax.all_gather(gain_attn, ("row", "col"), axis=0, tiled=True),
        lax.all_gather(gain_ffn, ("row", "col"), axis=0, tiled=True),
    )
    scale_one = norm_scale(inputs)
    normed_one = inputs * scale_one
    scaled_one = (normed_one * gain_one.astype(jnp.float32)).astype(jnp.bfloat16)
    projected = jnp.dot(scaled_one, qkv_full, preferred_element_type=jnp.float32)
    shaped = projected.reshape(tok_rows, 3, head_count, HEAD_DIM)
    queries = rotate(shaped[:, 0], cos_part, sin_part).astype(jnp.bfloat16)
    key_own = (
        rotate(shaped[:, 1], cos_part, sin_part).astype(jnp.bfloat16).reshape(tok_rows, model_width)
    )
    value_own = projected[:, 2 * model_width :].astype(jnp.bfloat16)
    keys_all, values_all, seq_k, var_k = (
        lax.all_gather(key_own, "col", axis=0, tiled=True),
        lax.all_gather(value_own, "col", axis=0, tiled=True),
        lax.all_gather(seq_q, "col", axis=0, tiled=True),
        lax.all_gather(var_q, "col", axis=0, tiled=True),
    )
    group_size = keys_all.shape[0]
    stride = min(KEY_BLOCK, group_size)
    block_count = group_size // stride

    def split_blocks(key_rows, value_rows, key_seq, key_var):
        return (
            key_rows.reshape(block_count, stride, head_count, HEAD_DIM),
            value_rows.reshape(block_count, stride, head_count, HEAD_DIM),
            key_seq.reshape(block_count, stride),
            key_var.reshape(block_count, stride),
        )

    def forward_step(running, block_data):
        denominator, numerator = running
        key_block, value_block, seq_block, var_block = block_data
        weights = score_weights(queries, seq_q, var_q, key_block, seq_block, var_block, var_bias)[0]
        denominator = denominator + jnp.sum(weights, axis=-1)
        numerator = numerator + jnp.einsum(
            "hqk,khd->qhd",
            weights.astype(jnp.bfloat16),
            value_block,
            preferred_element_type=jnp.float32,
        )
        return ((denominator, numerator), None)

    (denominator, numerator), unused = lax.scan(
        forward_step,
        (
            jnp.zeros((head_count, tok_rows), jnp.float32),
            jnp.zeros((tok_rows, head_count, HEAD_DIM), jnp.float32),
        ),
        split_blocks(keys_all, values_all, seq_k, var_k),
    )
    attended = numerator / denominator.T[:, :, None]
    attn_low = attended.reshape(tok_rows, model_width).astype(jnp.bfloat16)
    hidden_state = inputs + jnp.dot(attn_low, out_full, preferred_element_type=jnp.float32)
    scale_two = norm_scale(hidden_state)
    normed_two = hidden_state * scale_two
    scaled_two = (normed_two * gain_two.astype(jnp.float32)).astype(jnp.bfloat16)
    gate_up = jnp.dot(scaled_two, gate_up_full, preferred_element_type=jnp.float32)
    hidden_units = gate_up_full.shape[1] // 2
    gate_part = gate_up[:, :hidden_units]
    upper_part = gate_up[:, hidden_units:]
    sigmoid_gate = jax.nn.sigmoid(gate_part)
    active = gate_part * sigmoid_gate
    inner_act = (active * upper_part).astype(jnp.bfloat16)
    ffn_branch = jnp.dot(inner_act, down_full, preferred_element_type=jnp.float32)
    output = (hidden_state + ffn_branch).astype(jnp.bfloat16)
    qkv_back, out_back, gate_up_back, down_back, gain_one_back, gain_two_back = (
        lax.all_gather(w_qkv, ("row", "col"), axis=0, tiled=True),
        lax.all_gather(w_out, ("row", "col"), axis=0, tiled=True),
        lax.all_gather(w_gate_up, ("row", "col"), axis=0, tiled=True),
        lax.all_gather(w_down, ("row", "col"), axis=0, tiled=True),
        lax.all_gather(gain_attn, ("row", "col"), axis=0, tiled=True),
        lax.all_gather(gain_ffn, ("row", "col"), axis=0, tiled=True),
    )
    d_inner = contract_cols(cotangent, down_back)
    d_gate = (
        d_inner * upper_part * sigmoid_gate * (1.0 + gate_part * (1.0 - sigmoid_gate))
    ).astype(jnp.bfloat16)
    d_upper = (d_inner * active).astype(jnp.bfloat16)
    d_gate_up = jnp.concatenate([d_gate, d_upper], axis=1)
    d_scaled_two = contract_cols(d_gate_up, gate_up_back)
    term_gain_two = jnp.sum(d_scaled_two * normed_two, axis=0)
    term_gate_up = contract_rows(scaled_two, d_gate_up)
    term_down = contract_rows(inner_act, cotangent)
    d_hidden = cotangent.astype(jnp.float32) + norm_back(
        d_scaled_two * gain_two_back.astype(jnp.float32), normed_two, scale_two
    )
    d_branch = d_hidden.astype(jnp.bfloat16)
    term_out = contract_rows(attn_low, d_branch)
    d_attended = contract_cols(d_branch, out_back).reshape(tok_rows, head_count, HEAD_DIM)
    d_numerator = (d_attended / denominator.T[:, :, None]).astype(jnp.bfloat16)
    centre = (jnp.sum(d_attended * attended, axis=-1) / denominator.T).T
    back_keys = (
        lax.all_gather(key_own, "col", axis=0, tiled=True),
        lax.all_gather(value_own, "col", axis=0, tiled=True),
        lax.all_gather(seq_q, "col", axis=0, tiled=True),
        lax.all_gather(var_q, "col", axis=0, tiled=True),
    )

    def query_step(running, block_data):
        d_queries, same_sum, other_sum = running
        key_block, value_block, seq_block, var_block = block_data
        weights, matched = score_weights(
            queries, seq_q, var_q, key_block, seq_block, var_block, var_bias
        )
        d_probs = jnp.einsum(
            "qhd,khd->hqk", d_numerator, value_block, preferred_element_type=jnp.float32
        )
        d_scores = weights * (d_probs - centre[:, :, None])
        same_sum = same_sum + jnp.sum(jnp.where(matched[None], d_scores, 0.0), axis=(1, 2))
        other_sum = other_sum + jnp.sum(jnp.where(matched[None], 0.0, d_scores), axis=(1, 2))
        d_rounded = d_scores.astype(jnp.bfloat16)
        d_queries = d_queries + jnp.einsum(
            "hqk,khd->qhd", d_rounded, key_block, preferred_element_type=jnp.float32
        )
        return ((d_queries, same_sum, other_sum), (d_rounded, weights.astype(jnp.bfloat16)))

    def query_and_key_step(running, block_data):
        running, rounded = query_step(running, block_data)
        d_rounded, weights_low = rounded
        d_keys = (
            jnp.einsum("hqk,qhd->khd", d_rounded, queries, preferred_element_type=jnp.float32)
            * 0.125
        )
        d_values = jnp.einsum(
            "hqk,qhd->khd", weights_low, d_numerator, preferred_element_type=jnp.float32
        )
        return (running, (d_keys, d_values))

    start_running = (
        jnp.zeros((tok_rows, head_count, HEAD_DIM), jnp.float32),
        jnp.zeros((head_count,), jnp.float32),
        jnp.zeros((head_count,), jnp.float32),
    )
    (d_queries, same_sum, other_sum), (d_keys, d_values) = lax.scan(
        query_and_key_step,
        start_running,
        split_blocks(back_keys[0], back_keys[1], back_keys[2], back_keys[3]),
    )
    key_grad, value_grad = (
        lax.psum_scatter(
            d_keys.reshape(group_size, model_width).astype(jnp.bfloat16),
            "col",
            scatter_dimension=0,
            tiled=True,
        ).astype(jnp.float32),
        lax.psum_scatter(
            d_values.reshape(group_size, model_width).astype(jnp.bfloat16),
            "col",
            scatter_dimension=0,
            tiled=True,
        ).astype(jnp.float32),
    )
    d_query_pre = unrotate(d_queries * 0.125, cos_part, sin_part).reshape(tok_rows, model_width)
    d_key_pre = unrotate(
        key_grad.reshape(tok_rows, head_count, HEAD_DIM), cos_part, sin_part
    ).reshape(tok_rows, model_width)
    d_projected = jnp.concatenate([d_query_pre, d_key_pre, value_grad], axis=1).astype(jnp.bfloat16)
    d_scaled_one = contract_cols(d_projected, qkv_back)
    term_qkv = contract_rows(scaled_one, d_projected)
    term_gain_one = jnp.sum(d_scaled_one * normed_one, axis=0)
    grad_w_qkv, grad_w_out, grad_w_gate_up, grad_w_down, grad_gain_attn, grad_gain_ffn = (
        lax.psum_scatter(term_qkv, ("row", "col"), scatter_dimension=0, tiled=True),
        lax.psum_scatter(term_out, ("row", "col"), scatter_dimension=0, tiled=True),
        lax.psum_scatter(term_gate_up, ("row", "col"), scatter_dimension=0, tiled=True),
        lax.psum_scatter(term_down, ("row", "col"), scatter_dimension=0, tiled=True),
        lax.psum_scatter(term_gain_one, ("row", "col"), scatter_dimension=0, tiled=True),
        lax.psum_scatter(term_gain_two, ("row", "col"), scatter_dimension=0, tiled=True),
    )
    grad_var_bias = lax.psum(jnp.stack([same_sum, other_sum], axis=0), ("row", "col"))
    d_inputs = d_hidden + norm_back(
        d_scaled_one * gain_one_back.astype(jnp.float32), normed_one, scale_one
    )
    returned = lax.all_to_all(
        d_inputs.astype(jnp.bfloat16).reshape(n_col, piece_len, model_width),
        "col",
        split_axis=0,
        concat_axis=0,
        tiled=True,
    )
    grad_tokens = jnp.take(returned, target, axis=0).reshape(tok_rows, model_width)
    return (
        output,
        grad_tokens,
        grad_w_qkv,
        grad_w_out,
        grad_w_gate_up,
        grad_w_down,
        grad_gain_attn,
        grad_gain_ffn,
        grad_var_bias,
    )


def solution(mesh):
    return jax.shard_map(
        shards,
        mesh=mesh,
        in_specs=(
            P(("row", "col"), None),
            P(("row", "col")),
            P(("row", "col")),
            P("row", None),
            P("row", "col", None),
            P(("row", "col"), None),
            P(("row", "col"), None),
            P(("row", "col"), None),
            P(("row", "col"), None),
            P(("row", "col")),
            P(("row", "col")),
            P(),
            P(("row", "col"), None),
        ),
        out_specs=(
            P(("row", "col"), None),
            P(("row", "col"), None),
            P(("row", "col"), None),
            P(("row", "col"), None),
            P(("row", "col"), None),
            P(("row", "col"), None),
            P(("row", "col")),
            P(("row", "col")),
            P(),
        ),
        check_vma=False,
    )
```

profile of v0, /device:TPU:0, one launch (start us, length us, event | category | flops | bytes accessed | tf_op | source)
XLA Modules:
  0.0 1546.0 jit_solution(3545822266853017098)
XLA Ops:
  12.5 7.4 all-to-all-start.1
  31.9 42.2 %all-reduce.5 = (bf16[1024]{0:T(1024)(128)(2,1)S(1)}, bf16[1024]{0:T(1024)(128)(2,1)S(1)}) all-reduce(bf16[1024]{0:T(1024)(128)(2,1)S(1)} %dynamic-update-slice, bf16[1024]{0:T(1024)(128)(2,1)S(1)} %dynamic-update-slice.1), channel_id=1, replica_groups=mesh['row'=2,'col'=16] {'row','col'}, use_global_device_ids=true, to_apply=%add | all-reduce | flops 2048 | bytes 8192
  74.6 10.9 all-gather.9.cloned.1.call-done
  96.5 19.8 %all-gather = s32[16,1,128]{2,1,0:T(1,128)S(1)} all-gather(s32[1,1,128]{2,1,0:T(1,128)S(1)} %reshape.400), channel_id=1, replica_groups=mesh['row'=2,'col'=16] {'col'}, dimensions={0}, use_global_device_ids=true | all-gather | bytes 8704 | tf_op jit(solution)/shard_map/all_gather | solution.py:140
  117.6 17.9 %all-gather.1 = s32[16,1,128]{2,1,0:T(1,128)S(1)} all-gather(s32[1,1,128]{2,1,0:T(1,128)S(1)} %reshape.402), channel_id=1, replica_groups=mesh['row'=2,'col'=16] {'col'}, dimensions={0}, use_global_device_ids=true | all-gather | bytes 8704 | tf_op jit(solution)/shard_map/all_gather | solution.py:141
  136.2 9.0 all-gather.11.cloned.1.call-done
  145.2 7.9 reshape.357
  158.7 38.1 %all-gather.13.cloned.1.call-done = bf16[2048,1024]{1,0:T(8,128)(2,1)} async-done(((bf16[128,1024]{1,0:T(8,128)(2,1)}), bf16[2048,1024]{1,0:T(8,128)(2,1)}) %all-gather.13.cloned.1.call-update) | async-done | bytes 4194320 | tf_op jit(solution)/shard_map/all_gather | solution.py:139
  196.9 11.6 reshape.416
  208.5 9.8 copy.85
  218.3 31.6 %while.34 = (s32[]{:T(128)}, f32[16,128]{1,0:T(8,128)S(1)}, f32[128,16,64]{0,2,1:T(8,128)S(1)}, s32[16,1,8]{2,0,1:T(8,128)}, s32[2,1024]{1,0:T(2,128)S(1)}, /*in...) while((s32[]{:T(128)}, f32[16,128]{1,0:T(8,128)S(1)}, ...), condition=%wide.wide.region_6.8_spmd.clone, body=%wide.wide.region_4.7_spmd.clone.sunk | while | flops 558368768 | bytes 23127724 | solution.py:168
  218.7 8.7 fusion.161
  234.4 8.7 fusion.161
  256.7 114.3 %all-gather.17.cloned.1.call-done = bf16[1024,8192]{1,0:T(8,128)(2,1)} async-done(((bf16[32,8192]{1,0:T(8,128)(2,1)}), bf16[1024,8192]{1,0:T(8,128)(2,1)}) %all-gather.17.cloned.1.call-update) | async-done | bytes 16777232 | tf_op jit(solution)/shard_map/all_gather | solution.py:122
  371.1 10.2 fusion.99
  381.2 68.3 %all-gather.19.cloned.1.call-done = bf16[4096,1024]{1,0:T(8,128)(2,1)} async-done(((bf16[128,1024]{1,0:T(8,128)(2,1)}), bf16[4096,1024]{1,0:T(8,128)(2,1)}) %all-gather.19.cloned.1.call-update) | async-done | bytes 8388624 | tf_op jit(solution)/shard_map/all_gather | solution.py:123
  449.6 9.1 multiply_convert_fusion.1
  458.7 13.5 multiply_reduce_fusion
  476.6 46.4 %while.35 = (s32[]{:T(128)}, f32[128,16,64]{0,2,1:T(8,128)S(1)}, f32[16]{0:T(128)S(1)}, f32[16]{0:T(128)S(1)}, bf16[2,1024,16,64]{1,3,2,0:T(8,128)(2,1)}, /*inde...) while((s32[]{:T(128)}, f32[128,16,64]{0,2,1:T(8,128)S(1)}, ...), condition=%wide.wide.region_13.15_spmd.clone, body=%wide.wide.region_10.14_spmd.clone.sunk | while | flops 1377304576 | bytes 158108944 | solution.py:259
  523.0 10.9 copy.104
  533.9 11.9 reshape.412
  545.9 11.3 copy.105
  557.1 12.0 reshape.414
  573.9 43.1 %reduce-scatter.19.cloned.1.call-done = bf16[128,1024]{1,0:T(8,128)(2,1)} async-done(((bf16[2048,1024]{1,0:T(8,128)(2,1)}), bf16[128,1024]{1,0:T(8,128)(2,1)}) %reduce-scatter.19.cloned.1.call-update) | async-done | bytes 262160
  618.1 74.8 %reduce-scatter.21.cloned.1.call-done = bf16[128,1024]{1,0:T(8,128)(2,1)} async-done(((bf16[2048,1024]{1,0:T(8,128)(2,1)}), bf16[128,1024]{1,0:T(8,128)(2,1)}) %reduce-scatter.21.cloned.1.call-update) | async-done | bytes 262160
  702.6 8.1 fusion.100
  710.8 14.8 fusion.66
  741.6 41.3 %all-reduce.4 = (f32[1024]{0:T(1024)S(1)}, f32[1024]{0:T(1024)S(1)}, f32[2,16]{1,0:T(2,128)}) all-reduce(f32[1024]{0:T(1024)S(1)} %get-tuple-element.360, f32[1024]{0:T(1024)S(1)} %copy-done.25, f32[2,16]{1,0:T(2,128)S(1)} %pad_maximum_fusion.10), channel_id=8, replica_groups=mesh['row'=2,'col'=16] {'row','col'}, use_global_device_ids=true, to_apply=%region_22.24.clone | all-reduce | flops 2080 | bytes 16640
  785.4 51.2 %reduce-scatter.13.cloned.1.call-done = f32[32,1024]{1,0:T(8,128)} async-done(((f32[1024,1024]{1,0:T(8,128)}), f32[32,1024]{1,0:T(8,128)}) %reduce-scatter.13.cloned.1.call-update) | async-done | bytes 131088 | tf_op jit(solution)/shard_map/reduce_scatter | solution.py:288
  836.6 158.3 %reduce-scatter.11.cloned.1.call-done = f32[32,3072]{1,0:T(8,128)} async-done(((f32[1024,3072]{1,0:T(8,128)}), f32[32,3072]{1,0:T(8,128)}) %reduce-scatter.11.cloned.1.call-update) | async-done | bytes 393232 | tf_op jit(solution)/shard_map/reduce_scatter | solution.py:287
  994.9 186.0 %reduce-scatter.17.cloned.1.call-done = f32[128,1024]{1,0:T(8,128)} async-done(((f32[4096,1024]{1,0:T(8,128)}), f32[128,1024]{1,0:T(8,128)}) %reduce-scatter.17.cloned.1.call-update) | async-done | bytes 524304 | tf_op jit(solution)/shard_map/reduce_scatter | solution.py:290
  1180.9 357.8 %reduce-scatter.15.cloned.1.call-done = f32[32,8192]{1,0:T(8,128)} async-done(((f32[1024,8192]{1,0:T(8,128)}), f32[32,8192]{1,0:T(8,128)}) %reduce-scatter.15.cloned.1.call-update) | async-done | bytes 1048592 | tf_op jit(solution)/shard_map/reduce_scatter | solution.py:289
  (216 shorter events, 141.3 us)
Async XLA Ops:
  7.2 12.8 copy-start
  7.2 78.4 %all-gather.9.cloned.1.call-start = ((), (), s32[]{:S(2)}) async-start(), calls=%async_computation.9 | async-start | bytes 6488064 | tf_op jit(solution)/shard_map/all_gather | solution.py:120
  12.5 14.0 all-to-all-start.1
  26.6 47.8 %all-to-all-start = ((bf16[16,8,1024]{2,1,0:T(8,128)(2,1)}), bf16[16,8,1024]{2,1,0:T(8,128)(2,1)S(1)}, u32[]{:S(2)}, u32[]{:S(2)}) async-start(bf16[16,8,1024]{2,1,0:T(8,128)(2,1)} %broadcast_select_fusion.2), calls=%async_computation | async-start | bytes 524288 | tf_op jit(solution)/shard_map/all_to_all | solution.py:112
  30.1 115.1 %all-gather.11.cloned.1.call-start = ((), (), s32[]{:S(2)}) async-start(), calls=%async_computation.10 | async-start | bytes 4456448 | tf_op jit(solution)/shard_map/all_gather | solution.py:138
  74.1 15.3 copy-start.12
  74.3 18.0 %copy-start.16 = (f32[128,32]{0,1:T(8,128)}, f32[128,32]{0,1:T(8,128)S(1)}, u32[]{:S(2)}) copy-start(f32[128,32]{0,1:T(8,128)S(1)} %get-tuple-element.455) | copy-start | bytes 49156
  74.4 18.0 %copy-start.18 = (f32[128,32]{0,1:T(8,128)}, f32[128,32]{0,1:T(8,128)S(1)}, u32[]{:S(2)}) copy-start(f32[128,32]{0,1:T(8,128)S(1)} %get-tuple-element.456) | copy-start | bytes 49156
  74.6 14.8 copy-start.23
  93.3 103.6 %all-gather.13.cloned.1.call-start = ((), (), s32[]{:S(2)}) async-start(), calls=%async_computation.11 | async-start | bytes 4456448 | tf_op jit(solution)/shard_map/all_gather | solution.py:139
  94.1 160.5 %all-gather.15.cloned.1.call-start = ((), (), s32[]{:S(2)}) async-start(), calls=%async_computation.12 | async-start | bytes 2162688 | tf_op jit(solution)/shard_map/all_gather | solution.py:121
  94.7 276.4 %all-gather.17.cloned.1.call-start = ((), (), s32[]{:S(2)}) async-start(), calls=%async_computation.13 | async-start | bytes 17301504 | tf_op jit(solution)/shard_map/all_gather | solution.py:122
  95.3 354.3 %all-gather.19.cloned.1.call-start = ((), (), s32[]{:S(2)}) async-start(), calls=%async_computation.14 | async-start | bytes 8650752 | tf_op jit(solution)/shard_map/all_gather | solution.py:123
  95.8 521.1 %reduce-scatter.19.cloned.1.call-start = ((), (), s32[]{:S(2)}) async-start(), calls=%async_computation.19 | async-start | bytes 4456448
  96.0 57.0 %copy-start.21 = (s32[16,1,8]{2,1,0:T(1,128)}, s32[16,1,8]{2,1,0:T(1,128)S(1)}, u32[]{:S(2)}) copy-start(s32[16,1,8]{2,1,0:T(1,128)S(1)} %get-tuple-element.449) | copy-start | bytes 1540
  96.0 57.0 %copy-start.22 = (s32[16,1,8]{2,1,0:T(1,128)}, s32[16,1,8]{2,1,0:T(1,128)S(1)}, u32[]{:S(2)}) copy-start(s32[16,1,8]{2,1,0:T(1,128)S(1)} %get-tuple-element.452) | copy-start | bytes 1540
  208.5 9.8 copy-start.20
  249.9 131.3 %copy-start.8 = (f32[128,16,64]{0,2,1:T(8,128)}, f32[128,16,64]{0,2,1:T(8,128)S(1)}, u32[]{:S(2)}) copy-start(f32[128,16,64]{0,2,1:T(8,128)S(1)} %get-tuple-element.154) | copy-start | bytes 1572868
  250.0 131.2 %copy-start.6 = (bf16[128,16,64]{0,2,1:T(8,128)(2,1)}, bf16[128,16,64]{0,2,1:T(8,128)(2,1)S(1)}, u32[]{:S(2)}) copy-start(bf16[128,16,64]{0,2,1:T(8,128)(2,1)S(1)} %fusion.85) | copy-start | bytes 786436
  371.0 78.5 %copy-start.10 = (bf16[128,1024]{1,0:T(8,128)(2,1)S(1)}, bf16[128,1024]{1,0:T(8,128)(2,1)}, u32[]{:S(2)}) copy-start(bf16[128,1024]{1,0:T(8,128)(2,1)} %param.31) | copy-start | bytes 786436
  480.2 7.5 copy-start.3
  545.8 147.1 %reduce-scatter.21.cloned.1.call-start = ((), (), s32[]{:S(2)}) async-start(), calls=%async_computation.20 | async-start | bytes 4456448
  569.2 267.4 %reduce-scatter.13.cloned.1.call-start = ((), (), s32[]{:S(2)}) async-start(), calls=%async_computation.16 | async-start | bytes 4325376 | tf_op jit(solution)/shard_map/reduce_scatter | solution.py:288
  572.9 121.1 %copy-start.17 = (f32[128,32]{0,1:T(8,128)S(1)}, f32[128,32]{0,1:T(8,128)}, u32[]{:S(2)}) copy-start(f32[128,32]{0,1:T(8,128)} %copy-done.16) | copy-start | bytes 49156
  572.9 121.1 %copy-start.19 = (f32[128,32]{0,1:T(8,128)S(1)}, f32[128,32]{0,1:T(8,128)}, u32[]{:S(2)}) copy-start(f32[128,32]{0,1:T(8,128)} %copy-done.18) | copy-start | bytes 49156
  572.9 122.3 %copy-start.13 = (f32[1024]{0:T(1024)S(1)}, f32[1024]{0:T(1024)}, u32[]{:S(2)}) copy-start(f32[1024]{0:T(1024)} %copy-done.12) | copy-start | bytes 12292
  572.9 122.3 %copy-start.24 = (f32[128]{0:T(128)S(1)}, f32[128]{0:T(128)}, u32[]{:S(2)}) copy-start(f32[128]{0:T(128)} %copy-done.23) | copy-start | bytes 1540
  573.0 421.9 %reduce-scatter.11.cloned.1.call-start = ((), (), s32[]{:S(2)}) async-start(), calls=%async_computation.15 | async-start | bytes 12976128 | tf_op jit(solution)/shard_map/reduce_scatter | solution.py:287
  701.7 479.2 %reduce-scatter.17.cloned.1.call-start = ((), (), s32[]{:S(2)}) async-start(), calls=%async_computation.18 | async-start | bytes 17301504 | tf_op jit(solution)/shard_map/reduce_scatter | solution.py:290
  710.7 828.0 %reduce-scatter.15.cloned.1.call-start = ((), (), s32[]{:S(2)}) async-start(), calls=%async_computation.17 | async-start | bytes 34603008 | tf_op jit(solution)/shard_map/reduce_scatter | solution.py:289
  732.4 51.7 %all-to-all-start.2 = ((bf16[16,8,1024]{2,1,0:T(8,128)(2,1)}), bf16[16,8,1024]{2,1,0:T(8,128)(2,1)S(1)}, u32[]{:S(2)}, u32[]{:S(2)}) async-start(bf16[16,8,1024]{2,1,0:T(8,128)(2,1)} %fusion.84), calls=%async_computation.2 | async-start | bytes 524288 | tf_op jit(solution)/shard_map/all_to_all | solution.py:298
  736.2 802.5 %copy-start.1 = (bf16[128,1024]{1,0:T(8,128)(2,1)S(1)}, bf16[128,1024]{1,0:T(8,128)(2,1)}, u32[]{:S(2)}) copy-start(bf16[128,1024]{1,0:T(8,128)(2,1)} %param.19) | copy-start | bytes 786436
  (16 other events, 57.1 us)
Sparse Core Ops, SparseCore 0:
  10.9 74.5 all-gather.8
  93.4 51.7 all-gather.10
  147.9 48.8 all-gather.12
  199.6 54.9 all-gather.14
  257.3 113.7 all-gather.16
  373.8 75.7 all-gather.18
  545.9 70.9 reduce-scatter.18
  621.3 71.5 reduce-scatter.20
  695.7 140.8 reduce-scatter.12
  843.0 151.8 reduce-scatter.10
  997.9 183.0 reduce-scatter.16
  1183.8 354.9 reduce-scatter.14
where the time goes:
time: 1560 us; the launch traced here: 1550 us
  waiting for transfers between devices  1120 us (72%)
  matrix products  157 us (10%)
  blocking collectives  121 us (8%)
  local copies, waits for them, and re-layouts  99.5 us (6%)
    reduce_scatter x1, waiting for transfers between devices, shards(): lax.psum_scatter(term_gate_up, ('row', 'col'), scatter_dimension=0, tiled...  358 us
    reduce_scatter x1, waiting for transfers between devices, shards(): lax.psum_scatter(term_down, ('row', 'col'), scatter_dimension=0, tiled=True)  186 us
    reduce_scatter x1, waiting for transfers between devices, shards(): lax.psum_scatter(term_qkv, ('row', 'col'), scatter_dimension=0, tiled=True)  158 us
    unnamed x14, waiting for transfers between devices  120 us
    all_gather x1, waiting for transfers between devices, shards(): lax.all_gather(w_gate_up, ('row', 'col'), axis=0, tiled=True)  114 us
    unnamed x2, blocking collectives  83.5 us
    unnamed x58, local copies, waits for them, and re-layouts  69.3 us
    all_gather x1, waiting for transfers between devices, shards(): lax.all_gather(w_down, ('row', 'col'), axis=0, tiled=True)  68.3 us
  transfers between devices with their start and end apart: 15, of which 13 were waited for; matrix products, arithmetic and copies ran while one was open for 11% of the time, Pallas kernels for 0%

commit v1 on v0

--- a/solution.py
+++ b/solution.py
@@ -3,11 +3,14 @@
 import jax
 import jax.numpy as jnp
 from jax import lax
+from jax.experimental import pallas as pl
+from jax.experimental.pallas import tpu as pltpu
 from jax.sharding import PartitionSpec as P
 
 HEAD_DIM = 64
 UNIT = 128
 KEY_BLOCK = 1024
+NSEQ = 6
 
 
 epsilon = 1e-05
@@ -316,9 +319,950 @@
     )
 
 
+PLANES = 4
+QUAD = 4
+MEMBERS = 8
+WINDOW = 512
+AUG = 128
+f32 = jnp.float32
+bf16 = jnp.bfloat16
+VM = pl.BlockSpec(memory_space=pltpu.VMEM)
+SM = pl.BlockSpec(memory_space=pltpu.SMEM)
+
+
+def mm(a, b):
+    return lax.dot_general(a, b, (((1,), (0,)), ((), ())), preferred_element_type=f32)
+
+
+def mm_nt(a, b):
+    return lax.dot_general(a, b, (((1,), (1,)), ((), ())), preferred_element_type=f32)
+
+
+def mm_tn(a, b):
+    return lax.dot_general(a, b, (((0,), (0,)), ((), ())), preferred_element_type=f32)
+
+
+def flip(value, bits):
+    for bit in (1, 2, 4, 8, 16):
+        if bits & bit:
+            value = value + bit * (1 - 2 * ((value // bit) % 2))
+    return value
+
+
+def places():
+    row = lax.axis_index("row")
+    col = lax.axis_index("col")
+    return row, col, col // QUAD, row * QUAD + col % QUAD
+
+
+def in_plane(row, col, bits):
+    return flip(row, bits // QUAD), flip(col, bits % QUAD)
+
+
+def on_line(row, col, bits):
+    return row, flip(col, bits * QUAD)
+
+
+def anyone(row, col, bits):
+    return flip(row, bits // 16), flip(col, bits % 16)
+
+
+def push(source, target, send, recv, device):
+    return pltpu.make_async_remote_copy(
+        src_ref=source,
+        dst_ref=target,
+        send_sem=send,
+        recv_sem=recv,
+        device_id={"row": device[0], "col": device[1]},
+        device_id_type=pl.DeviceIdType.MESH,
+    )
+
+
+def meet(devices):
+    barrier = pltpu.get_barrier_semaphore()
+    for device in devices:
+        pl.semaphore_signal(
+            barrier,
+            1,
+            device_id={"row": device[0], "col": device[1]},
+            device_id_type=pl.DeviceIdType.MESH,
+        )
+    pl.semaphore_wait(barrier, len(devices))
+
+
+NEAR = (2, 4, 6, 1)
+
+
+def plane_near(row, col):
+    return [in_plane(row, col, bits) for bits in NEAR]
+
+
+def line_all(row, col):
+    return [on_line(row, col, bits) for bits in (1, 2, 3)]
+
+
+def gather_start(source, target, send, recv, row, col, place):
+    copies = {}
+    for bits in NEAR:
+        copies[bits] = push(
+            source, target.at[place], send.at[bits], recv.at[bits], in_plane(row, col, bits)
+        )
+        copies[bits].start()
+    return copies
+
+
+def gather_finish(copies, target, send, recv, row, col, place):
+    onward = []
+    for bits in (2, 4, 6):
+        copies[bits].wait_recv()
+        slot = target.at[flip(place, bits)]
+        copy = push(slot, slot, send.at[bits + 1], recv.at[bits + 1], in_plane(row, col, 1))
+        copy.start()
+        onward.append(copy)
+    copies[1].wait_recv()
+    for copy in onward:
+        copy.wait_recv()
+    for copy in list(copies.values()) + onward:
+        copy.wait_send()
+
+
+def scatter_start(part, inbox, send, recv, row, col):
+    other = 1 - col % 2
+    copies = []
+    for i in range(4):
+        copy = push(
+            part.at[2 * i + other], inbox.at[i], send.at[i], recv.at[i], in_plane(row, col, 1)
+        )
+        copy.start()
+        copies.append(copy)
+    return copies
+
+
+def scatter_middle(copies, part, inbox, outbox, second, send, recv, row, col, place):
+    core = col % 2
+    for copy in copies:
+        copy.wait_recv()
+    sent = []
+    for bits in (1, 2, 3):
+        i = flip(place // 2, bits)
+        outbox[bits - 1] = (part[2 * i + core].astype(f32) + inbox[i].astype(f32)).astype(bf16)
+        copy = push(
+            outbox.at[bits - 1],
+            second.at[bits - 1],
+            send.at[3 + bits],
+            recv.at[3 + bits],
+            in_plane(row, col, 2 * bits),
+        )
+        copy.start()
+        sent.append(copy)
+    return sent
+
+
+def scatter_finish(copies, sent, part, inbox, second, place):
+    for copy in sent:
+        copy.wait_recv()
+    total = part[place].astype(f32) + inbox[place // 2].astype(f32)
+    for i in range(3):
+        total = total + second[i].astype(f32)
+    for copy in copies + sent:
+        copy.wait_send()
+    return total
+
+
+def scatter_scratch(rows, width):
+    return [
+        pltpu.VMEM((4, rows, width), bf16),
+        pltpu.VMEM((3, rows, width), bf16),
+        pltpu.VMEM((3, rows, width), bf16),
+        pltpu.SemaphoreType.DMA((7,)),
+        pltpu.SemaphoreType.DMA((7,)),
+    ]
+
+
+def gather_body(
+    x, wq, wo, wg, cot, tile,
+    xp, wqp, wop, wgp, cotr, tiles, gains, times, labels,
+    wqs, wgs, sx, rx, sq, rq, st, rt, sw, rw, sg, rg, sc, rc,
+):
+    row, col, z, place = places()
+    me = row * 16 + col
+    meet([anyone(row, col, bits) for bits in range(1, 32)])
+    for p in range(MEMBERS):
+        for part in range(3):
+            wqs[p, :, part * 128 : part * 128 + 128] = wq[
+                :, part * 1024 + p * 128 : part * 1024 + p * 128 + 128
+            ]
+    first = gather_start(x, xp, sx, rx, row, col, place)
+    spread = []
+    for bits in range(1, 32):
+        there = anyone(row, col, bits)
+        member = there[0] * QUAD + there[1] % QUAD
+        copy = push(wqs.at[member], wqp.at[me], sq.at[bits], rq.at[bits], there)
+        copy.start()
+        spread.append(copy)
+        copy = push(tile, tiles.at[me], st.at[bits], rt.at[bits], there)
+        copy.start()
+        spread.append(copy)
+    xp[place] = x[...]
+    wqp[me] = wqs[place]
+    tiles[me] = tile[...]
+    for p in range(MEMBERS):
+        for half in range(2):
+            for plane in range(PLANES):
+                unit = (p // QUAD) * 16 + plane * QUAD + p % QUAD
+                at = half * 512 + plane * 128
+                start = half * 4096 + unit * 128
+                wgs[p, :, at : at + 128] = wg[:, start : start + 128]
+    for bits in range(1, 8):
+        there = in_plane(row, col, bits)
+        copy = push(wgs.at[flip(place, bits)], wgp.at[place], sg.at[bits], rg.at[bits], there)
+        copy.start()
+        spread.append(copy)
+    wgp[place] = wgs[place]
+    for bits in range(1, 16):
+        there = (row, flip(col, bits))
+        copy = push(cot.at[there[1]], cotr.at[col], sc.at[bits], rc.at[bits], there)
+        copy.start()
+        spread.append(copy)
+    cotr[col] = cot[col]
+    quarter = col % QUAD
+    for plane in range(PLANES):
+        there = (row, plane * QUAD + z)
+        mine = jnp.logical_and(z == plane, quarter == z)
+
+        @pl.when(jnp.logical_not(mine))
+        def _():
+            push(wo, wop.at[quarter], sw.at[plane], rw.at[quarter], there).start()
+
+        @pl.when(mine)
+        def _():
+            wop[quarter] = wo[...]
+
+    gather_finish(first, xp, sx, rx, row, col, place)
+    for copy in spread:
+        copy.wait_recv()
+    for j in range(4):
+        mine = jnp.logical_and(quarter == z, quarter == j)
+
+        @pl.when(jnp.logical_not(mine))
+        def _():
+            push(wo, wop.at[j], sw.at[j], rw.at[j], (row, quarter * QUAD + j)).wait_recv()
+
+    for k in range(8):
+        lanes = slice(k * 128, k * 128 + 128)
+        gains[:, lanes] = (tiles[4 * k] + tiles[4 * k + 1]) + (tiles[4 * k + 2] + tiles[4 * k + 3])
+        times[:, lanes] = tiles[(k // QUAD) * 16 + z * QUAD + k % QUAD]
+    for k in range(16):
+        labels[:, k * 128 : k * 128 + 128] = tiles[(z // 2) * 16 + k]
+    for copy in spread:
+        copy.wait_send()
+    for plane in range(PLANES):
+        there = (row, plane * QUAD + z)
+        mine = jnp.logical_and(z == plane, quarter == z)
+
+        @pl.when(jnp.logical_not(mine))
+        def _():
+            push(wo, wop.at[quarter], sw.at[plane], rw.at[quarter], there).wait_send()
+
+
+def project_body(
+    xp, wqp, gains, times, freq, cot,
+    s1, qkvt, cotp,
+    wt, box, cs, sn, sa, ra, sz, rz,
+):
+    row, col, z, place = places()
+    meet(plane_near(row, col) + line_all(row, col))
+    first = gather_start(cot, cotp, sa, ra, row, col, place)
+    cotp[place] = cot[...]
+    wt[...] = jnp.transpose(wqp[...])
+    phases = times[3:4, :] * freq[...]
+    cs[...] = jnp.cos(phases)
+    sn[...] = jnp.sin(phases)
+    gain = gains[0:1, :]
+
+    def step(t, unused):
+        rows = pl.ds(pl.multiple_of(t * 256, 256), 256)
+        values = xp[rows, :].astype(f32)
+        normed = values * norm_scale(values)
+        scaled = (normed * gain).astype(bf16)
+        s1[rows, :] = scaled
+        out = mm_nt(wt[...], scaled)
+        cos_part, sin_part = cs[:, rows], sn[:, rows]
+        lanes = pl.ds(pl.multiple_of((t % 2) * 256, 256), 256)
+        for head in range(2):
+            pair = (t // 2) * 2 + head
+            for part in range(2):
+                base = part * 128 + head * 64
+                former, latter = out[base : base + 32], out[base + 32 : base + 64]
+                factor = 0.125 if part == 0 else 1.0
+                turned = former * cos_part - latter * sin_part
+                other = latter * cos_part + former * sin_part
+                box[pair, part * 64 : part * 64 + 32, lanes] = (turned * factor).astype(bf16)
+                box[pair, part * 64 + 32 : part * 64 + 64, lanes] = (other * factor).astype(bf16)
+            box[pair, 128:192, lanes] = out[256 + head * 64 : 256 + head * 64 + 64].astype(bf16)
+        return unused
+
+    lax.fori_loop(0, 4, step, 0)
+    mine = pl.ds(pl.multiple_of(z * 512, 512), 512)
+    copies = []
+    for bits in (3, 2, 1):
+        copy = push(
+            box.at[flip(z, bits)], qkvt.at[:, mine], sz.at[bits], rz.at[bits], on_line(row, col, bits)
+        )
+        copy.start()
+        copies.append(copy)
+    qkvt[:, mine] = box[z]
+    gather_finish(first, cotp, sa, ra, row, col, place)
+    for copy in copies:
+        copy.wait()
+
+
+def split_three(value):
+    high = value.astype(bf16).astype(f32)
+    middle = (value - high).astype(bf16).astype(f32)
+    return high, middle, (value - high - middle).astype(bf16).astype(f32)
+
+
+def window_queries(qa, lanes, first, limit):
+    place = first + lax.broadcasted_iota(jnp.int32, (16, WINDOW), 1)
+    line = lax.broadcasted_iota(jnp.int32, (16, WINDOW), 0)
+    extra = jnp.where(
+        jnp.logical_and(line == 12, place >= limit), -1e30, qa[64:80, lanes].astype(f32)
+    )
+    return jnp.concatenate(
+        [qa[0:64, lanes], extra.astype(bf16), jnp.zeros((AUG - 80, WINDOW), bf16)], axis=0
+    )
+
+
+def attend_body(info, bias, qkvt, labels, att, den, low, qa, ka, kt):
+    size = qkvt.shape[1]
+    variate = labels[2:3, :]
+    line = lax.broadcasted_iota(jnp.int32, (16, size), 0)
+    same = (variate == (line % 4).astype(f32)).astype(f32)
+    same_pieces = split_three(jnp.full((16, size), bias[0] - bias[1], f32))
+    other_pieces = split_three(jnp.full((16, size), bias[1], f32))
+
+    def choose(pieces, number):
+        return jnp.where(number == 0, pieces[0], jnp.where(number == 1, pieces[1], pieces[2]))
+
+    extra_q = jnp.where(line < 12, same, jnp.where(line == 12, 0.0, 1.0))
+    extra_k = jnp.where(
+        line < 12,
+        same * choose(same_pieces, line // 4),
+        jnp.where(line == 12, 1.0, choose(other_pieces, line - 13)),
+    )
+    qa[0:64, 0:size] = qkvt[0:64, :]
+    qa[64:80, 0:size] = extra_q.astype(bf16)
+    qa[80:AUG, 0:size] = jnp.zeros((AUG - 80, size), bf16)
+    qa[:, size:] = jnp.zeros((AUG, WINDOW), bf16)
+    kt[0:64, :] = qkvt[64:128, :]
+    kt[64:80, :] = extra_k.astype(bf16)
+    kt[80:AUG, :] = jnp.zeros((AUG - 80, size), bf16)
+    ka[...] = jnp.transpose(kt[...])
+
+    def sequence(number, start):
+        length = info[number]
+        limit = (start + length) * 128
+
+        def window(j, unused):
+            first = (start + 4 * j) * 128
+            lanes = pl.ds(pl.multiple_of(first, 128), WINDOW)
+            queries = window_queries(qa, lanes, first, limit)
+
+            def key(k, running):
+                total, numerator = running
+                rows = pl.ds(pl.multiple_of((start + k) * 128, 128), 128)
+                weights = jnp.exp(mm(ka[rows, :], queries))
+                total = total + jnp.sum(weights, axis=0, keepdims=True)
+                numerator = numerator + mm(qkvt[128:192, rows], weights.astype(bf16))
+                return total, numerator
+
+            total, numerator = lax.fori_loop(
+                0, length, key, (jnp.zeros((1, WINDOW), f32), jnp.zeros((64, WINDOW), f32))
+            )
+            attended = numerator / total
+            att[:, lanes] = attended
+            den[:, lanes] = jnp.broadcast_to(total, (8, WINDOW))
+            low[:, lanes] = attended.astype(bf16)
+            return unused
+
+        lax.fori_loop(0, (length + 3) // 4, window, 0)
+        return start + length
+
+    lax.fori_loop(0, NSEQ, sequence, 0)
+
+
+def attend_back_body(
+    info, qkvt, qa, ka, labels, freq, grad, att, den,
+    dproj, bias_tile,
+    dn, cw, vn, dq, dk, dv,
+):
+    size = qkvt.shape[1]
+    lanes_all = slice(0, size)
+    inverse = 1.0 / den[0:1, lanes_all]
+    d_att = grad[...].astype(f32)
+    dn[:, lanes_all] = (d_att * inverse).astype(bf16)
+    dn[:, size:] = jnp.zeros((64, WINDOW), bf16)
+    cw[:, lanes_all] = jnp.broadcast_to(
+        jnp.sum(d_att * att[:, lanes_all], axis=0, keepdims=True) * inverse, (8, size)
+    )
+    cw[:, size:] = jnp.zeros((8, WINDOW), f32)
+    vn[...] = jnp.transpose(qkvt[128:192, :])
+    dk[...] = jnp.zeros_like(dk)
+    dv[...] = jnp.zeros_like(dv)
+
+    def sequence(number, start):
+        length = info[number]
+        limit = (start + length) * 128
+
+        def window(j, unused):
+            first = (start + 4 * j) * 128
+            lanes = pl.ds(pl.multiple_of(first, 128), WINDOW)
+            queries = window_queries(qa, lanes, first, limit)
+            upstream = dn[:, lanes]
+            centre = cw[0:1, lanes]
+
+            def key(k, running):
+                rows = pl.ds(pl.multiple_of((start + k) * 128, 128), 128)
+                weights = jnp.exp(mm(ka[rows, :], queries))
+                d_scores = weights * (mm(vn[rows, :], upstream) - centre)
+                rounded = d_scores.astype(bf16)
+                dk[:, rows] += mm_nt(queries, rounded)
+                dv[:, rows] += mm_nt(upstream, weights.astype(bf16))
+                return running + mm(qkvt[64:128, rows], rounded)
+
+            dq[:, lanes] = lax.fori_loop(0, length, key, jnp.zeros((64, WINDOW), f32))
+            return unused
+
+        lax.fori_loop(0, (length + 3) // 4, window, 0)
+        return start + length
+
+    lax.fori_loop(0, NSEQ, sequence, 0)
+    phases = labels[3:4, :] * freq[...]
+    cos_part, sin_part = jnp.cos(phases), jnp.sin(phases)
+    for part, source, factor in ((0, dq, 0.125), (1, dk, 1.0)):
+        former, latter = source[0:32, lanes_all], source[32:64, lanes_all]
+        dproj[part * 64 : part * 64 + 32, :] = (
+            (former * cos_part + latter * sin_part) * factor
+        ).astype(bf16)
+        dproj[part * 64 + 32 : part * 64 + 64, :] = (
+            (latter * cos_part - former * sin_part) * factor
+        ).astype(bf16)
+    dproj[128:192, :] = dv[...].astype(bf16)
+    variate = labels[2:3, :]
+    line = lax.broadcasted_iota(jnp.int32, (16, size), 0)
+    match = jnp.logical_and(variate == line.astype(f32), line < 4)
+    near = jnp.sum(jnp.where(match, dk[64:80, :], 0.0))
+    every = jnp.sum(dk[77:78, :])
+    lane = lax.broadcasted_iota(jnp.int32, (8, 128), 1)
+    line8 = lax.broadcasted_iota(jnp.int32, (8, 128), 0)
+    here = lane == info[NSEQ]
+    bias_tile[...] = jnp.where(
+        jnp.logical_and(here, line8 == 2),
+        near,
+        jnp.where(jnp.logical_and(here, line8 == 3), every - near, 0.0),
+    )
+
+
+def branch_body(
+    low, wop, x, gains,
+    atp, hidden, s2p,
+    atn, part, mine, sz, rz, inbox, outbox, second, ss, rs, sa, ra,
+):
+    row, col, z, place = places()
+    meet(plane_near(row, col) + line_all(row, col))
+    rows = pl.ds(pl.multiple_of((z % 2) * 64, 64), 64)
+    lanes = pl.ds(pl.multiple_of((z // 2) * 512, 512), 512)
+    copies = []
+    for bits in (3, 2, 1):
+        theirs = pl.ds(pl.multiple_of(flip(z, bits) * 512, 512), 512)
+        copy = push(
+            low.at[:, theirs], atp.at[rows, lanes], sz.at[bits], rz.at[bits], on_line(row, col, bits)
+        )
+        copy.start()
+        copies.append(copy)
+    atp[rows, lanes] = low[:, pl.ds(pl.multiple_of(z * 512, 512), 512)]
+    for copy in copies:
+        copy.wait()
+    atn[...] = jnp.transpose(atp[...])
+    for q in range(MEMBERS):
+        part[q] = mm(atn[q * 128 : q * 128 + 128, :], wop[...]).astype(bf16)
+    first = scatter_start(part, inbox, ss, rs, row, col)
+    sent = scatter_middle(first, part, inbox, outbox, second, ss, rs, row, col, place)
+    total = scatter_finish(first, sent, part, inbox, second, place)
+    state = x[...].astype(f32) + total
+    hidden[...] = state
+    mine[...] = (state * norm_scale(state) * gains[1:2, :]).astype(bf16)
+    spread = gather_start(mine, s2p, sa, ra, row, col, place)
+    s2p[place] = mine[...]
+    gather_finish(spread, s2p, sa, ra, row, col, place)
+
+
+def ffn_body(s2, cot, wg, wd, out_part, d_part, gwd, gwg, wgs, inner_s, dgu):
+    for plane in range(PLANES):
+        for r in range(2):
+            at = (r * PLANES + plane) * 128
+            wgs[at : at + 128, :] = wg[plane * 2 + r]
+
+    def step(t, unused):
+        rows = pl.ds(pl.multiple_of(t * 256, 256), 256)
+        both = mm(s2[rows, :], wgs[...])
+        gate, upper = both[:, 0:512], both[:, 512:1024]
+        sig = jax.nn.sigmoid(gate)
+        active = gate * sig
+        inner = (active * upper).astype(bf16)
+        inner_s[rows, :] = inner
+        out_part[rows, :] = mm(inner, wd[...]).astype(bf16)
+        d_inner = mm_nt(cot[rows, :], wd[...])
+        dgu[rows, 0:512] = (d_inner * upper * sig * (1.0 + gate * (1.0 - sig))).astype(bf16)
+        dgu[rows, 512:1024] = (d_inner * active).astype(bf16)
+        d_part[rows, :] = mm_nt(dgu[rows, :], wgs[...]).astype(bf16)
+        return unused
+
+    lax.fori_loop(0, 4, step, 0)
+    for k in range(2):
+        cols = slice(k * 256, k * 256 + 256)
+        gwd[cols, :] = mm_tn(inner_s[:, cols], cot[...]).astype(bf16)
+    for f in range(8):
+        cols = slice(f * 128, f * 128 + 128)
+        gwg[(f % PLANES) * 2 + f // PLANES] = mm_tn(s2[:, cols], dgu[...]).astype(bf16)
+
+
+def hidden_back_body(
+    d_part, out_part, cot, hidden, gains, wop, atp,
+    grad, d_hidden, out, gwo, gain_term,
+    low, dbp, dat, ia, oa, na, sa, ra, ib, ob, nb, sb, rb, sg, rg, sz, rz,
+):
+    row, col, z, place = places()
+    meet(plane_near(row, col) + line_all(row, col))
+    first = scatter_start(d_part, ia, sa, ra, row, col)
+    sent = scatter_middle(first, d_part, ia, oa, na, sa, ra, row, col, place)
+    d_scaled = scatter_finish(first, sent, d_part, ia, na, place)
+    state = hidden[...]
+    scale = norm_scale(state)
+    normed = state * scale
+    gain_term[...] = jnp.broadcast_to(jnp.sum(d_scaled * normed, axis=0, keepdims=True), (8, 1024))
+    d_state = cot[...].astype(f32) + norm_back(d_scaled * gains[1:2, :], normed, scale)
+    d_hidden[...] = d_state
+    low[...] = d_state.astype(bf16)
+    spread = gather_start(low, dbp, sg, rg, row, col, place)
+    dbp[place] = low[...]
+    other_first = scatter_start(out_part, ib, sb, rb, row, col)
+    gather_finish(spread, dbp, sg, rg, row, col, place)
+    for q in range(MEMBERS):
+        dat[:, q * 128 : q * 128 + 128] = mm_nt(wop[...], dbp[q]).astype(bf16)
+    mine = pl.ds(pl.multiple_of(z * 512, 512), 512)
+    copies = []
+    for bits in (3, 2, 1):
+        pair = flip(z, bits)
+        rows = pl.ds(pl.multiple_of((pair % 2) * 64, 64), 64)
+        lanes = pl.ds(pl.multiple_of((pair // 2) * 512, 512), 512)
+        copy = push(
+            dat.at[rows, lanes], grad.at[:, mine], sz.at[bits], rz.at[bits], on_line(row, col, bits)
+        )
+        copy.start()
+        copies.append(copy)
+    grad[:, mine] = dat[
+        pl.ds(pl.multiple_of((z % 2) * 64, 64), 64),
+        pl.ds(pl.multiple_of((z // 2) * 512, 512), 512),
+    ]
+    other_sent = scatter_middle(other_first, out_part, ib, ob, nb, sb, rb, row, col, place)
+    total = mm(atp[:, 0:128], dbp[0])
+    for q in range(1, MEMBERS):
+        total = total + mm(atp[:, q * 128 : q * 128 + 128], dbp[q])
+    gwo[...] = total.astype(bf16)
+    branch = scatter_finish(other_first, other_sent, out_part, ib, nb, place)
+    out[...] = (state + branch).astype(bf16)
+    for copy in copies:
+        copy.wait()
+
+
+def last_body(
+    dproj, wqp, s1, xp, gains, d_hidden, gwo, slots, gwg, gain_two, bias_tile,
+    grad_tokens, grad_q, grad_o, out, gwg_in, tile,
+    dpt, dpn, part, gq, gqin, goin, pack, tiles,
+    sz, rz, inbox, outbox, second, ss, rs, sq, rq, st, rt, sw, rw, sg, rg, sc, rc,
+):
+    row, col, z, place = places()
+    me = row * 16 + col
+    quarter = col % QUAD
+    meet([anyone(row, col, bits) for bits in range(1, 32)])
+    copies = []
+    lanes = pl.ds(pl.multiple_of((z // 2) * 512, 512), 512)
+    for bits in (3, 2, 1):
+        theirs = pl.ds(pl.multiple_of(flip(z, bits) * 512, 512), 512)
+        for kind in range(3):
+            rows = pl.ds(pl.multiple_of(kind * 128 + (z % 2) * 64, 64), 64)
+            copy = push(
+                dproj.at[kind * 64 : kind * 64 + 64, theirs],
+                dpt.at[rows, lanes],
+                sz.at[bits, kind],
+                rz.at[bits, kind],
+                on_line(row, col, bits),
+            )
+            copy.start()
+            copies.append(copy)
+    for kind in range(3):
+        rows = pl.ds(pl.multiple_of(kind * 128 + (z % 2) * 64, 64), 64)
+        dpt[rows, lanes] = dproj[
+            kind * 64 : kind * 64 + 64, pl.ds(pl.multiple_of(z * 512, 512), 512)
+        ]
+    spread = []
+    for bits in range(1, 8):
+        there = in_plane(row, col, bits)
+        copy = push(gwg.at[flip(place, bits)], gwg_in.at[place], sg.at[bits], rg.at[bits], there)
+        copy.start()
+        spread.append(copy)
+    gwg_in[place] = gwg[place]
+    for bits in range(1, 16):
+        there = (row, flip(col, bits))
+        copy = push(slots.at[there[1]], out.at[col], sc.at[bits], rc.at[bits], there)
+        copy.start()
+        spread.append(copy)
+    out[col] = slots[col]
+    for j in range(4):
+        there = (row, quarter * QUAD + j)
+        mine = jnp.logical_and(quarter == z, quarter == j)
+
+        @pl.when(jnp.logical_not(mine))
+        def _():
+            push(gwo.at[j], goin.at[z], sw.at[j], rw.at[z], there).start()
+
+        @pl.when(mine)
+        def _():
+            goin[z] = gwo[j]
+
+    for copy in copies:
+        copy.wait()
+    dpn[...] = jnp.transpose(dpt[...])
+    gain_one = gains[0:1, :]
+    term = jnp.zeros((1, 1024), f32)
+    for q in range(MEMBERS):
+        values = xp[q].astype(f32)
+        d_scaled = mm_nt(dpn[q * 128 : q * 128 + 128, :], wqp[...])
+        term = term + jnp.sum(d_scaled * (values * norm_scale(values)), axis=0, keepdims=True)
+        part[q] = d_scaled.astype(bf16)
+    first = scatter_start(part, inbox, ss, rs, row, col)
+    for k in range(8):
+        pack[k] = bias_tile[...]
+        pack[k, 0:1, :] = term[:, k * 128 : k * 128 + 128]
+        pack[k, 1:2, :] = gain_two[0:1, k * 128 : k * 128 + 128]
+    for f in range(8):
+        chunk = mm_tn(s1[:, f * 128 : f * 128 + 128], dpn[...]).astype(bf16)
+        for j in range(4):
+            gq[f * 4 + j] = chunk[j * 32 : j * 32 + 32, :]
+    sent = scatter_middle(first, part, inbox, outbox, second, ss, rs, row, col, place)
+    for bits in range(1, 32):
+        there = anyone(row, col, bits)
+        number = there[0] * 16 + there[1]
+        copy = push(gq.at[number], gqin.at[me], sq.at[bits], rq.at[bits], there)
+        copy.start()
+        spread.append(copy)
+        copy = push(pack.at[number // 4], tiles.at[me], st.at[bits], rt.at[bits], there)
+        copy.start()
+        spread.append(copy)
+    gqin[me] = gq[me]
+    tiles[me] = pack[me // 4]
+    d_one = scatter_finish(first, sent, part, inbox, second, place)
+    own = xp[place].astype(f32)
+    scale = norm_scale(own)
+    grad_tokens[...] = (
+        d_hidden[...] + norm_back(d_one * gain_one, own * scale, scale)
+    ).astype(bf16)
+    for copy in spread:
+        copy.wait_recv()
+    for plane in range(PLANES):
+        mine = jnp.logical_and(quarter == z, z == plane)
+
+        @pl.when(jnp.logical_not(mine))
+        def _():
+            push(
+                gwo.at[0], goin.at[plane], sw.at[plane], rw.at[plane], (row, plane * QUAD + z)
+            ).wait_recv()
+
+    grad_o[...] = (goin[0].astype(f32) + goin[1].astype(f32)) + (
+        goin[2].astype(f32) + goin[3].astype(f32)
+    )
+    for p in range(MEMBERS):
+        total = jnp.zeros((32, 384), f32)
+        for plane in range(PLANES):
+            total = total + gqin[(p // QUAD) * 16 + plane * QUAD + p % QUAD].astype(f32)
+        for kind in range(3):
+            at = kind * 1024 + p * 128
+            grad_q[:, at : at + 128] = total[:, kind * 128 : kind * 128 + 128]
+    total = tiles[0]
+    for k in range(1, 32):
+        total = total + tiles[k]
+    tile[...] = total
+    for copy in spread:
+        copy.wait_send()
+    for j in range(4):
+        there = (row, quarter * QUAD + j)
+        mine = jnp.logical_and(quarter == z, quarter == j)
+
+        @pl.when(jnp.logical_not(mine))
+        def _():
+            push(gwo.at[j], goin.at[z], sw.at[j], rw.at[z], there).wait_send()
+
+
+def sds(shape, dtype):
+    return jax.ShapeDtypeStruct(shape, dtype)
+
+
+def dma(*shape):
+    return pltpu.SemaphoreType.DMA(shape)
+
+
+def kernel(body, name, specs, outs, scratch, number=None, cost=0):
+    params = dict(vmem_limit_bytes=56 << 20)
+    if number is not None:
+        params.update(collective_id=number, has_side_effects=True)
+    return pl.pallas_call(
+        body,
+        name=name,
+        in_specs=specs,
+        out_shape=outs,
+        out_specs=[VM] * len(outs),
+        scratch_shapes=scratch,
+        compiler_params=pltpu.CompilerParams(**params),
+        cost_estimate=pl.CostEstimate(flops=cost, bytes_accessed=cost // 300, transcendentals=0),
+    )
+
+
+def plane_shards(
+    tokens, variate_ids, time_ids, lengths, deal, w_qkv, w_out, w_gate_up, w_down,
+    gain_attn, gain_ffn, var_bias, cotangent,
+):
+    row = lax.axis_index("row")
+    col = lax.axis_index("col")
+    z, q = col // QUAD, col % QUAD
+    place = row * QUAD + q
+    rows, width = tokens.shape
+    lines = [[plane * QUAD + k for plane in range(PLANES)] for k in range(QUAD)]
+    down = lax.all_gather(w_down, "col", axis=0, tiled=True, axis_index_groups=lines)
+    spot = (q * 32 + jnp.arange(32, dtype=jnp.int32))[:, None] == jnp.arange(128)[None, :]
+    gain_rows = jnp.sum(
+        jnp.where(
+            spot[None], jnp.stack([gain_attn, gain_ffn]).astype(f32)[:, :, None], 0.0
+        ),
+        axis=1,
+    )
+    tile = jnp.concatenate(
+        [
+            gain_rows,
+            variate_ids.astype(f32)[None],
+            time_ids.astype(f32)[None],
+            jnp.pad(lengths[0].astype(f32), (0, 128 - lengths.shape[1]))[None],
+            jnp.zeros((3, 128), f32),
+        ],
+        axis=0,
+    )
+    freq = jnp.exp(-math.log(10000.0) * jnp.arange(32, dtype=f32) / 32)[:, None]
+
+    xp, wqp, wop, wgp, cotr, tiles, gains, times, labels = kernel(
+        gather_body,
+        "gather_all",
+        [VM] * 6,
+        [
+            sds((8, rows, width), bf16),
+            sds((32, 32, 384), bf16),
+            sds((4, 32, 1024), bf16),
+            sds((8, 32, 1024), bf16),
+            sds((16, 8, width), bf16),
+            sds((32, 8, 128), f32),
+            sds((8, 1024), f32),
+            sds((8, 1024), f32),
+            sds((8, 2048), f32),
+        ],
+        [pltpu.VMEM((8, 32, 384), bf16), pltpu.VMEM((8, 32, 1024), bf16)]
+        + [dma(8), dma(8), dma(32), dma(32), dma(32), dma(32), dma(4), dma(4)]
+        + [dma(8), dma(8), dma(16), dma(16)],
+        number=1,
+    )(tokens, w_qkv, w_out, w_gate_up, cotangent.reshape(16, 8, width), tile)
+
+    gate_up = lax.all_gather(
+        wgp.reshape(256, 1024), "col", axis=0, tiled=True, axis_index_groups=lines
+    )
+    wqp = wqp.reshape(1024, 384)
+    wop = wop.reshape(128, 1024)
+    target = deal[0, 0]
+    cot = jnp.take(cotr, target, axis=0).reshape(rows, width)
+
+    s1, qkvt, cotp = kernel(
+        project_body,
+        "project",
+        [VM] * 6,
+        [sds((1024, width), bf16), sds((192, 2048), bf16), sds((8, rows, width), bf16)],
+        [
+            pltpu.VMEM((384, 1024), bf16),
+            pltpu.VMEM((4, 192, 512), bf16),
+            pltpu.VMEM((32, 1024), f32),
+            pltpu.VMEM((32, 1024), f32),
+            dma(8), dma(8), dma(4), dma(4),
+        ],
+        number=2,
+    )(xp.reshape(1024, width), wqp, gains, times, freq, cot)
+
+    head = place * 2 + z % 2
+    info = jnp.concatenate(
+        [labels[4, :NSEQ].astype(jnp.int32), head[None].astype(jnp.int32), jnp.zeros((1,), jnp.int32)]
+    )
+    bias = lax.dynamic_slice_in_dim(var_bias, head, 1, 1)[:, 0]
+    wide = 2048 + WINDOW
+    att, den, low, qa, ka = kernel(
+        attend_body,
+        "attend",
+        [SM, SM, VM, VM],
+        [
+            sds((64, wide), f32),
+            sds((8, wide), f32),
+            sds((64, wide), bf16),
+            sds((AUG, wide), bf16),
+            sds((2048, AUG), bf16),
+        ],
+        [pltpu.VMEM((AUG, 2048), bf16)],
+        cost=2 * 10**9,
+    )(info, bias, qkvt, labels)
+
+    atp, hidden, s2p = kernel(
+        branch_body,
+        "branch",
+        [VM] * 4,
+        [sds((128, 1024), bf16), sds((rows, width), f32), sds((8, rows, width), bf16)],
+        [
+            pltpu.VMEM((1024, 128), bf16),
+            pltpu.VMEM((8, rows, width), bf16),
+            pltpu.VMEM((rows, width), bf16),
+            dma(4), dma(4),
+        ]
+        + scatter_scratch(rows, width)
+        + [dma(8), dma(8)],
+        number=3,
+    )(low, wop, tokens, gains)
+
+    out_part, d_part, gwd, gwg = kernel(
+        ffn_body,
+        "ffn",
+        [VM] * 4,
+        [
+            sds((1024, width), bf16),
+            sds((1024, width), bf16),
+            sds((512, width), bf16),
+            sds((8, 128, 1024), bf16),
+        ],
+        [
+            pltpu.VMEM((1024, 1024), bf16),
+            pltpu.VMEM((1024, 512), bf16),
+            pltpu.VMEM((1024, 1024), bf16),
+        ],
+        cost=10**10,
+    )(s2p.reshape(1024, width), cotp.reshape(1024, width), gate_up.reshape(8, 128, 1024), down)
+
+    grad_down = lax.psum_scatter(
+        gwd, "col", scatter_dimension=0, tiled=True, axis_index_groups=lines
+    )
+    gate_up_sum = lax.psum_scatter(
+        gwg.reshape(1024, 1024), "col", scatter_dimension=0, tiled=True, axis_index_groups=lines
+    )
+
+    grad, d_hidden, out_rows, gwo, gain_two = kernel(
+        hidden_back_body,
+        "hidden_back",
+        [VM] * 7,
+        [
+            sds((64, 2048), bf16),
+            sds((rows, width), f32),
+            sds((rows, width), bf16),
+            sds((128, 1024), bf16),
+            sds((8, 1024), f32),
+        ],
+        [
+            pltpu.VMEM((rows, width), bf16),
+            pltpu.VMEM((8, rows, width), bf16),
+            pltpu.VMEM((128, 1024), bf16),
+        ]
+        + scatter_scratch(rows, width)
+        + scatter_scratch(rows, width)
+        + [dma(8), dma(8), dma(4), dma(4)],
+        number=4,
+    )(
+        d_part.reshape(8, rows, width), out_part.reshape(8, rows, width), cot, hidden, gains, wop, atp
+    )
+
+    slot = jnp.arange(16, dtype=jnp.int32)
+    inverse = jnp.sum(slot[:, None] * (target[:, None] == slot[None, :]).astype(jnp.int32), axis=0)
+    slots = jnp.take(out_rows.reshape(16, 8, width), inverse, axis=0)
+
+    dproj, bias_tile = kernel(
+        attend_back_body,
+        "attend_back",
+        [SM] + [VM] * 8,
+        [sds((192, 2048), bf16), sds((8, 128), f32)],
+        [
+            pltpu.VMEM((64, wide), bf16),
+            pltpu.VMEM((8, wide), f32),
+            pltpu.VMEM((2048, 64), bf16),
+            pltpu.VMEM((64, wide), f32),
+            pltpu.VMEM((AUG, 2048), f32),
+            pltpu.VMEM((64, 2048), f32),
+        ],
+        cost=5 * 10**9,
+    )(info, qkvt, qa, ka, labels, freq, grad, att, den)
+
+    grad_tokens, grad_q, grad_o, out, gwg_in, sums = kernel(
+        last_body,
+        "last",
+        [VM] * 11,
+        [
+            sds((rows, width), bf16),
+            sds((32, 3072), f32),
+            sds((32, 1024), f32),
+            sds((16, 8, width), bf16),
+            sds((8, 32, 1024), bf16),
+            sds((8, 128), f32),
+        ],
+        [
+            pltpu.VMEM((384, 1024), bf16),
+            pltpu.VMEM((1024, 384), bf16),
+            pltpu.VMEM((8, rows, width), bf16),
+            pltpu.VMEM((32, 32, 384), bf16),
+            pltpu.VMEM((32, 32, 384), bf16),
+            pltpu.VMEM((4, 32, 1024), bf16),
+            pltpu.VMEM((8, 8, 128), f32),
+            pltpu.VMEM((32, 8, 128), f32),
+            dma(4, 3), dma(4, 3),
+        ]
+        + scatter_scratch(rows, width)
+        + [dma(32), dma(32), dma(32), dma(32), dma(4), dma(4), dma(8), dma(8), dma(16), dma(16)],
+        number=5,
+    )(
+        dproj, wqp, s1, xp, gains, d_hidden, gwo.reshape(4, 32, 1024), slots,
+        gate_up_sum.reshape(8, 32, 1024), gain_two, bias_tile,
+    )
+    grad_gate_up = (
+        gwg_in.reshape(2, QUAD, 32, 2, PLANES, 128)
+        .transpose(2, 3, 0, 4, 1, 5)
+        .reshape(32, 8192)
+        .astype(f32)
+    )
+    gain_grads = lax.dynamic_slice_in_dim(sums[0:2], q * 32, 32, 1)
+    return (
+        out.reshape(rows, width),
+        grad_tokens,
+        grad_q,
+        grad_o,
+        grad_gate_up,
+        grad_down.astype(f32),
+        gain_grads[0],
+        gain_grads[1],
+        sums[2:4, :16],
+    )
+
+
 def solution(mesh):
+    planes = mesh.shape["row"] == 2 and mesh.shape["col"] == PLANES * QUAD
     return jax.shard_map(
-        shards,
+        plane_shards if planes else shards,
         mesh=mesh,
         in_specs=(
             P(("row", "col"), None),

time: 1560 us -> 352 us (0.23)
  waiting for transfers between devices: 1120 us -> 2.11 us
  Pallas kernels: 0 us -> 314 us
  matrix products: 157 us -> 0 us
  blocking collectives: 121 us -> 0 us
  local copies, waits for them, and re-layouts: 99.5 us -> 13.3 us
    reduce_scatter x4 -> x2, waiting for transfers between devices: 753 us -> 1.02 us  [the longest x1 1.01 us: plane_shards(): lax.psum_scatter(gwg.reshape(1024, 1024), 'col', scatter_dimension=0, til...]
    pallas_call x0 -> x8, Pallas kernels: none -> 314 us  [the longest x1 64.3 us: plane_shards(): kernel(last_body, 'last', [VM] * 11, [sds((rows, width), bf16), sds((32,...]
    all_gather x6 -> x2, waiting for transfers between devices: 245 us -> 0.04 us  [the longest x1 0.02 us: plane_shards(): lax.all_gather(w_down, 'col', axis=0, tiled=True, axis_index_groups=lines)]
    dot_general x26 -> x0, matrix products: 157 us -> none  [the longest x4 32.1 us: contract_rows(): lax.dot_general(operand, factor, (((0,), (0,)), ((), ())), preferred_elem...]
    unnamed x14 -> x4, waiting for transfers between devices: 120 us -> 1.06 us
    unnamed x2 -> x0, blocking collectives: 83.5 us -> none
    unnamed x58 -> x16, local copies, waits for them, and re-layouts: 69.3 us -> 2.84 us
    all_gather x2 -> x0, blocking collectives: 37.7 us -> none  [the longest x1 19.8 us: shards(): lax.all_gather(seq_q, 'col', axis=0, tiled=True)]
  transfers between devices with their start and end apart: 15 -> 4, of which waited for: 13 -> 1; matrix products, arithmetic and copies ran while one was open for 11% -> 3% of each run, Pallas kernels for 0% -> 66%
where the time goes in v1:
time: 352 us
  Pallas kernels  314 us (89%)
  between operations  14 us (4%)
  local copies, waits for them, and re-layouts  13.3 us (4%)
  other arithmetic  7.6 us (2%)
    pallas_call x1, Pallas kernels, plane_shards(): kernel(last_body, 'last', [VM] * 11, [sds((rows, width), bf16), sds((32,...  64.3 us
    pallas_call x1, Pallas kernels, plane_shards(): kernel(gather_body, 'gather_all', [VM] * 6, [sds((8, rows, width), bf16),...  57.8 us
    pallas_call x1, Pallas kernels, plane_shards(): kernel(hidden_back_body, 'hidden_back', [VM] * 7, [sds((64, 2048), bf16),...  53.2 us
    pallas_call x1, Pallas kernels, plane_shards(): kernel(project_body, 'project', [VM] * 6, [sds((1024, width), bf16), sds(...  50.6 us
    pallas_call x1, Pallas kernels, plane_shards(): kernel(branch_body, 'branch', [VM] * 4, [sds((128, 1024), bf16), sds((row...  47 us
    pallas_call x1, Pallas kernels, plane_shards(): kernel(ffn_body, 'ffn', [VM] * 4, [sds((1024, width), bf16), sds((1024, w...  16.3 us
    pallas_call x1, Pallas kernels, plane_shards(): kernel(attend_back_body, 'attend_back', [SM] + [VM] * 8, [sds((192, 2048)...  14.6 us
    pallas_call x1, Pallas kernels, plane_shards(): kernel(attend_body, 'attend', [SM, SM, VM, VM], [sds((64, wide), f32), sd...  10.6 us
  transfers between devices with their start and end apart: 4, of which 1 were waited for; matrix products, arithmetic and copies ran while one was open for 3% of the time, Pallas kernels for 66%

profile of v1, /device:TPU:0, one launch (start us, length us, event | category | flops | bytes accessed | tf_op | source)
XLA Modules:
  0.0 351.7 jit_solution(7642601044261378934)
XLA Ops:
  7.2 0.7 all-gather.5.cloned.1.call-update
  8.0 0.7 convert_bitcast_fusion.1
  8.7 0.7 maximum_convert_fusion
  9.5 0.7 convert_bitcast_fusion.2
  10.2 0.6 concatenate.10.tile
  10.8 57.8 %gather_all.1 = (bf16[8,128,1024]{2,1,0:T(8,128)(2,1)}, bf16[32,32,384]{2,1,0:T(8,128)(2,1)}, bf16[4,32,1024]{2,1,0:T(8,128)(2,1)}, bf16[8,32,1024]{2,1,0:T(8,12...) custom-call(bf16[128,1024]{1,0:T(8,128)(2,1)} %x.5, ...), custom_call_target="tpu_custom_call" | custom-call | tf_op jit(solution)/shard_map/gather_all/pallas_call | solution.py:1062
  68.8 1.5 gather_fusion
  70.3 0.7 dynamic-slice_reduce_fusion.bias
  71.0 0.6 multiply_exponential_fusion.freq
  71.7 0.8 select_bitcast_fusion.cot
  72.5 50.6 %project.1 = (bf16[1024,1024]{1,0:T(8,128)(2,1)}, bf16[192,2048]{1,0:T(8,128)(2,1)}, bf16[8,128,1024]{2,1,0:T(8,128)(2,1)}) custom-call(bf16[1024,1024]{1,0:T(8,128)(2,1)} %bitcast.39, bf16[1024,384]{1,0:T(8,128)(2,1)} %bitcast.41, f32[8,1024]{1,0:T(8,128)} %get-tuple-element.49.gains, f32[8,1024]{1,0:T(8,128)} %get-tuple-element.50.times, ...), custom_call_target="tpu_custom_call" | custom-call | tf_op jit(solution)/shard_map/project/pallas_call | solution.py:1091
  123.1 0.7 convert_bitcast_fusion
  123.8 0.6 pad_add_fusion.info
  124.3 10.6 %attend.1 = (f32[64,2560]{1,0:T(8,128)}, f32[8,2560]{1,0:T(8,128)}, bf16[64,2560]{1,0:T(8,128)(2,1)}, bf16[128,2560]{1,0:T(8,128)(2,1)}, bf16[2048,128]{1,0:T(8,128)(2,1)}) custom-call(s32[8]{0:T(128)} %pad_add_fusion.info, f32[2]{0:T(128)} %dynamic-slice_reduce_fusion.bias, bf16[192,2048]{1,0:T(8,128)(2,1)} %get-tuple-element.52.qkvt, ...), custom_call_target="tpu_custom_call" | custom-call | flops 2000000000 | bytes 6666666 | tf_op jit(solution)/shard_map/attend/pallas_call | solution.py:1112
  135.0 47.0 %branch.1 = (bf16[128,1024]{1,0:T(8,128)(2,1)}, f32[128,1024]{1,0:T(8,128)}, bf16[8,128,1024]{2,1,0:T(8,128)(2,1)}) custom-call(bf16[64,2560]{1,0:T(8,128)(2,1)} %get-tuple-element.55.low, bf16[128,1024]{1,0:T(8,128)(2,1)} %bitcast.46, bf16[128,1024]{1,0:T(8,128)(2,1)} %x.5, f32[8,1024]{1,0:T(8,128)} %get-tuple-element.49.gains), custom_call_target="tpu_custom_call" | custom-call | tf_op jit(solution)/shard_map/branch/pallas_call | solution.py:1127
  182.0 16.3 %ffn.1 = (bf16[1024,1024]{1,0:T(8,128)(2,1)}, bf16[1024,1024]{1,0:T(8,128)(2,1)}, bf16[512,1024]{1,0:T(8,128)(2,1)}, bf16[8,128,1024]{2,1,0:T(8,128)(2,1)}) custom-call(bf16[1024,1024]{1,0:T(8,128)(2,1)} %bitcast.59, bf16[1024,1024]{1,0:T(8,128)(2,1)} %bitcast.58, bf16[8,128,1024]{2,1,0:T(8,128)(2,1)} %bitcast.57, ...), custom_call_target="tpu_custom_call" | custom-call | flops 10000000000 | bytes 33333332 | tf_op jit(solution)/shard_map/ffn/pallas_call | solution.py:1143
  198.9 53.2 %hidden_back.1 = (bf16[64,2048]{1,0:T(8,128)(2,1)}, f32[128,1024]{1,0:T(8,128)}, bf16[128,1024]{1,0:T(8,128)(2,1)}, bf16[128,1024]{1,0:T(8,128)(2,1)}, f32[8,1024]{1,0:T(8,128)}) custom-call(bf16[8,128,1024]{2,1,0:T(8,128)(2,1)} %bitcast.45, bf16[8,128,1024]{2,1,0:T(8,128)(2,1)} %bitcast.44, bf16[128,1024]{1,0:T(8,128)(2,1)} %select_bitcast_fusion.cot, ...), custom_call_target="tpu_custom_call" | custom-call | tf_op jit(solution)/shard_map/hidden_back/pallas_call | solution.py:1168
  252.2 1.5 gather_fusion.1
  253.7 0.8 broadcast_select_fusion.slots
  254.5 14.6 %attend_back.1 = (bf16[192,2048]{1,0:T(8,128)(2,1)}, f32[8,128]{1,0:T(8,128)}) custom-call(s32[8]{0:T(128)} %pad_add_fusion.info, bf16[192,2048]{1,0:T(8,128)(2,1)} %get-tuple-element.52.qkvt, bf16[128,2560]{1,0:T(8,128)(2,1)} %get-tuple-element.53.qa, bf16[2048,128]{1,0:T(8,128)(2,1)} %get-tuple-element.54.ka, f32[8,2048]{1,0:T(8,128)} %get-tuple-element.46.labels, ...), custom_call_target="tpu_custom_call" | custom-call | flops 5000000000 | bytes 16666666 | tf_op jit(solution)/shard_map/attend_back/pallas_call | solution.py:1196
  269.1 1.8 convert_element_type.54
  270.9 1.0 reduce-scatter.3.cloned.1.call-done
  271.9 64.3 %last.1 = (bf16[128,1024]{1,0:T(8,128)(2,1)}, f32[32,3072]{1,0:T(8,128)}, f32[32,1024]{1,0:T(8,128)}, bf16[16,8,1024]{2,1,0:T(8,128)(2,1)}, bf16[8,32,1024]{2,1,0:T(8,128)(2,1)}, /*index=5*/f32[8,128]{1,0:T(8,128)}) custom-call(bf16[192,2048]{1,0:T(8,128)(2,1)} %get-tuple-element.67.dproj, bf16[1024,384]{1,0:T(8,128)(2,1)} %bitcast.42, ...), custom_call_target="tpu_custom_call" | custom-call | tf_op jit(solution)/shard_map/last/pallas_call | solution.py:1212
  336.2 0.7 slice.16
  336.9 1.2 slice.19
  338.1 1.5 reshape.147
  339.6 0.7 copy.23
  340.3 1.4 reshape.146
  342.4 0.7 copy.28
  343.1 0.7 copy.29
  343.8 0.7 copy.30
  344.5 0.7 copy.31
  (35 shorter events, 1.7 us)
Async XLA Ops:
  7.2 63.2 %copy-start = (f32[2,16]{1,0:T(2,128)S(1)}, f32[2,16]{1,0:T(2,128)}, u32[]{:S(2)}) copy-start(f32[2,16]{1,0:T(2,128)} %param.26) | copy-start | bytes 388
  7.2 61.5 %copy-start.5 = (s32[1,1,16]{2,1,0:T(1,128)S(1)}, s32[1,1,16]{2,1,0:T(1,128)}, u32[]{:S(2)}) copy-start(s32[1,1,16]{2,1,0:T(1,128)} %param.19) | copy-start | bytes 196
  7.2 174.8 %all-gather.5.cloned.1.call-start = ((), (), s32[]{:S(2)}) async-start(), calls=%async_computation.3 | async-start | bytes 1310720 | tf_op jit(solution)/shard_map/all_gather | solution.py:1042
  7.9 174.0 %all-gather.3.cloned.1.call-start = ((), (), s32[]{:S(2)}) async-start(), calls=%async_computation.2 | async-start | bytes 2621440 | tf_op jit(solution)/shard_map/all_gather | solution.py:1083
  68.6 200.5 %reduce-scatter.5.cloned.1.call-start = ((), (), s32[]{:S(2)}) async-start(), calls=%async_computation.5 | async-start | bytes 1310720 | tf_op jit(solution)/shard_map/reduce_scatter | solution.py:1161
  198.3 73.6 %reduce-scatter.3.cloned.1.call-start = ((), (), s32[]{:S(2)}) async-start(), calls=%async_computation.4 | async-start | bytes 2621440 | tf_op jit(solution)/shard_map/reduce_scatter | solution.py:1164
  339.6 2.8 copy-start.3
  339.6 3.5 copy-start.2
  340.3 3.5 copy-start.1
  340.3 4.2 %copy-start.4 = (f32[32,1024]{1,0:T(8,128)S(1)}, f32[32,1024]{1,0:T(8,128)}, u32[]{:S(2)}) copy-start(f32[32,1024]{1,0:T(8,128)} %get-tuple-element.100) | copy-start | bytes 393220
Sparse Core Ops, SparseCore 0:
  9.6 54.7 all-gather.4
  68.7 64.3 all-gather.2
  198.4 24.4 reduce-scatter.4
  225.2 46.6 reduce-scatter.2

commit v2 on v1

--- a/solution.py
+++ b/solution.py
@@ -328,6 +328,7 @@
 bf16 = jnp.bfloat16
 VM = pl.BlockSpec(memory_space=pltpu.VMEM)
 SM = pl.BlockSpec(memory_space=pltpu.SMEM)
+ANY = pl.BlockSpec(memory_space=pl.ANY)
 
 
 def mm(a, b):
@@ -401,72 +402,103 @@
     return [on_line(row, col, bits) for bits in (1, 2, 3)]
 
 
-def gather_start(source, target, send, recv, row, col, place):
-    copies = {}
-    for bits in NEAR:
-        copies[bits] = push(
-            source, target.at[place], send.at[bits], recv.at[bits], in_plane(row, col, bits)
-        )
-        copies[bits].start()
-    return copies
-
-
-def gather_finish(copies, target, send, recv, row, col, place):
-    onward = []
-    for bits in (2, 4, 6):
-        copies[bits].wait_recv()
-        slot = target.at[flip(place, bits)]
-        copy = push(slot, slot, send.at[bits + 1], recv.at[bits + 1], in_plane(row, col, 1))
+class Gather:
+    def __init__(self, target, send, recv):
+        self.target, self.send, self.recv = target, send, recv
+        self.row, self.col, _, self.place = places()
+        self.copies, self.onward = {}, {}
+
+    def start(self, source):
+        for bits in NEAR:
+            self.copies[bits] = push(
+                source,
+                self.target.at[self.place],
+                self.send.at[bits],
+                self.recv.at[bits],
+                in_plane(self.row, self.col, bits),
+            )
+            self.copies[bits].start()
+
+    def forward(self, bits):
+        self.copies[bits].wait_recv()
+        slot = self.target.at[flip(self.place, bits)]
+        self.onward[bits] = push(
+            slot,
+            slot,
+            self.send.at[bits + 1],
+            self.recv.at[bits + 1],
+            in_plane(self.row, self.col, 1),
+        )
+        self.onward[bits].start()
+
+    def arrived(self, bits):
+        (self.onward[bits] if bits else self.copies[1]).wait_recv()
+
+    def close(self):
+        for copy in list(self.copies.values()) + list(self.onward.values()):
+            copy.wait_send()
+
+    def finish(self):
+        for bits in (2, 4, 6):
+            self.forward(bits)
+        for bits in (0, 2, 4, 6):
+            self.arrived(bits)
+
+
+class Scatter:
+    def __init__(self, part, inbox, outbox, second, send, recv):
+        self.part, self.inbox, self.outbox, self.second = part, inbox, outbox, second
+        self.send, self.recv = send, recv
+        self.row, self.col, _, self.place = places()
+        self.core = self.col % 2
+        self.copies, self.sent = [], []
+
+    def near(self, chip, number):
+        copy = push(
+            self.part.at[2 * chip + 1 - self.core],
+            self.inbox.at[number],
+            self.send.at[number],
+            self.recv.at[number],
+            in_plane(self.row, self.col, 1),
+        )
         copy.start()
-        onward.append(copy)
-    copies[1].wait_recv()
-    for copy in onward:
-        copy.wait_recv()
-    for copy in list(copies.values()) + onward:
-        copy.wait_send()
-
-
-def scatter_start(part, inbox, send, recv, row, col):
-    other = 1 - col % 2
-    copies = []
-    for i in range(4):
+        self.copies.append(copy)
+
+    def far(self, bits):
+        self.copies[bits].wait_recv()
+        chip = flip(self.place // 2, bits)
+        total = self.part[2 * chip + self.core].astype(f32) + self.inbox[bits].astype(f32)
+        self.outbox[bits - 1] = total.astype(bf16)
         copy = push(
-            part.at[2 * i + other], inbox.at[i], send.at[i], recv.at[i], in_plane(row, col, 1)
+            self.outbox.at[bits - 1],
+            self.second.at[bits - 1],
+            self.send.at[3 + bits],
+            self.recv.at[3 + bits],
+            in_plane(self.row, self.col, 2 * bits),
         )
         copy.start()
-        copies.append(copy)
-    return copies
-
-
-def scatter_middle(copies, part, inbox, outbox, second, send, recv, row, col, place):
-    core = col % 2
-    for copy in copies:
-        copy.wait_recv()
-    sent = []
-    for bits in (1, 2, 3):
-        i = flip(place // 2, bits)
-        outbox[bits - 1] = (part[2 * i + core].astype(f32) + inbox[i].astype(f32)).astype(bf16)
-        copy = push(
-            outbox.at[bits - 1],
-            second.at[bits - 1],
-            send.at[3 + bits],
-            recv.at[3 + bits],
-            in_plane(row, col, 2 * bits),
-        )
-        copy.start()
-        sent.append(copy)
-    return sent
-
-
-def scatter_finish(copies, sent, part, inbox, second, place):
-    for copy in sent:
-        copy.wait_recv()
-    total = part[place].astype(f32) + inbox[place // 2].astype(f32)
-    for i in range(3):
-        total = total + second[i].astype(f32)
-    for copy in copies + sent:
-        copy.wait_send()
-    return total
+        self.sent.append(copy)
+
+    def near_all(self):
+        for bits in range(4):
+            self.near(flip(self.place // 2, bits), bits)
+
+    def far_all(self):
+        for bits in (3, 2, 1):
+            self.far(bits)
+
+    def finish(self):
+        self.copies[0].wait_recv()
+        total = self.part[self.place].astype(f32) + self.inbox[0].astype(f32)
+        for copy in self.sent:
+            copy.wait_recv()
+        for i in range(3):
+            total = total + self.second[i].astype(f32)
+        return total
+
+    def close(self):
+        for copy in self.copies + self.sent:
+            copy.wait_send()
 
 
 def scatter_scratch(rows, width):
@@ -479,33 +511,71 @@
     ]
 
 
-def gather_body(
-    x, wq, wo, wg, cot, tile,
-    xp, wqp, wop, wgp, cotr, tiles, gains, times, labels,
-    wqs, wgs, sx, rx, sq, rq, st, rt, sw, rw, sg, rg, sc, rc,
+def fetch(source, target, semaphore):
+    copy = pltpu.make_async_copy(source, target, semaphore)
+    copy.start()
+    return copy
+
+
+def block(number, size):
+    return pl.ds(pl.multiple_of(number * size, size), size)
+
+
+def enter_body(
+    x, wq, wo, wg, cot, ga, gf, variate, time, lengths, deal, freq,
+    xp_out, wqp_out, wop, wgp, cotp_out, s1_out, qkvt, gains, labels,
+    xp, wqp, cotp, s1, keep, wqs, wgs, cotr, cots, tile, tl, tiles, wt, box, cs, sn, times,
+    sx, rx, sq, rq, st, rt, su, ru, sw, rw, sg, rg, sc, rc, sa, ra, sz, rz,
 ):
     row, col, z, place = places()
     me = row * 16 + col
+    quarter = col % QUAD
+    lane = lax.broadcasted_iota(jnp.int32, (1, 128), 1)
+    for line, gain in ((0, ga), (1, gf)):
+        wide = gain[...].astype(f32)
+        wide = jnp.concatenate([wide] * 4, axis=1)
+        tile[line : line + 1, :] = jnp.where(lane // 32 == quarter, wide, 0.0)
+    tile[2:3, :] = variate[...].astype(f32)
+    tile[3:4, :] = time[...].astype(f32)
+    numbers = jnp.zeros((1, 128), jnp.int32)
+    for i in range(NSEQ):
+        numbers = jnp.where(lane == i, lengths[0, i], numbers)
+    tile[4:5, :] = numbers.astype(f32)
+    tile[5:8, :] = jnp.zeros((3, 128), f32)
     meet([anyone(row, col, bits) for bits in range(1, 32)])
+    rows_in = Gather(xp, sx, rx)
+    rows_in.start(x)
+    first = []
+    for bits in (1, 2, 3):
+        first.append(push(tile, tl.at[z], st.at[bits], rt.at[bits], on_line(row, col, bits)))
+        first[-1].start()
     for p in range(MEMBERS):
         for part in range(3):
-            wqs[p, :, part * 128 : part * 128 + 128] = wq[
-                :, part * 1024 + p * 128 : part * 1024 + p * 128 + 128
-            ]
-    first = gather_start(x, xp, sx, rx, row, col, place)
-    spread = []
+            at = part * 1024 + p * 128
+            wqs[p, :, part * 128 : part * 128 + 128] = wq[:, at : at + 128]
+    weights = []
     for bits in range(1, 32):
         there = anyone(row, col, bits)
         member = there[0] * QUAD + there[1] % QUAD
-        copy = push(wqs.at[member], wqp.at[me], sq.at[bits], rq.at[bits], there)
-        copy.start()
-        spread.append(copy)
-        copy = push(tile, tiles.at[me], st.at[bits], rt.at[bits], there)
-        copy.start()
-        spread.append(copy)
+        weights.append(push(wqs.at[member], wqp.at[me], sq.at[bits], rq.at[bits], there))
+        weights[-1].start()
+    pieces = []
+    for bits in range(1, 16):
+        there = (row, flip(col, bits))
+        pieces.append(push(cot.at[there[1]], cotr.at[col], sc.at[bits], rc.at[bits], there))
+        pieces[-1].start()
     xp[place] = x[...]
     wqp[me] = wqs[place]
-    tiles[me] = tile[...]
+    tl[z] = tile[...]
+    cotr[col] = cot[col]
+    for copy in first:
+        copy.wait_recv()
+    second = []
+    for bits in range(1, 8):
+        there = in_plane(row, col, bits)
+        second.append(push(tl, tiles.at[place], su.at[bits], ru.at[bits], there))
+        second[-1].start()
+    tiles[place] = tl[...]
     for p in range(MEMBERS):
         for half in range(2):
             for plane in range(PLANES):
@@ -513,107 +583,138 @@
                 at = half * 512 + plane * 128
                 start = half * 4096 + unit * 128
                 wgs[p, :, at : at + 128] = wg[:, start : start + 128]
-    for bits in range(1, 8):
-        there = in_plane(row, col, bits)
-        copy = push(wgs.at[flip(place, bits)], wgp.at[place], sg.at[bits], rg.at[bits], there)
-        copy.start()
-        spread.append(copy)
-    wgp[place] = wgs[place]
-    for bits in range(1, 16):
-        there = (row, flip(col, bits))
-        copy = push(cot.at[there[1]], cotr.at[col], sc.at[bits], rc.at[bits], there)
-        copy.start()
-        spread.append(copy)
-    cotr[col] = cot[col]
-    quarter = col % QUAD
-    for plane in range(PLANES):
-        there = (row, plane * QUAD + z)
-        mine = jnp.logical_and(z == plane, quarter == z)
-
-        @pl.when(jnp.logical_not(mine))
-        def _():
-            push(wo, wop.at[quarter], sw.at[plane], rw.at[quarter], there).start()
-
-        @pl.when(mine)
-        def _():
-            wop[quarter] = wo[...]
-
-    gather_finish(first, xp, sx, rx, row, col, place)
-    for copy in spread:
+    for copy in second:
         copy.wait_recv()
-    for j in range(4):
-        mine = jnp.logical_and(quarter == z, quarter == j)
-
-        @pl.when(jnp.logical_not(mine))
-        def _():
-            push(wo, wop.at[j], sw.at[j], rw.at[j], (row, quarter * QUAD + j)).wait_recv()
-
     for k in range(8):
         lanes = slice(k * 128, k * 128 + 128)
-        gains[:, lanes] = (tiles[4 * k] + tiles[4 * k + 1]) + (tiles[4 * k + 2] + tiles[4 * k + 3])
-        times[:, lanes] = tiles[(k // QUAD) * 16 + z * QUAD + k % QUAD]
+        r, plane = k // PLANES, k % PLANES
+        gains[:, lanes] = (tiles[r * QUAD, plane] + tiles[r * QUAD + 1, plane]) + (
+            tiles[r * QUAD + 2, plane] + tiles[r * QUAD + 3, plane]
+        )
+        times[:, lanes] = tiles[k, z]
     for k in range(16):
-        labels[:, k * 128 : k * 128 + 128] = tiles[(z // 2) * 16 + k]
-    for copy in spread:
-        copy.wait_send()
-    for plane in range(PLANES):
-        there = (row, plane * QUAD + z)
-        mine = jnp.logical_and(z == plane, quarter == z)
-
-        @pl.when(jnp.logical_not(mine))
-        def _():
-            push(wo, wop.at[quarter], sw.at[plane], rw.at[quarter], there).wait_send()
-
-
-def project_body(
-    xp, wqp, gains, times, freq, cot,
-    s1, qkvt, cotp,
-    wt, box, cs, sn, sa, ra, sz, rz,
-):
-    row, col, z, place = places()
-    meet(plane_near(row, col) + line_all(row, col))
-    first = gather_start(cot, cotp, sa, ra, row, col, place)
-    cotp[place] = cot[...]
-    wt[...] = jnp.transpose(wqp[...])
+        labels[:, k * 128 : k * 128 + 128] = tiles[(z // 2) * QUAD + k % QUAD, k // QUAD]
     phases = times[3:4, :] * freq[...]
     cs[...] = jnp.cos(phases)
     sn[...] = jnp.sin(phases)
     gain = gains[0:1, :]
-
-    def step(t, unused):
-        rows = pl.ds(pl.multiple_of(t * 256, 256), 256)
-        values = xp[rows, :].astype(f32)
-        normed = values * norm_scale(values)
-        scaled = (normed * gain).astype(bf16)
-        s1[rows, :] = scaled
-        out = mm_nt(wt[...], scaled)
-        cos_part, sin_part = cs[:, rows], sn[:, rows]
-        lanes = pl.ds(pl.multiple_of((t % 2) * 256, 256), 256)
+    rows_in.finish()
+
+    def scale(t, unused):
+        values = xp[t].astype(f32)
+        s1[t] = (values * norm_scale(values) * gain).astype(bf16)
+        return unused
+
+    lax.fori_loop(0, MEMBERS, scale, 0)
+    kept = [fetch(xp, xp_out, keep.at[0]), fetch(s1, s1_out, keep.at[1])]
+    for copy in pieces:
+        copy.wait_recv()
+    for j in range(16):
+        cots[j * 8 : j * 8 + 8, :] = cotr[jnp.clip(deal[j], 0, 15)]
+    cot_in = Gather(cotp, sa, ra)
+    cot_in.start(cots)
+    cotp[place] = cots[...]
+    for copy in weights:
+        copy.wait_recv()
+    kept.append(fetch(wqp, wqp_out, keep.at[2]))
+    for plane in range(PLANES):
+        there = (row, plane * QUAD + z)
+        mine = jnp.logical_and(z == plane, quarter == z)
+
+        @pl.when(jnp.logical_not(mine))
+        def _():
+            push(wo, wop.at[quarter], sw.at[plane], rw.at[quarter], there).start()
+
+        @pl.when(mine)
+        def _():
+            wop[quarter] = wo[...]
+
+    blocks = []
+    for bits in range(1, 8):
+        there = in_plane(row, col, bits)
+        blocks.append(
+            push(wgs.at[flip(place, bits)], wgp.at[place], sg.at[bits], rg.at[bits], there)
+        )
+        blocks[-1].start()
+    wgp[place] = wgs[place]
+    for k in range(8):
+        wt[:, k * 128 : k * 128 + 128] = jnp.transpose(
+            jnp.concatenate([wqp[4 * k + j] for j in range(4)], axis=0)
+        )
+    for group in range(2):
+
+        def project(t, unused):
+            number = group * 4 + 2 * t
+            rows = block(2 * group + t, 256)
+            scaled = jnp.concatenate([s1[number], s1[number + 1]], axis=0)
+            out = mm_nt(wt[...], scaled)
+            cos_part, sin_part = cs[:, rows], sn[:, rows]
+            lanes = block(t, 256)
+            for head in range(2):
+                pair = group * 2 + head
+                for part in range(2):
+                    base = part * 128 + head * 64
+                    former, latter = out[base : base + 32], out[base + 32 : base + 64]
+                    factor = 0.125 if part == 0 else 1.0
+                    turned = former * cos_part - latter * sin_part
+                    other = latter * cos_part + former * sin_part
+                    at = part * 64
+                    box[pair, at : at + 32, lanes] = (turned * factor).astype(bf16)
+                    box[pair, at + 32 : at + 64, lanes] = (other * factor).astype(bf16)
+                at = 256 + head * 64
+                box[pair, 128:192, lanes] = out[at : at + 64].astype(bf16)
+            return unused
+
+        lax.fori_loop(0, 2, project, 0)
         for head in range(2):
-            pair = (t // 2) * 2 + head
-            for part in range(2):
-                base = part * 128 + head * 64
-                former, latter = out[base : base + 32], out[base + 32 : base + 64]
-                factor = 0.125 if part == 0 else 1.0
-                turned = former * cos_part - latter * sin_part
-                other = latter * cos_part + former * sin_part
-                box[pair, part * 64 : part * 64 + 32, lanes] = (turned * factor).astype(bf16)
-                box[pair, part * 64 + 32 : part * 64 + 64, lanes] = (other * factor).astype(bf16)
-            box[pair, 128:192, lanes] = out[256 + head * 64 : 256 + head * 64 + 64].astype(bf16)
-        return unused
-
-    lax.fori_loop(0, 4, step, 0)
-    mine = pl.ds(pl.multiple_of(z * 512, 512), 512)
-    copies = []
-    for bits in (3, 2, 1):
-        copy = push(
-            box.at[flip(z, bits)], qkvt.at[:, mine], sz.at[bits], rz.at[bits], on_line(row, col, bits)
-        )
-        copy.start()
-        copies.append(copy)
-    qkvt[:, mine] = box[z]
-    gather_finish(first, cotp, sa, ra, row, col, place)
-    for copy in copies:
+            pair = group * 2 + head
+
+            @pl.when(z != pair)
+            def _():
+                push(
+                    box.at[pair], qkvt.at[:, block(z, 512)], sz.at[pair], rz.at[z],
+                    (row, pair * QUAD + quarter),
+                ).start()
+
+            @pl.when(z == pair)
+            def _():
+                qkvt[:, block(z, 512)] = box[pair]
+
+    cot_in.finish()
+    kept.append(fetch(cotp, cotp_out, keep.at[3]))
+    for copy in blocks:
+        copy.wait_recv()
+    for j in range(4):
+        mine = jnp.logical_and(quarter == z, quarter == j)
+
+        @pl.when(jnp.logical_not(mine))
+        def _():
+            push(wo, wop.at[j], sw.at[j], rw.at[j], (row, quarter * QUAD + j)).wait_recv()
+
+    for plane in range(PLANES):
+        there = (row, plane * QUAD + z)
+        mine = jnp.logical_and(z == plane, quarter == z)
+
+        @pl.when(jnp.logical_not(mine))
+        def _():
+            push(wo, wop.at[quarter], sw.at[plane], rw.at[quarter], there).wait_send()
+
+    for pair in range(4):
+
+        @pl.when(z != pair)
+        def _():
+            copy = push(
+                box.at[pair], qkvt.at[:, block(pair, 512)], sz.at[pair], rz.at[pair],
+                (row, pair * QUAD + quarter),
+            )
+            copy.wait_send()
+            copy.wait_recv()
+
+    rows_in.close()
+    cot_in.close()
+    for copy in first + second + weights + pieces + blocks:
+        copy.wait_send()
+    for copy in kept:
         copy.wait()
 
 
@@ -766,136 +867,221 @@
 
 def branch_body(
     low, wop, x, gains,
-    atp, hidden, s2p,
-    atn, part, mine, sz, rz, inbox, outbox, second, ss, rs, sa, ra,
+    atp, hidden, s2,
+    atn, part, sz, rz, inbox, outbox, second, ss, rs,
 ):
     row, col, z, place = places()
     meet(plane_near(row, col) + line_all(row, col))
-    rows = pl.ds(pl.multiple_of((z % 2) * 64, 64), 64)
-    lanes = pl.ds(pl.multiple_of((z // 2) * 512, 512), 512)
+    rows, lanes = block(z % 2, 64), block(z // 2, 512)
     copies = []
     for bits in (3, 2, 1):
-        theirs = pl.ds(pl.multiple_of(flip(z, bits) * 512, 512), 512)
         copy = push(
-            low.at[:, theirs], atp.at[rows, lanes], sz.at[bits], rz.at[bits], on_line(row, col, bits)
+            low.at[:, block(flip(z, bits), 512)],
+            atp.at[rows, lanes],
+            sz.at[bits],
+            rz.at[bits],
+            on_line(row, col, bits),
         )
         copy.start()
         copies.append(copy)
-    atp[rows, lanes] = low[:, pl.ds(pl.multiple_of(z * 512, 512), 512)]
+    atp[rows, lanes] = low[:, block(z, 512)]
     for copy in copies:
         copy.wait()
     atn[...] = jnp.transpose(atp[...])
-    for q in range(MEMBERS):
-        part[q] = mm(atn[q * 128 : q * 128 + 128, :], wop[...]).astype(bf16)
-    first = scatter_start(part, inbox, ss, rs, row, col)
-    sent = scatter_middle(first, part, inbox, outbox, second, ss, rs, row, col, place)
-    total = scatter_finish(first, sent, part, inbox, second, place)
-    state = x[...].astype(f32) + total
+    total = Scatter(part, inbox, outbox, second, ss, rs)
+    core = col % 2
+    for bits in (3, 2, 1, 0):
+        chip = flip(place // 2, bits)
+        part[2 * chip + 1 - core] = mm(atn[block(2 * chip + 1 - core, 128), :], wop[...]).astype(bf16)
+    for bits in range(4):
+        total.near(flip(place // 2, bits), bits)
+    for bits in (3, 2, 1, 0):
+        chip = flip(place // 2, bits)
+        part[2 * chip + core] = mm(atn[block(2 * chip + core, 128), :], wop[...]).astype(bf16)
+    total.far_all()
+    state = x[...].astype(f32) + total.finish()
     hidden[...] = state
-    mine[...] = (state * norm_scale(state) * gains[1:2, :]).astype(bf16)
-    spread = gather_start(mine, s2p, sa, ra, row, col, place)
-    s2p[place] = mine[...]
-    gather_finish(spread, s2p, sa, ra, row, col, place)
-
-
-def ffn_body(s2, cot, wg, wd, out_part, d_part, gwd, gwg, wgs, inner_s, dgu):
+    s2[...] = (state * norm_scale(state) * gains[1:2, :]).astype(bf16)
+    total.close()
+
+
+def ffn_body(
+    s2, cotp_in, wg_in, w_down, hidden, gains,
+    out_keep, down_in, gwg_out, d_hidden, low, gain_term,
+    cotp, wg, s2p, wgs, wd, actives, factors, inner_s, dgu, d_part, out_part, gwd, gwg,
+    keep, sa, ra, sw, rw, sd, rd, inbox, outbox, second, ss, rs,
+):
+    row, col, z, place = places()
+    loads = [fetch(wg_in, wg, keep.at[0]), fetch(cotp_in, cotp, keep.at[1])]
+    meet(plane_near(row, col) + line_all(row, col))
+    rows_in = Gather(s2p, sa, ra)
+    rows_in.start(s2)
+    s2p[place] = s2[...]
+    downs = []
+    for bits in (3, 2, 1):
+        downs.append(
+            push(w_down, wd.at[block(z, 128), :], sw.at[bits], rw.at[bits], on_line(row, col, bits))
+        )
+        downs[-1].start()
+    wd[block(z, 128), :] = w_down[...]
+    loads[0].wait()
     for plane in range(PLANES):
         for r in range(2):
             at = (r * PLANES + plane) * 128
             wgs[at : at + 128, :] = wg[plane * 2 + r]
-
-    def step(t, unused):
-        rows = pl.ds(pl.multiple_of(t * 256, 256), 256)
-        both = mm(s2[rows, :], wgs[...])
+    for k in range(4):
+        chip = flip(place // 2, k)
+        if k:
+            rows_in.forward(2 * k)
+        rows_in.arrived(2 * k)
+        rows = block(chip, 256)
+        scaled = jnp.concatenate([s2p[2 * chip], s2p[2 * chip + 1]], axis=0)
+        both = mm(scaled, wgs[...])
         gate, upper = both[:, 0:512], both[:, 512:1024]
         sig = jax.nn.sigmoid(gate)
         active = gate * sig
-        inner = (active * upper).astype(bf16)
-        inner_s[rows, :] = inner
-        out_part[rows, :] = mm(inner, wd[...]).astype(bf16)
-        d_inner = mm_nt(cot[rows, :], wd[...])
-        dgu[rows, 0:512] = (d_inner * upper * sig * (1.0 + gate * (1.0 - sig))).astype(bf16)
-        dgu[rows, 512:1024] = (d_inner * active).astype(bf16)
-        d_part[rows, :] = mm_nt(dgu[rows, :], wgs[...]).astype(bf16)
-        return unused
-
-    lax.fori_loop(0, 4, step, 0)
-    for k in range(2):
-        cols = slice(k * 256, k * 256 + 256)
-        gwd[cols, :] = mm_tn(inner_s[:, cols], cot[...]).astype(bf16)
+        inner_s[rows, :] = (active * upper).astype(bf16)
+        actives[rows, :] = active
+        factors[rows, :] = upper * sig * (1.0 + gate * (1.0 - sig))
+    loads[1].wait()
+    cot_all = jnp.concatenate([cotp[t] for t in range(MEMBERS)], axis=0)
+    for k in range(4):
+        cols = slice(k * 128, k * 128 + 128)
+        gwd[k] = mm_tn(inner_s[:, cols], cot_all).astype(bf16)
+    grads = []
+    for bits in (3, 2, 1):
+        grads.append(
+            push(gwd.at[flip(z, bits)], down_in.at[z], sd.at[bits], rd.at[bits], on_line(row, col, bits))
+        )
+        grads[-1].start()
+    down_in[z] = gwd[z]
+    total = Scatter(d_part, inbox, outbox, second, ss, rs)
+    for copy in downs:
+        copy.wait_recv()
+    for k in range(4):
+        chip = flip(place // 2, k)
+        rows = block(chip, 256)
+        upstream = jnp.concatenate([cotp[2 * chip], cotp[2 * chip + 1]], axis=0)
+        d_inner = mm_nt(upstream, wd[...])
+        dgu[rows, 0:512] = (d_inner * factors[rows, :]).astype(bf16)
+        dgu[rows, 512:1024] = (d_inner * actives[rows, :]).astype(bf16)
+        tile = mm_nt(dgu[rows, :], wgs[...]).astype(bf16)
+        d_part[2 * chip] = tile[0:128]
+        d_part[2 * chip + 1] = tile[128:256]
+        total.near(chip, k)
+        if k > 1:
+            total.far(k - 1)
+    for k in range(4):
+        chip = flip(place // 2, k)
+        tile = mm(inner_s[block(chip, 256), :], wd[...]).astype(bf16)
+        out_part[2 * chip] = tile[0:128]
+        out_part[2 * chip + 1] = tile[128:256]
+        if k == 0:
+            total.far(3)
+    kept = [fetch(out_part, out_keep, keep.at[10])]
     for f in range(8):
         cols = slice(f * 128, f * 128 + 128)
-        gwg[(f % PLANES) * 2 + f // PLANES] = mm_tn(s2[:, cols], dgu[...]).astype(bf16)
-
-
-def hidden_back_body(
-    d_part, out_part, cot, hidden, gains, wop, atp,
-    grad, d_hidden, out, gwo, gain_term,
-    low, dbp, dat, ia, oa, na, sa, ra, ib, ob, nb, sb, rb, sg, rg, sz, rz,
-):
-    row, col, z, place = places()
-    meet(plane_near(row, col) + line_all(row, col))
-    first = scatter_start(d_part, ia, sa, ra, row, col)
-    sent = scatter_middle(first, d_part, ia, oa, na, sa, ra, row, col, place)
-    d_scaled = scatter_finish(first, sent, d_part, ia, na, place)
+        lhs = jnp.concatenate([s2p[t, :, cols] for t in range(MEMBERS)], axis=0)
+        at = (f % PLANES) * 2 + f // PLANES
+        gwg[at] = mm_tn(lhs, dgu[...]).astype(bf16)
+        kept.append(fetch(gwg.at[at], gwg_out.at[at], keep.at[2 + f]))
+    d_scaled = total.finish()
     state = hidden[...]
     scale = norm_scale(state)
     normed = state * scale
     gain_term[...] = jnp.broadcast_to(jnp.sum(d_scaled * normed, axis=0, keepdims=True), (8, 1024))
-    d_state = cot[...].astype(f32) + norm_back(d_scaled * gains[1:2, :], normed, scale)
+    d_state = cotp[place].astype(f32) + norm_back(d_scaled * gains[1:2, :], normed, scale)
     d_hidden[...] = d_state
     low[...] = d_state.astype(bf16)
-    spread = gather_start(low, dbp, sg, rg, row, col, place)
+    rows_in.close()
+    total.close()
+    for copy in grads:
+        copy.wait_recv()
+    for copy in downs + grads:
+        copy.wait_send()
+    for copy in kept:
+        copy.wait()
+
+
+def attended_back_body(
+    low, wop, atp,
+    grad, gwo,
+    dbp, dat, sg, rg, sz, rz,
+):
+    row, col, z, place = places()
+    meet(plane_near(row, col) + line_all(row, col))
+    quarter = col % QUAD
+    rows_in = Gather(dbp, sg, rg)
+    rows_in.start(low)
     dbp[place] = low[...]
-    other_first = scatter_start(out_part, ib, sb, rb, row, col)
-    gather_finish(spread, dbp, sg, rg, row, col, place)
-    for q in range(MEMBERS):
-        dat[:, q * 128 : q * 128 + 128] = mm_nt(wop[...], dbp[q]).astype(bf16)
-    mine = pl.ds(pl.multiple_of(z * 512, 512), 512)
-    copies = []
-    for bits in (3, 2, 1):
-        pair = flip(z, bits)
-        rows = pl.ds(pl.multiple_of((pair % 2) * 64, 64), 64)
-        lanes = pl.ds(pl.multiple_of((pair // 2) * 512, 512), 512)
-        copy = push(
-            dat.at[rows, lanes], grad.at[:, mine], sz.at[bits], rz.at[bits], on_line(row, col, bits)
-        )
-        copy.start()
-        copies.append(copy)
-    grad[:, mine] = dat[
-        pl.ds(pl.multiple_of((z % 2) * 64, 64), 64),
-        pl.ds(pl.multiple_of((z // 2) * 512, 512), 512),
-    ]
-    other_sent = scatter_middle(other_first, out_part, ib, ob, nb, sb, rb, row, col, place)
+    for k in range(4):
+        chip = flip(place // 2, k)
+        if k:
+            rows_in.forward(2 * k)
+        rows_in.arrived(2 * k)
+        for core in range(2):
+            dat[:, block(2 * chip + core, 128)] = mm_nt(wop[...], dbp[2 * chip + core]).astype(bf16)
+        if k % 2 == 0:
+            continue
+        group = row if k == 1 else 1 - row
+        for head in range(2):
+            pair = group * 2 + head
+            source = dat.at[head * 64 : head * 64 + 64, block(group, 512)]
+
+            @pl.when(z != pair)
+            def _():
+                push(
+                    source, grad.at[:, block(z, 512)], sz.at[pair], rz.at[z],
+                    (row, pair * QUAD + quarter),
+                ).start()
+
+            @pl.when(z == pair)
+            def _():
+                grad[:, block(z, 512)] = source[...]
+
     total = mm(atp[:, 0:128], dbp[0])
     for q in range(1, MEMBERS):
         total = total + mm(atp[:, q * 128 : q * 128 + 128], dbp[q])
     gwo[...] = total.astype(bf16)
-    branch = scatter_finish(other_first, other_sent, out_part, ib, nb, place)
-    out[...] = (state + branch).astype(bf16)
-    for copy in copies:
-        copy.wait()
+    for pair in range(4):
+
+        @pl.when(z != pair)
+        def _():
+            copy = push(
+                dat.at[0:64, 0:512], grad.at[:, block(pair, 512)], sz.at[pair], rz.at[pair],
+                (row, pair * QUAD + quarter),
+            )
+            copy.wait_send()
+            copy.wait_recv()
+
+    rows_in.close()
 
 
 def last_body(
-    dproj, wqp, s1, xp, gains, d_hidden, gwo, slots, gwg, gain_two, bias_tile,
-    grad_tokens, grad_q, grad_o, out, gwg_in, tile,
-    dpt, dpn, part, gq, gqin, goin, pack, tiles,
-    sz, rz, inbox, outbox, second, ss, rs, sq, rq, st, rt, sw, rw, sg, rg, sc, rc,
+    dproj, wqp_in, s1_in, xp_in, out_in, gains, d_hidden, hidden, gwo, gwg, gain_two, bias_tile, deal,
+    grad_tokens, gqin, goin, gwg_in, sums, out,
+    wqp, s1, xp, out_part, pieces, slots, keep, dpt, dpn, part, gq, pack, packs, packed,
+    sz, rz, inbox, outbox, second, ss, rs,
+    sq, rq, st, rt, su, ru, sw, rw, sg, rg, sc, rc, inbox2, outbox2, second2, ss2, rs2,
 ):
     row, col, z, place = places()
     me = row * 16 + col
     quarter = col % QUAD
+    core = col % 2
+    loads = [
+        fetch(out_in, out_part, keep.at[3]),
+        fetch(s1_in, s1, keep.at[0]),
+        fetch(xp_in, xp, keep.at[1]),
+        fetch(wqp_in, wqp, keep.at[2]),
+    ]
     meet([anyone(row, col, bits) for bits in range(1, 32)])
     copies = []
-    lanes = pl.ds(pl.multiple_of((z // 2) * 512, 512), 512)
+    lanes = block(z // 2, 512)
     for bits in (3, 2, 1):
-        theirs = pl.ds(pl.multiple_of(flip(z, bits) * 512, 512), 512)
         for kind in range(3):
-            rows = pl.ds(pl.multiple_of(kind * 128 + (z % 2) * 64, 64), 64)
             copy = push(
-                dproj.at[kind * 64 : kind * 64 + 64, theirs],
-                dpt.at[rows, lanes],
+                dproj.at[kind * 64 : kind * 64 + 64, block(flip(z, bits), 512)],
+                dpt.at[pl.ds(pl.multiple_of(kind * 128 + (z % 2) * 64, 64), 64), lanes],
                 sz.at[bits, kind],
                 rz.at[bits, kind],
                 on_line(row, col, bits),
@@ -904,9 +1090,11 @@
             copies.append(copy)
     for kind in range(3):
         rows = pl.ds(pl.multiple_of(kind * 128 + (z % 2) * 64, 64), 64)
-        dpt[rows, lanes] = dproj[
-            kind * 64 : kind * 64 + 64, pl.ds(pl.multiple_of(z * 512, 512), 512)
-        ]
+        dpt[rows, lanes] = dproj[kind * 64 : kind * 64 + 64, block(z, 512)]
+    loads[0].wait()
+    output = Scatter(out_part, inbox2, outbox2, second2, ss2, rs2)
+    output.near_all()
+    output.far_all()
     spread = []
     for bits in range(1, 8):
         there = in_plane(row, col, bits)
@@ -914,6 +1102,18 @@
         copy.start()
         spread.append(copy)
     gwg_in[place] = gwg[place]
+    for copy in loads[1:]:
+        copy.wait()
+    rows_out = (hidden[...] + output.finish()).astype(bf16)
+    for j in range(16):
+        pieces[j] = rows_out[j * 8 : j * 8 + 8, :]
+    for d in range(16):
+        number = 0
+        for j in range(1, 16):
+            number = jnp.where(deal[j] == d, j, number)
+        slots[d] = pieces[number]
+    for copy in copies:
+        copy.wait_recv()
     for bits in range(1, 16):
         there = (row, flip(col, bits))
         copy = push(slots.at[there[1]], out.at[col], sc.at[bits], rc.at[bits], there)
@@ -932,42 +1132,63 @@
         def _():
             goin[z] = gwo[j]
 
-    for copy in copies:
-        copy.wait()
     dpn[...] = jnp.transpose(dpt[...])
-    gain_one = gains[0:1, :]
-    term = jnp.zeros((1, 1024), f32)
-    for q in range(MEMBERS):
-        values = xp[q].astype(f32)
-        d_scaled = mm_nt(dpn[q * 128 : q * 128 + 128, :], wqp[...])
-        term = term + jnp.sum(d_scaled * (values * norm_scale(values)), axis=0, keepdims=True)
-        part[q] = d_scaled.astype(bf16)
-    first = scatter_start(part, inbox, ss, rs, row, col)
-    for k in range(8):
-        pack[k] = bias_tile[...]
-        pack[k, 0:1, :] = term[:, k * 128 : k * 128 + 128]
-        pack[k, 1:2, :] = gain_two[0:1, k * 128 : k * 128 + 128]
     for f in range(8):
-        chunk = mm_tn(s1[:, f * 128 : f * 128 + 128], dpn[...]).astype(bf16)
+        lhs = jnp.concatenate([s1[t, :, f * 128 : f * 128 + 128] for t in range(MEMBERS)], axis=0)
+        chunk = mm_tn(lhs, dpn[...]).astype(bf16)
         for j in range(4):
             gq[f * 4 + j] = chunk[j * 32 : j * 32 + 32, :]
-    sent = scatter_middle(first, part, inbox, outbox, second, ss, rs, row, col, place)
-    for bits in range(1, 32):
+    for bits in range(31, 0, -1):
         there = anyone(row, col, bits)
         number = there[0] * 16 + there[1]
         copy = push(gq.at[number], gqin.at[me], sq.at[bits], rq.at[bits], there)
         copy.start()
         spread.append(copy)
-        copy = push(pack.at[number // 4], tiles.at[me], st.at[bits], rt.at[bits], there)
+    gqin[me] = gq[me]
+    gain_one = gains[0:1, :]
+    total = Scatter(part, inbox, outbox, second, ss, rs)
+    term = jnp.zeros((1, 1024), f32)
+    for own in range(2):
+        for bits in (3, 2, 1, 0):
+            number = 2 * flip(place // 2, bits) + (core if own else 1 - core)
+            values = xp[number].astype(f32)
+            d_scaled = mm_nt(dpn[block(number, 128), :], wqp[...])
+            term = term + jnp.sum(d_scaled * (values * norm_scale(values)), axis=0, keepdims=True)
+            part[number] = d_scaled.astype(bf16)
+        if own == 0:
+            total.near_all()
+    total.far_all()
+    for k in range(8):
+        pack[k] = bias_tile[...]
+        pack[k, 0:1, :] = term[:, k * 128 : k * 128 + 128]
+        pack[k, 1:2, :] = gain_two[0:1, k * 128 : k * 128 + 128]
+    first = []
+    for bits in range(1, 8):
+        there = in_plane(row, col, bits)
+        copy = push(
+            pack.at[pl.ds(there[0] * PLANES, PLANES)], packs.at[place], st.at[bits], rt.at[bits], there
+        )
+        copy.start()
+        first.append(copy)
+    packs[place] = pack[pl.ds(row * PLANES, PLANES)]
+    for copy in first:
+        copy.wait_recv()
+    summed = packs[0]
+    for p in range(1, MEMBERS):
+        summed = summed + packs[p]
+    packed[...] = summed
+    for bits in (1, 2, 3):
+        copy = push(
+            packed.at[flip(z, bits)], sums.at[z], su.at[bits], ru.at[bits], on_line(row, col, bits)
+        )
         copy.start()
         spread.append(copy)
-    gqin[me] = gq[me]
-    tiles[me] = pack[me // 4]
-    d_one = scatter_finish(first, sent, part, inbox, second, place)
-    own = xp[place].astype(f32)
-    scale = norm_scale(own)
+    sums[z] = packed[z]
+    d_one = total.finish()
+    own_rows = xp[place].astype(f32)
+    scale = norm_scale(own_rows)
     grad_tokens[...] = (
-        d_hidden[...] + norm_back(d_one * gain_one, own * scale, scale)
+        d_hidden[...] + norm_back(d_one * gain_one, own_rows * scale, scale)
     ).astype(bf16)
     for copy in spread:
         copy.wait_recv()
@@ -980,8 +1201,31 @@
                 gwo.at[0], goin.at[plane], sw.at[plane], rw.at[plane], (row, plane * QUAD + z)
             ).wait_recv()
 
+    for j in range(4):
+        there = (row, quarter * QUAD + j)
+        mine = jnp.logical_and(quarter == z, quarter == j)
+
+        @pl.when(jnp.logical_not(mine))
+        def _():
+            push(gwo.at[j], goin.at[z], sw.at[j], rw.at[z], there).wait_send()
+
+    for copy in copies + first + spread:
+        copy.wait_send()
+    total.close()
+    output.close()
+
+
+def finish_body(
+    place_info, grad_tokens_in, gqin, goin, out_in, gwg, gwd, tiles,
+    out, grad_tokens, grad_q, grad_o, grad_gu, grad_d, grad_gains, grad_bias,
+):
+    grad_tokens[...] = grad_tokens_in[...]
+    out[...] = out_in[...]
     grad_o[...] = (goin[0].astype(f32) + goin[1].astype(f32)) + (
         goin[2].astype(f32) + goin[3].astype(f32)
+    )
+    grad_d[...] = (gwd[0].astype(f32) + gwd[1].astype(f32)) + (
+        gwd[2].astype(f32) + gwd[3].astype(f32)
     )
     for p in range(MEMBERS):
         total = jnp.zeros((32, 384), f32)
@@ -990,19 +1234,19 @@
         for kind in range(3):
             at = kind * 1024 + p * 128
             grad_q[:, at : at + 128] = total[:, kind * 128 : kind * 128 + 128]
-    total = tiles[0]
-    for k in range(1, 32):
-        total = total + tiles[k]
-    tile[...] = total
-    for copy in spread:
-        copy.wait_send()
-    for j in range(4):
-        there = (row, quarter * QUAD + j)
-        mine = jnp.logical_and(quarter == z, quarter == j)
-
-        @pl.when(jnp.logical_not(mine))
-        def _():
-            push(gwo.at[j], goin.at[z], sw.at[j], rw.at[z], there).wait_send()
+        for half in range(2):
+            for plane in range(PLANES):
+                unit = (p // QUAD) * 16 + plane * QUAD + p % QUAD
+                at = half * 512 + plane * 128
+                start = half * 4096 + unit * 128
+                grad_gu[:, start : start + 128] = gwg[p, :, at : at + 128].astype(f32)
+    total = (tiles[0] + tiles[1]) + (tiles[2] + tiles[3])
+    quarter = place_info[0]
+    chosen = jnp.zeros((2, 32), f32)
+    for k in range(4):
+        chosen = chosen + jnp.where(quarter == k, total[0:2, k * 32 : k * 32 + 32], 0.0)
+    grad_gains[...] = chosen
+    grad_bias[...] = total[2:4, 0:16]
 
 
 def sds(shape, dtype):
@@ -1013,7 +1257,7 @@
     return pltpu.SemaphoreType.DMA(shape)
 
 
-def kernel(body, name, specs, outs, scratch, number=None, cost=0):
+def kernel(body, name, specs, outs, scratch, number=None, cost=0, places_out=None):
     params = dict(vmem_limit_bytes=56 << 20)
     if number is not None:
         params.update(collective_id=number, has_side_effects=True)
@@ -1022,7 +1266,7 @@
         name=name,
         in_specs=specs,
         out_shape=outs,
-        out_specs=[VM] * len(outs),
+        out_specs=places_out or [VM] * len(outs),
         scratch_shapes=scratch,
         compiler_params=pltpu.CompilerParams(**params),
         cost_estimate=pl.CostEstimate(flops=cost, bytes_accessed=cost // 300, transcendentals=0),
@@ -1039,69 +1283,57 @@
     place = row * QUAD + q
     rows, width = tokens.shape
     lines = [[plane * QUAD + k for plane in range(PLANES)] for k in range(QUAD)]
-    down = lax.all_gather(w_down, "col", axis=0, tiled=True, axis_index_groups=lines)
-    spot = (q * 32 + jnp.arange(32, dtype=jnp.int32))[:, None] == jnp.arange(128)[None, :]
-    gain_rows = jnp.sum(
-        jnp.where(
-            spot[None], jnp.stack([gain_attn, gain_ffn]).astype(f32)[:, :, None], 0.0
-        ),
-        axis=1,
-    )
-    tile = jnp.concatenate(
-        [
-            gain_rows,
-            variate_ids.astype(f32)[None],
-            time_ids.astype(f32)[None],
-            jnp.pad(lengths[0].astype(f32), (0, 128 - lengths.shape[1]))[None],
-            jnp.zeros((3, 128), f32),
-        ],
-        axis=0,
-    )
     freq = jnp.exp(-math.log(10000.0) * jnp.arange(32, dtype=f32) / 32)[:, None]
-
-    xp, wqp, wop, wgp, cotr, tiles, gains, times, labels = kernel(
-        gather_body,
-        "gather_all",
-        [VM] * 6,
+    target = deal[0, 0]
+
+    xp, wqp, wop, wgp, cotp, s1, qkvt, gains, labels = kernel(
+        enter_body,
+        "enter",
+        [VM] * 9 + [SM, SM, VM],
         [
             sds((8, rows, width), bf16),
             sds((32, 32, 384), bf16),
             sds((4, 32, 1024), bf16),
             sds((8, 32, 1024), bf16),
-            sds((16, 8, width), bf16),
-            sds((32, 8, 128), f32),
-            sds((8, 1024), f32),
+            sds((8, rows, width), bf16),
+            sds((8, rows, width), bf16),
+            sds((192, 2048), bf16),
             sds((8, 1024), f32),
             sds((8, 2048), f32),
         ],
-        [pltpu.VMEM((8, 32, 384), bf16), pltpu.VMEM((8, 32, 1024), bf16)]
-        + [dma(8), dma(8), dma(32), dma(32), dma(32), dma(32), dma(4), dma(4)]
-        + [dma(8), dma(8), dma(16), dma(16)],
-        number=1,
-    )(tokens, w_qkv, w_out, w_gate_up, cotangent.reshape(16, 8, width), tile)
-
-    gate_up = lax.all_gather(
-        wgp.reshape(256, 1024), "col", axis=0, tiled=True, axis_index_groups=lines
-    )
-    wqp = wqp.reshape(1024, 384)
-    wop = wop.reshape(128, 1024)
-    target = deal[0, 0]
-    cot = jnp.take(cotr, target, axis=0).reshape(rows, width)
-
-    s1, qkvt, cotp = kernel(
-        project_body,
-        "project",
-        [VM] * 6,
-        [sds((1024, width), bf16), sds((192, 2048), bf16), sds((8, rows, width), bf16)],
         [
+            pltpu.VMEM((8, rows, width), bf16),
+            pltpu.VMEM((32, 32, 384), bf16),
+            pltpu.VMEM((8, rows, width), bf16),
+            pltpu.VMEM((8, rows, width), bf16),
+            dma(4),
+            pltpu.VMEM((8, 32, 384), bf16),
+            pltpu.VMEM((8, 32, 1024), bf16),
+            pltpu.VMEM((16, 8, width), bf16),
+            pltpu.VMEM((rows, width), bf16),
+            pltpu.VMEM((8, 128), f32),
+            pltpu.VMEM((4, 8, 128), f32),
+            pltpu.VMEM((8, 4, 8, 128), f32),
             pltpu.VMEM((384, 1024), bf16),
             pltpu.VMEM((4, 192, 512), bf16),
             pltpu.VMEM((32, 1024), f32),
             pltpu.VMEM((32, 1024), f32),
-            dma(8), dma(8), dma(4), dma(4),
-        ],
-        number=2,
-    )(xp.reshape(1024, width), wqp, gains, times, freq, cot)
+            pltpu.VMEM((8, 1024), f32),
+        ]
+        + [dma(8), dma(8), dma(32), dma(32), dma(4), dma(4), dma(8), dma(8), dma(4), dma(4)]
+        + [dma(8), dma(8), dma(16), dma(16), dma(8), dma(8), dma(4), dma(4)],
+        number=1,
+        places_out=[ANY, ANY, VM, VM, ANY, ANY, VM, VM, VM],
+    )(
+        tokens, w_qkv, w_out, w_gate_up, cotangent.reshape(16, 8, width), gain_attn[None],
+        gain_ffn[None], variate_ids[None], time_ids[None], lengths, target, freq,
+    )
+
+    gate_up = lax.all_gather(
+        wgp.reshape(256, 1024), "col", axis=0, tiled=True, axis_index_groups=lines
+    )
+    wqp = wqp.reshape(1024, 384)
+    wop = wop.reshape(128, 1024)
 
     head = place * 2 + z % 2
     info = jnp.concatenate(
@@ -1124,74 +1356,70 @@
         cost=2 * 10**9,
     )(info, bias, qkvt, labels)
 
-    atp, hidden, s2p = kernel(
+    atp, hidden, s2 = kernel(
         branch_body,
         "branch",
         [VM] * 4,
-        [sds((128, 1024), bf16), sds((rows, width), f32), sds((8, rows, width), bf16)],
+        [sds((128, 1024), bf16), sds((rows, width), f32), sds((rows, width), bf16)],
         [
             pltpu.VMEM((1024, 128), bf16),
             pltpu.VMEM((8, rows, width), bf16),
-            pltpu.VMEM((rows, width), bf16),
             dma(4), dma(4),
         ]
-        + scatter_scratch(rows, width)
-        + [dma(8), dma(8)],
-        number=3,
+        + scatter_scratch(rows, width),
+        number=2,
     )(low, wop, tokens, gains)
 
-    out_part, d_part, gwd, gwg = kernel(
+    out_part, down_in, gwg, d_hidden, d_branch, gain_two = kernel(
         ffn_body,
         "ffn",
-        [VM] * 4,
+        [VM, ANY, ANY, VM, VM, VM],
         [
-            sds((1024, width), bf16),
-            sds((1024, width), bf16),
-            sds((512, width), bf16),
+            sds((8, rows, width), bf16),
+            sds((4, rows, width), bf16),
             sds((8, 128, 1024), bf16),
-        ],
-        [
-            pltpu.VMEM((1024, 1024), bf16),
-            pltpu.VMEM((1024, 512), bf16),
-            pltpu.VMEM((1024, 1024), bf16),
-        ],
-        cost=10**10,
-    )(s2p.reshape(1024, width), cotp.reshape(1024, width), gate_up.reshape(8, 128, 1024), down)
-
-    grad_down = lax.psum_scatter(
-        gwd, "col", scatter_dimension=0, tiled=True, axis_index_groups=lines
-    )
-    gate_up_sum = lax.psum_scatter(
-        gwg.reshape(1024, 1024), "col", scatter_dimension=0, tiled=True, axis_index_groups=lines
-    )
-
-    grad, d_hidden, out_rows, gwo, gain_two = kernel(
-        hidden_back_body,
-        "hidden_back",
-        [VM] * 7,
-        [
-            sds((64, 2048), bf16),
             sds((rows, width), f32),
             sds((rows, width), bf16),
-            sds((128, 1024), bf16),
             sds((8, 1024), f32),
         ],
         [
-            pltpu.VMEM((rows, width), bf16),
+            pltpu.VMEM((8, rows, width), bf16),
+            pltpu.VMEM((8, 128, 1024), bf16),
+            pltpu.VMEM((8, rows, width), bf16),
+            pltpu.VMEM((1024, 1024), bf16),
+            pltpu.VMEM((512, width), bf16),
+            pltpu.VMEM((1024, 512), f32),
+            pltpu.VMEM((1024, 512), f32),
+            pltpu.VMEM((1024, 512), bf16),
+            pltpu.VMEM((1024, 1024), bf16),
+            pltpu.VMEM((8, rows, width), bf16),
+            pltpu.VMEM((8, rows, width), bf16),
+            pltpu.VMEM((4, rows, width), bf16),
+            pltpu.VMEM((8, 128, 1024), bf16),
+            dma(11), dma(8), dma(8), dma(4), dma(4), dma(4), dma(4),
+        ]
+        + scatter_scratch(rows, width),
+        number=3,
+        cost=10**10,
+        places_out=[ANY, VM, ANY, VM, VM, VM],
+    )(s2, cotp, gate_up.reshape(8, 128, 1024), w_down, hidden, gains)
+
+    gate_up_sum = lax.psum_scatter(
+        gwg.reshape(1024, 1024), "col", scatter_dimension=0, tiled=True, axis_index_groups=lines
+    )
+
+    grad, gwo = kernel(
+        attended_back_body,
+        "attended_back",
+        [VM] * 3,
+        [sds((64, 2048), bf16), sds((128, 1024), bf16)],
+        [
             pltpu.VMEM((8, rows, width), bf16),
             pltpu.VMEM((128, 1024), bf16),
-        ]
-        + scatter_scratch(rows, width)
-        + scatter_scratch(rows, width)
-        + [dma(8), dma(8), dma(4), dma(4)],
+            dma(8), dma(8), dma(4), dma(4),
+        ],
         number=4,
-    )(
-        d_part.reshape(8, rows, width), out_part.reshape(8, rows, width), cot, hidden, gains, wop, atp
-    )
-
-    slot = jnp.arange(16, dtype=jnp.int32)
-    inverse = jnp.sum(slot[:, None] * (target[:, None] == slot[None, :]).astype(jnp.int32), axis=0)
-    slots = jnp.take(out_rows.reshape(16, 8, width), inverse, axis=0)
+    )(d_branch, wop, atp)
 
     dproj, bias_tile = kernel(
         attend_back_body,
@@ -1209,53 +1437,73 @@
         cost=5 * 10**9,
     )(info, qkvt, qa, ka, labels, freq, grad, att, den)
 
-    grad_tokens, grad_q, grad_o, out, gwg_in, sums = kernel(
+    grad_tokens, gqin, goin, gwg_in, sums, out = kernel(
         last_body,
         "last",
-        [VM] * 11,
+        [VM] + [ANY] * 4 + [VM] * 7 + [SM],
         [
             sds((rows, width), bf16),
-            sds((32, 3072), f32),
-            sds((32, 1024), f32),
+            sds((32, 32, 384), bf16),
+            sds((4, 32, 1024), bf16),
+            sds((8, 32, 1024), bf16),
+            sds((4, 8, 128), f32),
             sds((16, 8, width), bf16),
-            sds((8, 32, 1024), bf16),
-            sds((8, 128), f32),
         ],
         [
+            pltpu.VMEM((1024, 384), bf16),
+            pltpu.VMEM((8, rows, width), bf16),
+            pltpu.VMEM((8, rows, width), bf16),
+            pltpu.VMEM((8, rows, width), bf16),
+            pltpu.VMEM((16, 8, width), bf16),
+            pltpu.VMEM((16, 8, width), bf16),
+            dma(4),
             pltpu.VMEM((384, 1024), bf16),
             pltpu.VMEM((1024, 384), bf16),
             pltpu.VMEM((8, rows, width), bf16),
             pltpu.VMEM((32, 32, 384), bf16),
-            pltpu.VMEM((32, 32, 384), bf16),
-            pltpu.VMEM((4, 32, 1024), bf16),
             pltpu.VMEM((8, 8, 128), f32),
-            pltpu.VMEM((32, 8, 128), f32),
+            pltpu.VMEM((8, 4, 8, 128), f32),
+            pltpu.VMEM((4, 8, 128), f32),
             dma(4, 3), dma(4, 3),
         ]
         + scatter_scratch(rows, width)
-        + [dma(32), dma(32), dma(32), dma(32), dma(4), dma(4), dma(8), dma(8), dma(16), dma(16)],
+        + [dma(32), dma(32), dma(8), dma(8), dma(4), dma(4), dma(4), dma(4), dma(8), dma(8)]
+        + [dma(16), dma(16)]
+        + scatter_scratch(rows, width),
         number=5,
     )(
-        dproj, wqp, s1, xp, gains, d_hidden, gwo.reshape(4, 32, 1024), slots,
-        gate_up_sum.reshape(8, 32, 1024), gain_two, bias_tile,
-    )
-    grad_gate_up = (
-        gwg_in.reshape(2, QUAD, 32, 2, PLANES, 128)
-        .transpose(2, 3, 0, 4, 1, 5)
-        .reshape(32, 8192)
-        .astype(f32)
-    )
-    gain_grads = lax.dynamic_slice_in_dim(sums[0:2], q * 32, 32, 1)
+        dproj, wqp, s1, xp, out_part, gains, d_hidden, hidden, gwo.reshape(4, 32, 1024),
+        gate_up_sum.reshape(8, 32, 1024), gain_two, bias_tile, target,
+    )
+    out, grad_tokens, grad_q, grad_o, grad_gate_up, grad_down, gain_grads, bias_grads = kernel(
+        finish_body,
+        "finish",
+        [SM] + [VM] * 7,
+        [
+            sds((rows, width), bf16),
+            sds((rows, width), bf16),
+            sds((32, 3072), f32),
+            sds((32, 1024), f32),
+            sds((32, 8192), f32),
+            sds((rows, width), f32),
+            sds((2, 32), f32),
+            sds((2, 16), f32),
+        ],
+        [],
+    )(
+        q[None].astype(jnp.int32), grad_tokens, gqin, goin, out.reshape(rows, width), gwg_in,
+        down_in, sums,
+    )
     return (
-        out.reshape(rows, width),
+        out,
         grad_tokens,
         grad_q,
         grad_o,
         grad_gate_up,
-        grad_down.astype(f32),
+        grad_down,
         gain_grads[0],
         gain_grads[1],
-        sums[2:4, :16],
+        bias_grads,
     )
 
 

time: 352 us -> 307 us (0.87)
  Pallas kernels: 314 us -> 278 us
  local copies, waits for them, and re-layouts: 13.3 us -> 1.96 us
  waiting for transfers between devices: 2.11 us -> 10.3 us
  other arithmetic: 7.6 us -> 1.89 us
    pallas_call x5, Pallas kernels: 242 us -> 215 us  [the longest x1 64.2 us: plane_shards(): kernel(last_body, 'last', [VM] + [ANY] * 4 + [VM] * 7 + [SM], [sds((rows,...]
    pallas_call x1, Pallas kernels: 47 us -> 37.6 us  [plane_shards(): kernel(branch_body, 'branch', [VM] * 4, [sds((128, 1024), bf16), sds((row...]
    reduce_scatter x1, waiting for transfers between devices: 1.01 us -> 7.29 us  [plane_shards(): lax.psum_scatter(gwg.reshape(1024, 1024), 'col', scatter_dimension=0, til...]
    convert_element_type x3 -> x0, local copies, waits for them, and re-layouts: 3.62 us -> none  [plane_shards(): grad_gate_up = gwg_in.reshape(2, QUAD, 32, 2, PLANES, 128).transpose(2, 3...]
  transfers between devices with their start and end apart: 4 -> 2, of which waited for: 1 -> 2; matrix products, arithmetic and copies ran while one was open for 3% -> 1% of each run, Pallas kernels for 66% -> 28%
where the time goes in v2:
time: 307 us; the launch traced here: 306 us
  Pallas kernels  278 us (91%)
  between operations  14.2 us (5%)
  waiting for transfers between devices  10.3 us (3%)
    pallas_call x1, Pallas kernels, plane_shards(): kernel(last_body, 'last', [VM] + [ANY] * 4 + [VM] * 7 + [SM], [sds((rows,...  64.2 us
    pallas_call x1, Pallas kernels, plane_shards(): kernel(enter_body, 'enter', [VM] * 9 + [SM, SM, VM], [sds((8, rows, width...  62.8 us
    pallas_call x1, Pallas kernels, plane_shards(): kernel(ffn_body, 'ffn', [VM, ANY, ANY, VM, VM, VM], [sds((8, rows, width)...  60.9 us
    pallas_call x1, Pallas kernels, plane_shards(): kernel(branch_body, 'branch', [VM] * 4, [sds((128, 1024), bf16), sds((row...  37.6 us
    pallas_call x1, Pallas kernels, plane_shards(): kernel(attended_back_body, 'attended_back', [VM] * 3, [sds((64, 2048), bf...  23.9 us
    pallas_call x1, Pallas kernels, plane_shards(): kernel(attend_back_body, 'attend_back', [SM] + [VM] * 8, [sds((192, 2048)...  14.5 us
    pallas_call x1, Pallas kernels, plane_shards(): kernel(attend_body, 'attend', [SM, SM, VM, VM], [sds((64, wide), f32), sd...  10.6 us
    reduce_scatter x1, waiting for transfers between devices, plane_shards(): lax.psum_scatter(gwg.reshape(1024, 1024), 'col', scatter_dimension=0, til...  7.29 us
  transfers between devices with their start and end apart: 2, of which 2 were waited for; matrix products, arithmetic and copies ran while one was open for 1% of the time, Pallas kernels for 28%

profile of v2, /device:TPU:0, one launch (start us, length us, event | category | flops | bytes accessed | tf_op | source)
XLA Modules:
  0.0 306.3 jit_solution(9949829244258679506)
XLA Ops:
  7.2 0.0 copy-start
  7.2 0.0 all-gather.2.cloned.1.call-start
  7.2 0.6 multiply_exponential_fusion.freq
  7.9 62.8 %enter.1 = (bf16[8,128,1024]{2,1,0:T(8,128)(2,1)}, bf16[32,32,384]{2,1,0:T(8,128)(2,1)}, bf16[4,32,1024]{2,1,0:T(8,128)(2,1)}, bf16[8,32,1024]{2,1,0:T(8,128)(2,...) custom-call(bf16[128,1024]{1,0:T(8,128)(2,1)} %x.3, ...), custom_call_target="tpu_custom_call" | custom-call | tf_op jit(solution)/shard_map/enter/pallas_call | solution.py:1289
  70.7 0.0 all-gather.2.cloned.1.call-update
  70.7 0.0 reduce-scatter.2.cloned.1.call-start
  70.8 0.0 copy-done
  70.8 0.7 dynamic-slice_reduce_fusion.bias
  71.5 0.7 convert_bitcast_fusion
  72.2 0.6 pad_add_fusion.info
  72.8 10.6 %attend.1 = (f32[64,2560]{1,0:T(8,128)}, f32[8,2560]{1,0:T(8,128)}, bf16[64,2560]{1,0:T(8,128)(2,1)}, bf16[128,2560]{1,0:T(8,128)(2,1)}, bf16[2048,128]{1,0:T(8,128)(2,1)}) custom-call(s32[8]{0:T(128)} %pad_add_fusion.info, f32[2]{0:T(128)} %dynamic-slice_reduce_fusion.bias, bf16[192,2048]{1,0:T(8,128)(2,1)} %get-tuple-element.51.qkvt, ...), custom_call_target="tpu_custom_call" | custom-call | flops 2000000000 | bytes 6666666 | tf_op jit(solution)/shard_map/attend/pallas_call | solution.py:1344
  83.4 37.6 %branch.1 = (bf16[128,1024]{1,0:T(8,128)(2,1)}, f32[128,1024]{1,0:T(8,128)}, bf16[128,1024]{1,0:T(8,128)(2,1)}) custom-call(bf16[64,2560]{1,0:T(8,128)(2,1)} %get-tuple-element.54.low, bf16[128,1024]{1,0:T(8,128)(2,1)} %bitcast.23, bf16[128,1024]{1,0:T(8,128)(2,1)} %x.3, f32[8,1024]{1,0:T(8,128)} %get-tuple-element.56.gains), custom_call_target="tpu_custom_call" | custom-call | tf_op jit(solution)/shard_map/branch/pallas_call | solution.py:1359
  121.0 3.0 all-gather.2.cloned.1.call-done
  124.0 60.9 %ffn.1 = (bf16[8,128,1024]{2,1,0:T(8,128)(2,1)}, bf16[4,128,1024]{2,1,0:T(8,128)(2,1)}, bf16[8,128,1024]{2,1,0:T(8,128)(2,1)}, f32[128,1024]{1,0:T(8,128)}, bf16...) custom-call(bf16[128,1024]{1,0:T(8,128)(2,1)} %get-tuple-element.57.s2, bf16[8,128,1024]{2,1,0:T(8,128)(2,1)} %get-tuple-element.58.cotp_in, ...), custom_call_target="tpu_custom_call" | custom-call | flops 10000000000 | bytes 33333332 | tf_op jit(solution)/shard_map/ffn/pallas_call | solution.py:1373
  184.9 0.0 reduce-scatter.2.cloned.1.call-update
  184.9 23.9 %attended_back.1 = (bf16[64,2048]{1,0:T(8,128)(2,1)}, bf16[128,1024]{1,0:T(8,128)(2,1)}) custom-call(bf16[128,1024]{1,0:T(8,128)(2,1)} %get-tuple-element.61.low, bf16[128,1024]{1,0:T(8,128)(2,1)} %bitcast.24, bf16[128,1024]{1,0:T(8,128)(2,1)} %get-tuple-element.62.atp), custom_call_target="tpu_custom_call" | custom-call | tf_op jit(solution)/shard_map/attended_back/pallas_call | solution.py:1411
  208.8 14.5 %attend_back.1 = (bf16[192,2048]{1,0:T(8,128)(2,1)}, f32[8,128]{1,0:T(8,128)}) custom-call(s32[8]{0:T(128)} %pad_add_fusion.info, bf16[192,2048]{1,0:T(8,128)(2,1)} %get-tuple-element.51.qkvt, bf16[128,2560]{1,0:T(8,128)(2,1)} %get-tuple-element.52.qa, bf16[2048,128]{1,0:T(8,128)(2,1)} %get-tuple-element.53.ka, f32[8,2048]{1,0:T(8,128)} %get-tuple-element.50.labels, ...), custom_call_target="tpu_custom_call" | custom-call | flops 5000000000 | bytes 16666666 | tf_op jit(solution)/shard_map/attend_back/pallas_call | solution.py:1424
  223.3 7.3 %reduce-scatter.2.cloned.1.call-done = bf16[256,1024]{1,0:T(8,128)(2,1)} async-done(((bf16[1024,1024]{1,0:T(8,128)(2,1)}), bf16[256,1024]{1,0:T(8,128)(2,1)}) %reduce-scatter.2.cloned.1.call-update) | async-done | bytes 524304 | tf_op jit(solution)/shard_map/reduce_scatter | solution.py:1407
  230.6 64.2 %last.1 = (bf16[128,1024]{1,0:T(8,128)(2,1)}, bf16[32,32,384]{2,1,0:T(8,128)(2,1)}, bf16[4,32,1024]{2,1,0:T(8,128)(2,1)}, bf16[8,32,1024]{2,1,0:T(8,128)(2,1)}, ...) custom-call(bf16[192,2048]{1,0:T(8,128)(2,1)} %get-tuple-element.66.dproj, bf16[1024,384]{1,0:T(8,128)(2,1)} %bitcast.25, ...), custom_call_target="tpu_custom_call" | custom-call | tf_op jit(solution)/shard_map/last/pallas_call | solution.py:1440
  294.8 3.5 %finish.1 = (bf16[128,1024]{1,0:T(8,128)(2,1)}, bf16[128,1024]{1,0:T(8,128)(2,1)}, f32[32,3072]{1,0:T(8,128)}, f32[32,1024]{1,0:T(8,128)}, f32[32,8192]{1,0:T(8,...) custom-call(s32[1]{0:T(128)} %bitcast.place_info, ...), custom_call_target="tpu_custom_call" | custom-call | tf_op jit(solution)/shard_map/finish/pallas_call | solution.py:1478
  298.3 1.3 slice_bitcast_fusion
Async XLA Ops:
  7.2 63.6 %copy-start = (f32[2,16]{1,0:T(2,128)S(1)}, f32[2,16]{1,0:T(2,128)}, u32[]{:S(2)}) copy-start(f32[2,16]{1,0:T(2,128)} %param.24) | copy-start | bytes 388
  7.2 116.8 %all-gather.2.cloned.1.call-start = ((), (), s32[]{:S(2)}) async-start(), calls=%async_computation.1 | async-start | bytes 2621440 | tf_op jit(solution)/shard_map/all_gather | solution.py:1332
  70.7 159.9 %reduce-scatter.2.cloned.1.call-start = ((), (), s32[]{:S(2)}) async-start(), calls=%async_computation.2 | async-start | bytes 2621440 | tf_op jit(solution)/shard_map/reduce_scatter | solution.py:1407
Sparse Core Ops, SparseCore 0:
  70.8 53.1 all-gather.1
  185.0 45.5 reduce-scatter.1

commit v3 on v2

--- a/solution.py
+++ b/solution.py
@@ -2,6 +2,7 @@
 
 import jax
 import jax.numpy as jnp
+import numpy as np
 from jax import lax
 from jax.experimental import pallas as pl
 from jax.experimental.pallas import tpu as pltpu
@@ -360,6 +361,10 @@
     return flip(row, bits // QUAD), flip(col, bits % QUAD)
 
 
+def in_line(row, col, bits):
+    return row, flip(col, bits // 2 * QUAD + bits % 2)
+
+
 def on_line(row, col, bits):
     return row, flip(col, bits * QUAD)
 
@@ -402,10 +407,18 @@
     return [on_line(row, col, bits) for bits in (1, 2, 3)]
 
 
+def column_all(row, col):
+    return [
+        (flip(row, bits // 4), flip(col, bits % 4 * QUAD)) for bits in (1, 2, 3, 5, 6, 7)
+    ]
+
+
 class Gather:
-    def __init__(self, target, send, recv):
-        self.target, self.send, self.recv = target, send, recv
+    def __init__(self, target, send, recv, peer=in_plane, place=None):
+        self.target, self.send, self.recv, self.peer = target, send, recv, peer
         self.row, self.col, _, self.place = places()
+        if place is not None:
+            self.place = place
         self.copies, self.onward = {}, {}
 
     def start(self, source):
@@ -415,7 +428,7 @@
                 self.target.at[self.place],
                 self.send.at[bits],
                 self.recv.at[bits],
-                in_plane(self.row, self.col, bits),
+                self.peer(self.row, self.col, bits),
             )
             self.copies[bits].start()
 
@@ -427,7 +440,7 @@
             slot,
             self.send.at[bits + 1],
             self.recv.at[bits + 1],
-            in_plane(self.row, self.col, 1),
+            self.peer(self.row, self.col, 1),
         )
         self.onward[bits].start()
 
@@ -445,11 +458,59 @@
             self.arrived(bits)
 
 
+class LineGather(Gather):
+    def __init__(self, target, send, recv):
+        row, col, z, _ = places()
+        super().__init__(target, send, recv, in_line, z * 2 + col % 2)
+        self.inner = jnp.logical_or(z == 1, z == 2)
+
+    def start(self, source):
+        for bits in (4, 2, 6, 1):
+            self.copies[bits] = push(
+                source,
+                self.target.at[self.place],
+                self.send.at[bits],
+                self.recv.at[bits],
+                in_line(self.row, self.col, bits),
+            )
+            if bits != 6:
+                self.copies[bits].start()
+        slot = self.target.at[flip(self.place, 4)]
+        self.passing = push(
+            slot, slot, self.send.at[0], self.recv.at[6], in_line(self.row, self.col, 2)
+        )
+
+        @pl.when(self.inner)
+        def _():
+            self.copies[6].start()
+
+    def forward(self, bits):
+        super().forward(bits)
+        if bits == 4:
+
+            @pl.when(self.inner)
+            def _():
+                self.passing.start()
+
+    def close(self):
+        for bits in (4, 2, 1):
+            self.copies[bits].wait_send()
+        for copy in self.onward.values():
+            copy.wait_send()
+
+        @pl.when(self.inner)
+        def _():
+            self.copies[6].wait_send()
+            self.passing.wait_send()
+
+
 class Scatter:
-    def __init__(self, part, inbox, outbox, second, send, recv):
+    def __init__(self, part, inbox, outbox, second, send, recv, peer=in_plane, place=None):
         self.part, self.inbox, self.outbox, self.second = part, inbox, outbox, second
-        self.send, self.recv = send, recv
+        self.send, self.recv, self.peer = send, recv, peer
         self.row, self.col, _, self.place = places()
+        if place is not None:
+            self.place = place
         self.core = self.col % 2
         self.copies, self.sent = [], []
 
@@ -459,7 +520,7 @@
             self.inbox.at[number],
             self.send.at[number],
             self.recv.at[number],
-            in_plane(self.row, self.col, 1),
+            self.peer(self.row, self.col, 1),
         )
         copy.start()
         self.copies.append(copy)
@@ -474,7 +535,7 @@
             self.second.at[bits - 1],
             self.send.at[3 + bits],
             self.recv.at[3 + bits],
-            in_plane(self.row, self.col, 2 * bits),
+            self.peer(self.row, self.col, 2 * bits),
         )
         copy.start()
         self.sent.append(copy)
@@ -501,6 +562,84 @@
             copy.wait_send()
 
 
+class LineScatter(Scatter):
+    def __init__(self, part, inbox, outbox, second, send, recv, passed, sems):
+        row, col, z, _ = places()
+        super().__init__(part, inbox, outbox, second, send, recv, in_line, z * 2 + col % 2)
+        self.passed, self.sems = passed, sems
+        self.inner = jnp.logical_or(z == 1, z == 2)
+        self.end = jnp.logical_not(self.inner)
+
+    def sum_for(self, bits):
+        self.copies[bits].wait_recv()
+        chip = flip(self.place // 2, bits)
+        return self.part[2 * chip + self.core].astype(f32) + self.inbox[bits].astype(f32)
+
+    def to(self, bits):
+        return push(
+            self.outbox.at[bits - 1],
+            self.second.at[bits - 1],
+            self.send.at[3 + bits],
+            self.recv.at[3 + bits],
+            in_line(self.row, self.col, 2 * bits),
+        )
+
+    def far_all(self):
+        self.outbox[2] = self.sum_for(3).astype(bf16)
+        self.across = self.to(3)
+        self.passing = push(
+            self.outbox.at[2],
+            self.passed,
+            self.sems.at[0],
+            self.sems.at[1],
+            in_line(self.row, self.col, 2),
+        )
+
+        @pl.when(self.end)
+        def _():
+            self.passing.start()
+            self.second[2] = jnp.zeros(self.second.shape[1:], bf16)
+
+        @pl.when(self.inner)
+        def _():
+            self.across.start()
+
+        total = self.sum_for(2)
+        self.sent = [self.to(2), self.to(1)]
+
+        @pl.when(self.end)
+        def _():
+            self.outbox[1] = total.astype(bf16)
+            self.sent[0].start()
+
+        self.outbox[0] = self.sum_for(1).astype(bf16)
+        self.sent[1].start()
+
+        @pl.when(self.inner)
+        def _():
+            self.passing.wait_recv()
+            self.outbox[1] = (total + self.passed[...].astype(f32)).astype(bf16)
+            self.sent[0].start()
+
+    def finish(self):
+        @pl.when(self.inner)
+        def _():
+            self.across.wait_recv()
+
+        return super().finish()
+
+    def close(self):
+        super().close()
+
+        @pl.when(self.inner)
+        def _():
+            self.across.wait_send()
+
+        @pl.when(self.end)
+        def _():
+            self.passing.wait_send()
+
+
 def scatter_scratch(rows, width):
     return [
         pltpu.VMEM((4, rows, width), bf16),
@@ -523,13 +662,14 @@
 
 def enter_body(
     x, wq, wo, wg, cot, ga, gf, variate, time, lengths, deal, freq,
-    xp_out, wqp_out, wop, wgp, cotp_out, s1_out, qkvt, gains, labels,
-    xp, wqp, cotp, s1, keep, wqs, wgs, cotr, cots, tile, tl, tiles, wt, box, cs, sn, times,
-    sx, rx, sq, rq, st, rt, su, ru, sw, rw, sg, rg, sc, rc, sa, ra, sz, rz,
+    xp_out, wt_out, wop, wgp, cotp_out, s1_out, qkvt, gains, labels,
+    xp, cotp, s1, keep, wqs, wline, wqp, wgs, cotr, cots, tile, tl, tiles, wt, box, cs, sn, times,
+    sx, rx, sq, rq, sv, rv, st, rt, su, ru, sw, rw, sg, rg, sc, rc, sa, ra, sz, rz,
 ):
     row, col, z, place = places()
-    me = row * 16 + col
     quarter = col % QUAD
+    y, core = col // 2 % 2, col % 2
+    member = z * 2 + core
     lane = lax.broadcasted_iota(jnp.int32, (1, 128), 1)
     for line, gain in ((0, ga), (1, gf)):
         wide = gain[...].astype(f32)
@@ -542,40 +682,30 @@
         numbers = jnp.where(lane == i, lengths[0, i], numbers)
     tile[4:5, :] = numbers.astype(f32)
     tile[5:8, :] = jnp.zeros((3, 128), f32)
-    meet([anyone(row, col, bits) for bits in range(1, 32)])
-    rows_in = Gather(xp, sx, rx)
-    rows_in.start(x)
-    first = []
-    for bits in (1, 2, 3):
-        first.append(push(tile, tl.at[z], st.at[bits], rt.at[bits], on_line(row, col, bits)))
-        first[-1].start()
     for p in range(MEMBERS):
         for part in range(3):
             at = part * 1024 + p * 128
             wqs[p, :, part * 128 : part * 128 + 128] = wq[:, at : at + 128]
-    weights = []
-    for bits in range(1, 32):
-        there = anyone(row, col, bits)
-        member = there[0] * QUAD + there[1] % QUAD
-        weights.append(push(wqs.at[member], wqp.at[me], sq.at[bits], rq.at[bits], there))
-        weights[-1].start()
+    meet([anyone(row, col, bits) for bits in range(1, 32)])
+    first = []
+    for bits in range(1, 8):
+        there = in_line(row, col, bits)
+        first.append(push(wqs.at[flip(member, bits)], wline.at[member], sq.at[bits], rq.at[bits], there))
+        first[-1].start()
+    for bits in (1, 2, 3):
+        first.append(push(tile, tl.at[z], st.at[bits], rt.at[bits], on_line(row, col, bits)))
+        first[-1].start()
     pieces = []
     for bits in range(1, 16):
         there = (row, flip(col, bits))
         pieces.append(push(cot.at[there[1]], cotr.at[col], sc.at[bits], rc.at[bits], there))
         pieces[-1].start()
-    xp[place] = x[...]
-    wqp[me] = wqs[place]
+    rows_in = LineGather(xp, sx, rx)
+    rows_in.start(x)
+    xp[member] = x[...]
+    wline[member] = wqs[member]
     tl[z] = tile[...]
     cotr[col] = cot[col]
-    for copy in first:
-        copy.wait_recv()
-    second = []
-    for bits in range(1, 8):
-        there = in_plane(row, col, bits)
-        second.append(push(tl, tiles.at[place], su.at[bits], ru.at[bits], there))
-        second[-1].start()
-    tiles[place] = tl[...]
     for p in range(MEMBERS):
         for half in range(2):
             for plane in range(PLANES):
@@ -583,6 +713,35 @@
                 at = half * 512 + plane * 128
                 start = half * 4096 + unit * 128
                 wgs[p, :, at : at + 128] = wg[:, start : start + 128]
+    for copy in first:
+        copy.wait_recv()
+    column = row * 2 + y
+    second = []
+    for bits in (1, 2, 3):
+        there = (flip(row, bits // 2), flip(col, bits % 2 * 2))
+        second.append(push(wline, wqp.at[column], sv.at[bits], rv.at[bits], there))
+        second[-1].start()
+    wqp[column] = wline[...]
+    for bits in range(1, 8):
+        there = in_plane(row, col, bits)
+        second.append(push(tl, tiles.at[place], su.at[bits], ru.at[bits], there))
+        second[-1].start()
+    tiles[place] = tl[...]
+    blocks = []
+    for bits in range(1, 8):
+        there = in_plane(row, col, bits)
+        blocks.append(
+            push(wgs.at[flip(place, bits)], wgp.at[place], sg.at[bits], rg.at[bits], there)
+        )
+        blocks[-1].start()
+    wgp[place] = wgs[place]
+    for copy in pieces:
+        copy.wait_recv()
+    for j in range(16):
+        cots[j * 8 : j * 8 + 8, :] = cotr[jnp.clip(deal[j], 0, 15)]
+    cot_in = Gather(cotp, sa, ra)
+    cot_in.start(cots)
+    cotp[place] = cots[...]
     for copy in second:
         copy.wait_recv()
     for k in range(8):
@@ -591,128 +750,112 @@
         gains[:, lanes] = (tiles[r * QUAD, plane] + tiles[r * QUAD + 1, plane]) + (
             tiles[r * QUAD + 2, plane] + tiles[r * QUAD + 3, plane]
         )
-        times[:, lanes] = tiles[k, z]
+        times[:, lanes] = tiles[row * QUAD + y * 2 + k % 2, k // 2]
+        wt[:, lanes] = jnp.transpose(
+            jnp.concatenate(
+                [wqp[r * 2 + j // 2, plane * 2 + j % 2] for j in range(4)], axis=0
+            )
+        )
     for k in range(16):
-        labels[:, k * 128 : k * 128 + 128] = tiles[(z // 2) * QUAD + k % QUAD, k // QUAD]
+        labels[:, k * 128 : k * 128 + 128] = tiles[row * QUAD + k % QUAD, k // QUAD]
     phases = times[3:4, :] * freq[...]
     cs[...] = jnp.cos(phases)
     sn[...] = jnp.sin(phases)
     gain = gains[0:1, :]
-    rows_in.finish()
-
-    def scale(t, unused):
-        values = xp[t].astype(f32)
-        s1[t] = (values * norm_scale(values) * gain).astype(bf16)
-        return unused
-
-    lax.fori_loop(0, MEMBERS, scale, 0)
-    kept = [fetch(xp, xp_out, keep.at[0]), fetch(s1, s1_out, keep.at[1])]
-    for copy in pieces:
-        copy.wait_recv()
-    for j in range(16):
-        cots[j * 8 : j * 8 + 8, :] = cotr[jnp.clip(deal[j], 0, 15)]
-    cot_in = Gather(cotp, sa, ra)
-    cot_in.start(cots)
-    cotp[place] = cots[...]
-    for copy in weights:
-        copy.wait_recv()
-    kept.append(fetch(wqp, wqp_out, keep.at[2]))
-    for plane in range(PLANES):
-        there = (row, plane * QUAD + z)
-        mine = jnp.logical_and(z == plane, quarter == z)
-
-        @pl.when(jnp.logical_not(mine))
-        def _():
-            push(wo, wop.at[quarter], sw.at[plane], rw.at[quarter], there).start()
-
-        @pl.when(mine)
-        def _():
-            wop[quarter] = wo[...]
-
-    blocks = []
-    for bits in range(1, 8):
-        there = in_plane(row, col, bits)
-        blocks.append(
-            push(wgs.at[flip(place, bits)], wgp.at[place], sg.at[bits], rg.at[bits], there)
-        )
-        blocks[-1].start()
-    wgp[place] = wgs[place]
-    for k in range(8):
-        wt[:, k * 128 : k * 128 + 128] = jnp.transpose(
-            jnp.concatenate([wqp[4 * k + j] for j in range(4)], axis=0)
-        )
-    for group in range(2):
-
-        def project(t, unused):
-            number = group * 4 + 2 * t
-            rows = block(2 * group + t, 256)
-            scaled = jnp.concatenate([s1[number], s1[number + 1]], axis=0)
-            out = mm_nt(wt[...], scaled)
-            cos_part, sin_part = cs[:, rows], sn[:, rows]
-            lanes = block(t, 256)
-            for head in range(2):
-                pair = group * 2 + head
-                for part in range(2):
-                    base = part * 128 + head * 64
-                    former, latter = out[base : base + 32], out[base + 32 : base + 64]
-                    factor = 0.125 if part == 0 else 1.0
-                    turned = former * cos_part - latter * sin_part
-                    other = latter * cos_part + former * sin_part
-                    at = part * 64
-                    box[pair, at : at + 32, lanes] = (turned * factor).astype(bf16)
-                    box[pair, at + 32 : at + 64, lanes] = (other * factor).astype(bf16)
-                at = 256 + head * 64
-                box[pair, 128:192, lanes] = out[at : at + 64].astype(bf16)
-            return unused
-
-        lax.fori_loop(0, 2, project, 0)
+    kept = [fetch(wt, wt_out, keep.at[2])]
+
+    def project(chip):
+        rows = block(chip, 256)
+        values = jnp.concatenate([xp[2 * chip], xp[2 * chip + 1]], axis=0).astype(f32)
+        scaled = (values * norm_scale(values) * gain).astype(bf16)
+        s1[2 * chip] = scaled[0:128]
+        s1[2 * chip + 1] = scaled[128:256]
+        out = mm_nt(wt[...], scaled)
+        cos_part, sin_part = cs[:, rows], sn[:, rows]
         for head in range(2):
-            pair = group * 2 + head
-
-            @pl.when(z != pair)
-            def _():
-                push(
-                    box.at[pair], qkvt.at[:, block(z, 512)], sz.at[pair], rz.at[z],
-                    (row, pair * QUAD + quarter),
-                ).start()
-
-            @pl.when(z == pair)
-            def _():
-                qkvt[:, block(z, 512)] = box[pair]
-
-    cot_in.finish()
+            for part in range(2):
+                base = part * 128 + head * 64
+                former, latter = out[base : base + 32], out[base + 32 : base + 64]
+                factor = 0.125 if part == 0 else 1.0
+                turned = former * cos_part - latter * sin_part
+                other = latter * cos_part + former * sin_part
+                at = part * 64
+                box[head, at : at + 32, rows] = (turned * factor).astype(bf16)
+                box[head, at + 32 : at + 64, rows] = (other * factor).astype(bf16)
+            at = 256 + head * 64
+            box[head, 128:192, rows] = out[at : at + 64].astype(bf16)
+
+    turned = []
+
+    def exchange(chip, number):
+        lanes = pl.ds(pl.multiple_of(chip * 512 + y * 256, 256), 256)
+        copy = push(
+            box.at[1 - y, :, block(chip, 256)],
+            qkvt.at[:, lanes],
+            sz.at[number],
+            rz.at[number],
+            (row, flip(col, 2)),
+        )
+        copy.start()
+        turned.append(copy)
+        qkvt[:, lanes] = box[y, :, block(chip, 256)]
+
+    for k, bits in enumerate((0, 4, 2, 6)):
+        if bits:
+            rows_in.forward(bits)
+        if bits == 4:
+            cot_in.forward(2)
+            cot_in.forward(4)
+            cot_in.forward(6)
+        rows_in.arrived(bits)
+        chip = flip(z, bits // 2)
+        project(chip)
+        exchange(chip, k)
+        if bits == 2:
+            target = col // 2 % 2 * 2 + col // 4 % 2
+            slot = col // 8 * 2 + col % 2
+            for plane in range(PLANES):
+                there = (row, plane * QUAD + target)
+                mine = jnp.logical_and(z == plane, quarter == target)
+
+                @pl.when(jnp.logical_not(mine))
+                def _():
+                    push(wo, wop.at[slot], sw.at[plane], rw.at[slot], there).start()
+
+                @pl.when(mine)
+                def _():
+                    wop[slot] = wo[...]
+
+    kept.append(fetch(xp, xp_out, keep.at[0]))
+    kept.append(fetch(s1, s1_out, keep.at[1]))
+    for bits in (0, 2, 4, 6):
+        cot_in.arrived(bits)
     kept.append(fetch(cotp, cotp_out, keep.at[3]))
     for copy in blocks:
         copy.wait_recv()
     for j in range(4):
-        mine = jnp.logical_and(quarter == z, quarter == j)
+        source = j // 2 * 8 + core * 4 + y * 2 + j % 2
+        mine = col == source
 
         @pl.when(jnp.logical_not(mine))
         def _():
-            push(wo, wop.at[j], sw.at[j], rw.at[j], (row, quarter * QUAD + j)).wait_recv()
-
+            push(wo, wop.at[j], sw.at[j], rw.at[j], (row, source)).wait_recv()
+
+    target = col // 2 % 2 * 2 + col // 4 % 2
+    slot = col // 8 * 2 + col % 2
     for plane in range(PLANES):
-        there = (row, plane * QUAD + z)
-        mine = jnp.logical_and(z == plane, quarter == z)
+        there = (row, plane * QUAD + target)
+        mine = jnp.logical_and(z == plane, quarter == target)
 
         @pl.when(jnp.logical_not(mine))
         def _():
-            push(wo, wop.at[quarter], sw.at[plane], rw.at[quarter], there).wait_send()
-
-    for pair in range(4):
-
-        @pl.when(z != pair)
-        def _():
-            copy = push(
-                box.at[pair], qkvt.at[:, block(pair, 512)], sz.at[pair], rz.at[pair],
-                (row, pair * QUAD + quarter),
-            )
-            copy.wait_send()
-            copy.wait_recv()
-
+            push(wo, wop.at[slot], sw.at[plane], rw.at[slot], there).wait_send()
+
+    for copy in turned:
+        copy.wait()
     rows_in.close()
     cot_in.close()
-    for copy in first + second + weights + pieces + blocks:
+    for copy in first + second + pieces + blocks:
         copy.wait_send()
     for copy in kept:
         copy.wait()
@@ -735,8 +878,31 @@
     )
 
 
-def attend_body(info, bias, qkvt, labels, att, den, low, qa, ka, kt):
+def head_of():
+    row, col, z, place = places()
+    return (z * 2 + col % 2) * 2 + col // 2 % 2
+
+
+def read_lengths(labels, info):
+    lane = lax.broadcasted_iota(jnp.int32, (1, 128), 1)
+    numbers = labels[4:5, 0:128]
+    for i in range(NSEQ):
+        info[i] = jnp.sum(jnp.where(lane == i, numbers, 0.0)).astype(jnp.int32)
+
+
+def over_keys(start, length, step, carry):
+    carry = lax.fori_loop(
+        0, length // 2, lambda k, c: step((start + 2 * k) * 128, 256, c), carry
+    )
+    return lax.fori_loop(
+        0, length % 2, lambda k, c: step((start + length - 1) * 128, 128, c), carry
+    )
+
+
+def attend_body(bias_all, qkvt, labels, att, den, low, qa, ka, kt, info):
     size = qkvt.shape[1]
+    head = head_of()
+    bias = (bias_all[0, head], bias_all[1, head])
     variate = labels[2:3, :]
     line = lax.broadcasted_iota(jnp.int32, (16, size), 0)
     same = (variate == (line % 4).astype(f32)).astype(f32)
@@ -760,6 +926,7 @@
     kt[64:80, :] = extra_k.astype(bf16)
     kt[80:AUG, :] = jnp.zeros((AUG - 80, size), bf16)
     ka[...] = jnp.transpose(kt[...])
+    read_lengths(labels, info)
 
     def sequence(number, start):
         length = info[number]
@@ -770,16 +937,16 @@
             lanes = pl.ds(pl.multiple_of(first, 128), WINDOW)
             queries = window_queries(qa, lanes, first, limit)
 
-            def key(k, running):
+            def keys(first_key, count, running):
                 total, numerator = running
-                rows = pl.ds(pl.multiple_of((start + k) * 128, 128), 128)
+                rows = pl.ds(pl.multiple_of(first_key, 128), count)
                 weights = jnp.exp(mm(ka[rows, :], queries))
                 total = total + jnp.sum(weights, axis=0, keepdims=True)
                 numerator = numerator + mm(qkvt[128:192, rows], weights.astype(bf16))
                 return total, numerator
 
-            total, numerator = lax.fori_loop(
-                0, length, key, (jnp.zeros((1, WINDOW), f32), jnp.zeros((64, WINDOW), f32))
+            total, numerator = over_keys(
+                start, length, keys, (jnp.zeros((1, WINDOW), f32), jnp.zeros((64, WINDOW), f32))
             )
             attended = numerator / total
             att[:, lanes] = attended
@@ -794,9 +961,9 @@
 
 
 def attend_back_body(
-    info, qkvt, qa, ka, labels, freq, grad, att, den,
+    qkvt, qa, ka, labels, freq, grad, att, den,
     dproj, bias_tile,
-    dn, cw, vn, dq, dk, dv,
+    dn, cw, vn, dq, dk, dv, info,
 ):
     size = qkvt.shape[1]
     lanes_all = slice(0, size)
@@ -812,6 +979,8 @@
     dk[...] = jnp.zeros_like(dk)
     dv[...] = jnp.zeros_like(dv)
 
+    read_lengths(labels, info)
+
     def sequence(number, start):
         length = info[number]
         limit = (start + length) * 128
@@ -823,8 +992,8 @@
             upstream = dn[:, lanes]
             centre = cw[0:1, lanes]
 
-            def key(k, running):
-                rows = pl.ds(pl.multiple_of((start + k) * 128, 128), 128)
+            def keys(first_key, count, running):
+                rows = pl.ds(pl.multiple_of(first_key, 128), count)
                 weights = jnp.exp(mm(ka[rows, :], queries))
                 d_scores = weights * (mm(vn[rows, :], upstream) - centre)
                 rounded = d_scores.astype(bf16)
@@ -832,13 +1001,14 @@
                 dv[:, rows] += mm_nt(upstream, weights.astype(bf16))
                 return running + mm(qkvt[64:128, rows], rounded)
 
-            dq[:, lanes] = lax.fori_loop(0, length, key, jnp.zeros((64, WINDOW), f32))
+            dq[:, lanes] = over_keys(start, length, keys, jnp.zeros((64, WINDOW), f32))
             return unused
 
         lax.fori_loop(0, (length + 3) // 4, window, 0)
         return start + length
 
     lax.fori_loop(0, NSEQ, sequence, 0)
+
     phases = labels[3:4, :] * freq[...]
     cos_part, sin_part = jnp.cos(phases), jnp.sin(phases)
     for part, source, factor in ((0, dq, 0.125), (1, dk, 1.0)):
@@ -857,7 +1027,7 @@
     every = jnp.sum(dk[77:78, :])
     lane = lax.broadcasted_iota(jnp.int32, (8, 128), 1)
     line8 = lax.broadcasted_iota(jnp.int32, (8, 128), 0)
-    here = lane == info[NSEQ]
+    here = lane == head_of()
     bias_tile[...] = jnp.where(
         jnp.logical_and(here, line8 == 2),
         near,
@@ -871,22 +1041,43 @@
     atn, part, sz, rz, inbox, outbox, second, ss, rs,
 ):
     row, col, z, place = places()
-    meet(plane_near(row, col) + line_all(row, col))
-    rows, lanes = block(z % 2, 64), block(z // 2, 512)
-    copies = []
-    for bits in (3, 2, 1):
-        copy = push(
-            low.at[:, block(flip(z, bits), 512)],
-            atp.at[rows, lanes],
-            sz.at[bits],
-            rz.at[bits],
-            on_line(row, col, bits),
-        )
-        copy.start()
-        copies.append(copy)
-    atp[rows, lanes] = low[:, block(z, 512)]
-    for copy in copies:
-        copy.wait()
+    quarter = col % QUAD
+    meet(plane_near(row, col) + column_all(row, col))
+    rows, lanes = block(z % 2, 64), block(row, 512)
+    for plane in range(PLANES):
+        mine = jnp.logical_and(row == z // 2, z == plane)
+
+        @pl.when(jnp.logical_not(mine))
+        def _():
+            push(
+                low.at[:, plane * 512 : plane * 512 + 512], atp.at[rows, lanes],
+                sz.at[plane], rz.at[row * 2 + z % 2], (z // 2, plane * QUAD + quarter),
+            ).start()
+
+        @pl.when(mine)
+        def _():
+            atp[rows, lanes] = low[:, plane * 512 : plane * 512 + 512]
+
+    for j in range(4):
+        source = (j // 2, (2 * row + j % 2) * QUAD + quarter)
+        mine = jnp.logical_and(row == j // 2, z == 2 * row + j % 2)
+
+        @pl.when(jnp.logical_not(mine))
+        def _():
+            push(
+                low.at[:, 0:512], atp.at[0:64, 0:512], sz.at[j], rz.at[j], source
+            ).wait_recv()
+
+    for plane in range(PLANES):
+        mine = jnp.logical_and(row == z // 2, z == plane)
+
+        @pl.when(jnp.logical_not(mine))
+        def _():
+            push(
+                low.at[:, plane * 512 : plane * 512 + 512], atp.at[rows, lanes],
+                sz.at[plane], rz.at[row * 2 + z % 2], (z // 2, plane * QUAD + quarter),
+            ).wait_send()
+
     atn[...] = jnp.transpose(atp[...])
     total = Scatter(part, inbox, outbox, second, ss, rs)
     core = col % 2
@@ -908,7 +1099,7 @@
 def ffn_body(
     s2, cotp_in, wg_in, w_down, hidden, gains,
     out_keep, down_in, gwg_out, d_hidden, low, gain_term,
-    cotp, wg, s2p, wgs, wd, actives, factors, inner_s, dgu, d_part, out_part, gwd, gwg,
+    cotp, wg, s2p, wgs, wd, actives, factors, inner_s, dgu, d_part, out_part, gwd, gwg, relayed, both_terms,
     keep, sa, ra, sw, rw, sd, rd, inbox, outbox, second, ss, rs,
 ):
     row, col, z, place = places()
@@ -917,12 +1108,23 @@
     rows_in = Gather(s2p, sa, ra)
     rows_in.start(s2)
     s2p[place] = s2[...]
-    downs = []
-    for bits in (3, 2, 1):
-        downs.append(
-            push(w_down, wd.at[block(z, 128), :], sw.at[bits], rw.at[bits], on_line(row, col, bits))
-        )
-        downs[-1].start()
+    inner = jnp.logical_or(z == 1, z == 2)
+    end = jnp.logical_not(inner)
+    downs = {
+        bits: push(
+            w_down, wd.at[block(z, 128), :], sw.at[bits], rw.at[bits], on_line(row, col, bits)
+        )
+        for bits in (2, 1, 3)
+    }
+    passed = wd.at[block(flip(z, 2), 128), :]
+    downs[0] = push(passed, passed, sw.at[0], rw.at[3], on_line(row, col, 1))
+    downs[2].start()
+
+    @pl.when(inner)
+    def _():
+        downs[3].start()
+
+    downs[1].start()
     wd[block(z, 128), :] = w_down[...]
     loads[0].wait()
     for plane in range(PLANES):
@@ -934,6 +1136,13 @@
         if k:
             rows_in.forward(2 * k)
         rows_in.arrived(2 * k)
+        if k == 1:
+            downs[2].wait_recv()
+
+            @pl.when(inner)
+            def _():
+                downs[0].start()
+
         rows = block(chip, 256)
         scaled = jnp.concatenate([s2p[2 * chip], s2p[2 * chip + 1]], axis=0)
         both = mm(scaled, wgs[...])
@@ -948,16 +1157,31 @@
     for k in range(4):
         cols = slice(k * 128, k * 128 + 128)
         gwd[k] = mm_tn(inner_s[:, cols], cot_all).astype(bf16)
-    grads = []
-    for bits in (3, 2, 1):
-        grads.append(
-            push(gwd.at[flip(z, bits)], down_in.at[z], sd.at[bits], rd.at[bits], on_line(row, col, bits))
-        )
-        grads[-1].start()
-    down_in[z] = gwd[z]
+    grads = {
+        bits: push(
+            gwd.at[flip(z, bits)], down_in.at[bits], sd.at[bits], rd.at[bits], on_line(row, col, bits)
+        )
+        for bits in (1, 3)
+    }
+    grads[2] = push(both_terms, down_in.at[2], sd.at[2], rd.at[2], on_line(row, col, 2))
+    grads[0] = push(gwd.at[flip(z, 3)], relayed, sd.at[0], rd.at[0], on_line(row, col, 1))
+
+    @pl.when(end)
+    def _():
+        grads[0].start()
+        both_terms[...] = gwd[flip(z, 2)]
+        grads[2].start()
+        down_in[3] = jnp.zeros(down_in.shape[1:], bf16)
+
+    @pl.when(inner)
+    def _():
+        grads[3].start()
+
+    grads[1].start()
+    down_in[0] = gwd[z]
     total = Scatter(d_part, inbox, outbox, second, ss, rs)
-    for copy in downs:
-        copy.wait_recv()
+    downs[1].wait_recv()
+    downs[3].wait_recv()
     for k in range(4):
         chip = flip(place // 2, k)
         rows = block(chip, 256)
@@ -971,6 +1195,16 @@
         total.near(chip, k)
         if k > 1:
             total.far(k - 1)
+        if k == 1:
+
+            @pl.when(inner)
+            def _():
+                grads[0].wait_recv()
+                both_terms[...] = (
+                    gwd[flip(z, 2)].astype(f32) + relayed[...].astype(f32)
+                ).astype(bf16)
+                grads[2].start()
+
     for k in range(4):
         chip = flip(place // 2, k)
         tile = mm(inner_s[block(chip, 256), :], wd[...]).astype(bf16)
@@ -995,10 +1229,21 @@
     low[...] = d_state.astype(bf16)
     rows_in.close()
     total.close()
-    for copy in grads:
-        copy.wait_recv()
-    for copy in downs + grads:
+    grads[1].wait_recv()
+    grads[2].wait_recv()
+    for copy in (downs[1], downs[2], grads[1], grads[2]):
         copy.wait_send()
+
+    @pl.when(inner)
+    def _():
+        grads[3].wait_recv()
+        for copy in (downs[3], downs[0], grads[3]):
+            copy.wait_send()
+
+    @pl.when(end)
+    def _():
+        grads[0].wait_send()
+
     for copy in kept:
         copy.wait()
 
@@ -1009,7 +1254,7 @@
     dbp, dat, sg, rg, sz, rz,
 ):
     row, col, z, place = places()
-    meet(plane_near(row, col) + line_all(row, col))
+    meet(plane_near(row, col) + column_all(row, col))
     quarter = col % QUAD
     rows_in = Gather(dbp, sg, rg)
     rows_in.start(low)
@@ -1025,72 +1270,102 @@
             continue
         group = row if k == 1 else 1 - row
         for head in range(2):
-            pair = group * 2 + head
+            plane = 2 * row + head
             source = dat.at[head * 64 : head * 64 + 64, block(group, 512)]
-
-            @pl.when(z != pair)
-            def _():
+            if k == 1:
+
+                @pl.when(z != plane)
+                def _():
+                    push(
+                        source, grad.at[:, block(z, 512)], sz.at[head], rz.at[z],
+                        (group, plane * QUAD + quarter),
+                    ).start()
+
+                @pl.when(z == plane)
+                def _():
+                    grad[:, block(z, 512)] = source[...]
+
+            else:
                 push(
-                    source, grad.at[:, block(z, 512)], sz.at[pair], rz.at[z],
-                    (row, pair * QUAD + quarter),
+                    source, grad.at[:, block(z, 512)], sz.at[2 + head], rz.at[z],
+                    (group, plane * QUAD + quarter),
                 ).start()
-
-            @pl.when(z == pair)
-            def _():
-                grad[:, block(z, 512)] = source[...]
 
     total = mm(atp[:, 0:128], dbp[0])
     for q in range(1, MEMBERS):
         total = total + mm(atp[:, q * 128 : q * 128 + 128], dbp[q])
     gwo[...] = total.astype(bf16)
-    for pair in range(4):
-
-        @pl.when(z != pair)
-        def _():
-            copy = push(
-                dat.at[0:64, 0:512], grad.at[:, block(pair, 512)], sz.at[pair], rz.at[pair],
-                (row, pair * QUAD + quarter),
-            )
-            copy.wait_send()
-            copy.wait_recv()
+    for plane in range(PLANES):
+        mine = jnp.logical_and(row == z // 2, z == plane)
+
+        @pl.when(jnp.logical_not(mine))
+        def _():
+            push(
+                dat.at[0:64, 0:512], grad.at[:, plane * 512 : plane * 512 + 512], sz.at[0],
+                rz.at[plane], (z // 2, plane * QUAD + quarter),
+            ).wait_recv()
+
+    for head in range(2):
+        plane = 2 * row + head
+
+        @pl.when(z != plane)
+        def _():
+            push(
+                dat.at[0:64, 0:512], grad.at[:, 0:512], sz.at[head], rz.at[z],
+                (row, plane * QUAD + quarter),
+            ).wait_send()
+
+        push(
+            dat.at[0:64, 0:512], grad.at[:, 0:512], sz.at[2 + head], rz.at[z],
+            (1 - row, plane * QUAD + quarter),
+        ).wait_send()
 
     rows_in.close()
 
 
 def last_body(
-    dproj, wqp_in, s1_in, xp_in, out_in, gains, d_hidden, hidden, gwo, gwg, gain_two, bias_tile, deal,
+    dproj, wt_in, s1_in, xp_in, out_in, gains, d_hidden, hidden, gwo, gwg, gain_two, bias_tile, deal,
     grad_tokens, gqin, goin, gwg_in, sums, out,
-    wqp, s1, xp, out_part, pieces, slots, keep, dpt, dpn, part, gq, pack, packs, packed,
-    sz, rz, inbox, outbox, second, ss, rs,
-    sq, rq, st, rt, su, ru, sw, rw, sg, rg, sc, rc, inbox2, outbox2, second2, ss2, rs2,
+    wt, s1, xp, out_part, pieces, slots, keep, dpt, dpn, part, gq, gqcol, gqsum, pack, packs, packed,
+    passed, sz, rz, inbox, outbox, second, ss, rs, sp,
+    sq, rq, sv, rv, st, rt, su, ru, sw, rw, sg, rg, sc, rc, inbox2, outbox2, second2, ss2, rs2,
 ):
     row, col, z, place = places()
-    me = row * 16 + col
     quarter = col % QUAD
-    core = col % 2
+    y, core = col // 2 % 2, col % 2
+    member = z * 2 + core
+    column = row * 2 + y
     loads = [
         fetch(out_in, out_part, keep.at[3]),
         fetch(s1_in, s1, keep.at[0]),
         fetch(xp_in, xp, keep.at[1]),
-        fetch(wqp_in, wqp, keep.at[2]),
+        fetch(wt_in, wt, keep.at[2]),
     ]
     meet([anyone(row, col, bits) for bits in range(1, 32)])
     copies = []
-    lanes = block(z // 2, 512)
-    for bits in (3, 2, 1):
-        for kind in range(3):
-            copy = push(
-                dproj.at[kind * 64 : kind * 64 + 64, block(flip(z, bits), 512)],
-                dpt.at[pl.ds(pl.multiple_of(kind * 128 + (z % 2) * 64, 64), 64), lanes],
-                sz.at[bits, kind],
-                rz.at[bits, kind],
-                on_line(row, col, bits),
-            )
-            copy.start()
-            copies.append(copy)
-    for kind in range(3):
-        rows = pl.ds(pl.multiple_of(kind * 128 + (z % 2) * 64, 64), 64)
-        dpt[rows, lanes] = dproj[kind * 64 : kind * 64 + 64, block(z, 512)]
+    for plane in range(PLANES):
+        ours = pl.ds(pl.multiple_of(plane * 512 + y * 256, 256), 256)
+        theirs = pl.ds(pl.multiple_of(plane * 512 + (1 - y) * 256, 256), 256)
+        lanes = slice(plane * 256, plane * 256 + 256)
+        copy = push(
+            dproj.at[:, theirs], dpt.at[y, :, lanes], sz.at[plane], rz.at[plane], (row, flip(col, 2))
+        )
+        copy.start()
+        copies.append(copy)
+        dpt[y, :, lanes] = dproj[:, ours]
+    owner = core * 4 + y * 2
+    for j in range(4):
+        there = (row, j // 2 * 8 + owner + j % 2)
+        mine = col == there[1]
+
+        @pl.when(jnp.logical_not(mine))
+        def _():
+            push(gwo.at[j], goin.at[z], sw.at[j], rw.at[z], there).start()
+
+        @pl.when(mine)
+        def _():
+            goin[z] = gwo[j]
+
     loads[0].wait()
     output = Scatter(out_part, inbox2, outbox2, second2, ss2, rs2)
     output.near_all()
@@ -1104,60 +1379,41 @@
     gwg_in[place] = gwg[place]
     for copy in loads[1:]:
         copy.wait()
-    rows_out = (hidden[...] + output.finish()).astype(bf16)
-    for j in range(16):
-        pieces[j] = rows_out[j * 8 : j * 8 + 8, :]
-    for d in range(16):
-        number = 0
-        for j in range(1, 16):
-            number = jnp.where(deal[j] == d, j, number)
-        slots[d] = pieces[number]
     for copy in copies:
         copy.wait_recv()
-    for bits in range(1, 16):
-        there = (row, flip(col, bits))
-        copy = push(slots.at[there[1]], out.at[col], sc.at[bits], rc.at[bits], there)
-        copy.start()
-        spread.append(copy)
-    out[col] = slots[col]
-    for j in range(4):
-        there = (row, quarter * QUAD + j)
-        mine = jnp.logical_and(quarter == z, quarter == j)
-
-        @pl.when(jnp.logical_not(mine))
-        def _():
-            push(gwo.at[j], goin.at[z], sw.at[j], rw.at[z], there).start()
-
-        @pl.when(mine)
-        def _():
-            goin[z] = gwo[j]
-
-    dpn[...] = jnp.transpose(dpt[...])
+    for plane in range(PLANES):
+        lanes = slice(plane * 256, plane * 256 + 256)
+        for kind in range(3):
+            both = jnp.concatenate(
+                [dpt[head, kind * 64 : kind * 64 + 64, lanes] for head in range(2)], axis=0
+            )
+            dpn[lanes, kind * 128 : kind * 128 + 128] = jnp.transpose(both)
+    total = LineScatter(part, inbox, outbox, second, ss, rs, passed, sp)
+    term = jnp.zeros((1, 1024), f32)
+    for own in range(2):
+        for bits in (3, 2, 1, 0):
+            number = 2 * flip(z, bits) + (core if own else 1 - core)
+            values = xp[number].astype(f32)
+            d_scaled = mm(dpn[block(number, 128), :], wt[...])
+            term = term + jnp.sum(d_scaled * (values * norm_scale(values)), axis=0, keepdims=True)
+            part[number] = d_scaled.astype(bf16)
+        if own == 0:
+            for bits in range(4):
+                total.near(flip(z, bits), bits)
+    total.far_all()
     for f in range(8):
         lhs = jnp.concatenate([s1[t, :, f * 128 : f * 128 + 128] for t in range(MEMBERS)], axis=0)
         chunk = mm_tn(lhs, dpn[...]).astype(bf16)
         for j in range(4):
-            gq[f * 4 + j] = chunk[j * 32 : j * 32 + 32, :]
-    for bits in range(31, 0, -1):
-        there = anyone(row, col, bits)
-        number = there[0] * 16 + there[1]
-        copy = push(gq.at[number], gqin.at[me], sq.at[bits], rq.at[bits], there)
+            gq[f // PLANES * 2 + j // 2, f % PLANES * 2 + j % 2] = chunk[j * 32 : j * 32 + 32, :]
+    columns = []
+    for bits in (3, 2, 1):
+        there = (flip(row, bits // 2), flip(col, bits % 2 * 2))
+        copy = push(
+            gq.at[flip(column, bits)], gqcol.at[bits - 1], sv.at[bits], rv.at[bits], there
+        )
         copy.start()
-        spread.append(copy)
-    gqin[me] = gq[me]
-    gain_one = gains[0:1, :]
-    total = Scatter(part, inbox, outbox, second, ss, rs)
-    term = jnp.zeros((1, 1024), f32)
-    for own in range(2):
-        for bits in (3, 2, 1, 0):
-            number = 2 * flip(place // 2, bits) + (core if own else 1 - core)
-            values = xp[number].astype(f32)
-            d_scaled = mm_nt(dpn[block(number, 128), :], wqp[...])
-            term = term + jnp.sum(d_scaled * (values * norm_scale(values)), axis=0, keepdims=True)
-            part[number] = d_scaled.astype(bf16)
-        if own == 0:
-            total.near_all()
-    total.far_all()
+        columns.append(copy)
     for k in range(8):
         pack[k] = bias_tile[...]
         pack[k, 0:1, :] = term[:, k * 128 : k * 128 + 128]
@@ -1171,6 +1427,20 @@
         copy.start()
         first.append(copy)
     packs[place] = pack[pl.ds(row * PLANES, PLANES)]
+    rows_out = (hidden[...] + output.finish()).astype(bf16)
+    for j in range(16):
+        pieces[j] = rows_out[j * 8 : j * 8 + 8, :]
+    for d in range(16):
+        number = 0
+        for j in range(1, 16):
+            number = jnp.where(deal[j] == d, j, number)
+        slots[d] = pieces[number]
+    for bits in range(1, 16):
+        there = (row, flip(col, bits))
+        copy = push(slots.at[there[1]], out.at[col], sc.at[bits], rc.at[bits], there)
+        copy.start()
+        spread.append(copy)
+    out[col] = slots[col]
     for copy in first:
         copy.wait_recv()
     summed = packs[0]
@@ -1184,39 +1454,53 @@
         copy.start()
         spread.append(copy)
     sums[z] = packed[z]
+    for copy in columns:
+        copy.wait_recv()
+    for m in range(MEMBERS):
+        gqsum[m] = (
+            (gq[column, m].astype(f32) + gqcol[0, m].astype(f32))
+            + (gqcol[1, m].astype(f32) + gqcol[2, m].astype(f32))
+        ).astype(bf16)
+    for bits in range(7, 0, -1):
+        there = in_line(row, col, bits)
+        copy = push(gqsum.at[flip(member, bits)], gqin.at[member], sq.at[bits], rq.at[bits], there)
+        copy.start()
+        spread.append(copy)
+    gqin[member] = gqsum[member]
     d_one = total.finish()
-    own_rows = xp[place].astype(f32)
+    own_rows = xp[member].astype(f32)
     scale = norm_scale(own_rows)
     grad_tokens[...] = (
-        d_hidden[...] + norm_back(d_one * gain_one, own_rows * scale, scale)
+        d_hidden[...] + norm_back(d_one * gains[0:1, :], own_rows * scale, scale)
     ).astype(bf16)
     for copy in spread:
         copy.wait_recv()
+    senders = col // 2 % 2 * 2 + col // 4 % 2
     for plane in range(PLANES):
-        mine = jnp.logical_and(quarter == z, z == plane)
+        mine = jnp.logical_and(quarter == senders, z == plane)
 
         @pl.when(jnp.logical_not(mine))
         def _():
             push(
-                gwo.at[0], goin.at[plane], sw.at[plane], rw.at[plane], (row, plane * QUAD + z)
+                gwo.at[0], goin.at[plane], sw.at[0], rw.at[plane], (row, plane * QUAD + senders)
             ).wait_recv()
 
     for j in range(4):
-        there = (row, quarter * QUAD + j)
-        mine = jnp.logical_and(quarter == z, quarter == j)
+        there = (row, j // 2 * 8 + owner + j % 2)
+        mine = col == there[1]
 
         @pl.when(jnp.logical_not(mine))
         def _():
             push(gwo.at[j], goin.at[z], sw.at[j], rw.at[z], there).wait_send()
 
-    for copy in copies + first + spread:
+    for copy in copies + columns + first + spread:
         copy.wait_send()
     total.close()
     output.close()
 
 
 def finish_body(
-    place_info, grad_tokens_in, gqin, goin, out_in, gwg, gwd, tiles,
+    grad_tokens_in, gqin, goin, out_in, gwg, gwd, tiles,
     out, grad_tokens, grad_q, grad_o, grad_gu, grad_d, grad_gains, grad_bias,
 ):
     grad_tokens[...] = grad_tokens_in[...]
@@ -1228,9 +1512,7 @@
         gwd[2].astype(f32) + gwd[3].astype(f32)
     )
     for p in range(MEMBERS):
-        total = jnp.zeros((32, 384), f32)
-        for plane in range(PLANES):
-            total = total + gqin[(p // QUAD) * 16 + plane * QUAD + p % QUAD].astype(f32)
+        total = gqin[p].astype(f32)
         for kind in range(3):
             at = kind * 1024 + p * 128
             grad_q[:, at : at + 128] = total[:, kind * 128 : kind * 128 + 128]
@@ -1241,7 +1523,7 @@
                 start = half * 4096 + unit * 128
                 grad_gu[:, start : start + 128] = gwg[p, :, at : at + 128].astype(f32)
     total = (tiles[0] + tiles[1]) + (tiles[2] + tiles[3])
-    quarter = place_info[0]
+    quarter = lax.axis_index("col") % QUAD
     chosen = jnp.zeros((2, 32), f32)
     for k in range(4):
         chosen = chosen + jnp.where(quarter == k, total[0:2, k * 32 : k * 32 + 32], 0.0)
@@ -1277,22 +1559,18 @@
     tokens, variate_ids, time_ids, lengths, deal, w_qkv, w_out, w_gate_up, w_down,
     gain_attn, gain_ffn, var_bias, cotangent,
 ):
-    row = lax.axis_index("row")
-    col = lax.axis_index("col")
-    z, q = col // QUAD, col % QUAD
-    place = row * QUAD + q
     rows, width = tokens.shape
     lines = [[plane * QUAD + k for plane in range(PLANES)] for k in range(QUAD)]
-    freq = jnp.exp(-math.log(10000.0) * jnp.arange(32, dtype=f32) / 32)[:, None]
+    freq = jnp.asarray(np.exp(-math.log(10000.0) * np.arange(32) / 32).astype(np.float32)[:, None])
     target = deal[0, 0]
 
-    xp, wqp, wop, wgp, cotp, s1, qkvt, gains, labels = kernel(
+    xp, wt, wop, wgp, cotp, s1, qkvt, gains, labels = kernel(
         enter_body,
         "enter",
         [VM] * 9 + [SM, SM, VM],
         [
             sds((8, rows, width), bf16),
-            sds((32, 32, 384), bf16),
+            sds((384, 1024), bf16),
             sds((4, 32, 1024), bf16),
             sds((8, 32, 1024), bf16),
             sds((8, rows, width), bf16),
@@ -1303,11 +1581,12 @@
         ],
         [
             pltpu.VMEM((8, rows, width), bf16),
-            pltpu.VMEM((32, 32, 384), bf16),
             pltpu.VMEM((8, rows, width), bf16),
             pltpu.VMEM((8, rows, width), bf16),
             dma(4),
             pltpu.VMEM((8, 32, 384), bf16),
+            pltpu.VMEM((8, 32, 384), bf16),
+            pltpu.VMEM((4, 8, 32, 384), bf16),
             pltpu.VMEM((8, 32, 1024), bf16),
             pltpu.VMEM((16, 8, width), bf16),
             pltpu.VMEM((rows, width), bf16),
@@ -1315,13 +1594,13 @@
             pltpu.VMEM((4, 8, 128), f32),
             pltpu.VMEM((8, 4, 8, 128), f32),
             pltpu.VMEM((384, 1024), bf16),
-            pltpu.VMEM((4, 192, 512), bf16),
+            pltpu.VMEM((2, 192, 1024), bf16),
             pltpu.VMEM((32, 1024), f32),
             pltpu.VMEM((32, 1024), f32),
             pltpu.VMEM((8, 1024), f32),
         ]
-        + [dma(8), dma(8), dma(32), dma(32), dma(4), dma(4), dma(8), dma(8), dma(4), dma(4)]
-        + [dma(8), dma(8), dma(16), dma(16), dma(8), dma(8), dma(4), dma(4)],
+        + [dma(8), dma(8), dma(8), dma(8), dma(4), dma(4), dma(4), dma(4), dma(8), dma(8)]
+        + [dma(4), dma(4), dma(8), dma(8), dma(16), dma(16), dma(8), dma(8), dma(4), dma(4)],
         number=1,
         places_out=[ANY, ANY, VM, VM, ANY, ANY, VM, VM, VM],
     )(
@@ -1332,19 +1611,13 @@
     gate_up = lax.all_gather(
         wgp.reshape(256, 1024), "col", axis=0, tiled=True, axis_index_groups=lines
     )
-    wqp = wqp.reshape(1024, 384)
     wop = wop.reshape(128, 1024)
 
-    head = place * 2 + z % 2
-    info = jnp.concatenate(
-        [labels[4, :NSEQ].astype(jnp.int32), head[None].astype(jnp.int32), jnp.zeros((1,), jnp.int32)]
-    )
-    bias = lax.dynamic_slice_in_dim(var_bias, head, 1, 1)[:, 0]
     wide = 2048 + WINDOW
     att, den, low, qa, ka = kernel(
         attend_body,
         "attend",
-        [SM, SM, VM, VM],
+        [SM, VM, VM],
         [
             sds((64, wide), f32),
             sds((8, wide), f32),
@@ -1352,9 +1625,9 @@
             sds((AUG, wide), bf16),
             sds((2048, AUG), bf16),
         ],
-        [pltpu.VMEM((AUG, 2048), bf16)],
+        [pltpu.VMEM((AUG, 2048), bf16), pltpu.SMEM((8,), jnp.int32)],
         cost=2 * 10**9,
-    )(info, bias, qkvt, labels)
+    )(var_bias, qkvt, labels)
 
     atp, hidden, s2 = kernel(
         branch_body,
@@ -1396,6 +1669,8 @@
             pltpu.VMEM((8, rows, width), bf16),
             pltpu.VMEM((4, rows, width), bf16),
             pltpu.VMEM((8, 128, 1024), bf16),
+            pltpu.VMEM((rows, width), bf16),
+            pltpu.VMEM((rows, width), bf16),
             dma(11), dma(8), dma(8), dma(4), dma(4), dma(4), dma(4),
         ]
         + scatter_scratch(rows, width),
@@ -1424,7 +1699,7 @@
     dproj, bias_tile = kernel(
         attend_back_body,
         "attend_back",
-        [SM] + [VM] * 8,
+        [VM] * 8,
         [sds((192, 2048), bf16), sds((8, 128), f32)],
         [
             pltpu.VMEM((64, wide), bf16),
@@ -1433,9 +1708,10 @@
             pltpu.VMEM((64, wide), f32),
             pltpu.VMEM((AUG, 2048), f32),
             pltpu.VMEM((64, 2048), f32),
+            pltpu.SMEM((8,), jnp.int32),
         ],
         cost=5 * 10**9,
-    )(info, qkvt, qa, ka, labels, freq, grad, att, den)
+    )(qkvt, qa, ka, labels, freq, grad, att, den)
 
     grad_tokens, gqin, goin, gwg_in, sums, out = kernel(
         last_body,
@@ -1443,42 +1719,45 @@
         [VM] + [ANY] * 4 + [VM] * 7 + [SM],
         [
             sds((rows, width), bf16),
-            sds((32, 32, 384), bf16),
+            sds((8, 32, 384), bf16),
             sds((4, 32, 1024), bf16),
             sds((8, 32, 1024), bf16),
             sds((4, 8, 128), f32),
             sds((16, 8, width), bf16),
         ],
         [
-            pltpu.VMEM((1024, 384), bf16),
+            pltpu.VMEM((384, 1024), bf16),
             pltpu.VMEM((8, rows, width), bf16),
             pltpu.VMEM((8, rows, width), bf16),
             pltpu.VMEM((8, rows, width), bf16),
             pltpu.VMEM((16, 8, width), bf16),
             pltpu.VMEM((16, 8, width), bf16),
             dma(4),
-            pltpu.VMEM((384, 1024), bf16),
+            pltpu.VMEM((2, 192, 1024), bf16),
             pltpu.VMEM((1024, 384), bf16),
             pltpu.VMEM((8, rows, width), bf16),
-            pltpu.VMEM((32, 32, 384), bf16),
+            pltpu.VMEM((4, 8, 32, 384), bf16),
+            pltpu.VMEM((3, 8, 32, 384), bf16),
+            pltpu.VMEM((8, 32, 384), bf16),
             pltpu.VMEM((8, 8, 128), f32),
             pltpu.VMEM((8, 4, 8, 128), f32),
             pltpu.VMEM((4, 8, 128), f32),
-            dma(4, 3), dma(4, 3),
+            pltpu.VMEM((rows, width), bf16),
+            dma(4), dma(4),
         ]
         + scatter_scratch(rows, width)
-        + [dma(32), dma(32), dma(8), dma(8), dma(4), dma(4), dma(4), dma(4), dma(8), dma(8)]
-        + [dma(16), dma(16)]
+        + [dma(2), dma(8), dma(8), dma(4), dma(4), dma(8), dma(8), dma(4), dma(4)]
+        + [dma(4), dma(4), dma(8), dma(8), dma(16), dma(16)]
         + scatter_scratch(rows, width),
         number=5,
     )(
-        dproj, wqp, s1, xp, out_part, gains, d_hidden, hidden, gwo.reshape(4, 32, 1024),
+        dproj, wt, s1, xp, out_part, gains, d_hidden, hidden, gwo.reshape(4, 32, 1024),
         gate_up_sum.reshape(8, 32, 1024), gain_two, bias_tile, target,
     )
     out, grad_tokens, grad_q, grad_o, grad_gate_up, grad_down, gain_grads, bias_grads = kernel(
         finish_body,
         "finish",
-        [SM] + [VM] * 7,
+        [VM] * 7,
         [
             sds((rows, width), bf16),
             sds((rows, width), bf16),
@@ -1491,7 +1770,7 @@
         ],
         [],
     )(
-        q[None].astype(jnp.int32), grad_tokens, gqin, goin, out.reshape(rows, width), gwg_in,
+        grad_tokens, gqin, goin, out.reshape(rows, width), gwg_in,
         down_in, sums,
     )
     return (

time: 307 us -> 288 us (0.938)
  Pallas kernels: 278 us -> 244 us
  waiting for transfers between devices: 10.3 us -> 28.1 us
    pallas_call x1, Pallas kernels: 60.9 us -> 44.9 us  [plane_shards(): kernel(ffn_body, 'ffn', [VM, ANY, ANY, VM, VM, VM], [sds((8, rows, width)...]
    all_gather x1, waiting for transfers between devices: 3.02 us -> 12.5 us  [plane_shards(): lax.all_gather(wgp.reshape(256, 1024), 'col', axis=0, tiled=True, axis_in...]
    reduce_scatter x1, waiting for transfers between devices: 7.29 us -> 15.6 us  [plane_shards(): lax.psum_scatter(gwg.reshape(1024, 1024), 'col', scatter_dimension=0, til...]
    pallas_call x1, Pallas kernels: 37.6 us -> 31.1 us  [plane_shards(): kernel(branch_body, 'branch', [VM] * 4, [sds((128, 1024), bf16), sds((row...]
    pallas_call x3, Pallas kernels: 28.6 us -> 22.2 us  [the longest x1 11.4 us: plane_shards(): kernel(attend_back_body, 'attend_back', [VM] * 8, [sds((192, 2048), bf16)...]
    pallas_call x1, Pallas kernels: 62.8 us -> 58.1 us  [plane_shards(): kernel(enter_body, 'enter', [VM] * 9 + [SM, SM, VM], [sds((8, rows, width...]
    pallas_call x1, Pallas kernels: 23.9 us -> 28.5 us  [plane_shards(): kernel(attended_back_body, 'attended_back', [VM] * 3, [sds((64, 2048), bf...]
    pallas_call x1, Pallas kernels: 64.2 us -> 59.7 us  [plane_shards(): kernel(last_body, 'last', [VM] + [ANY] * 4 + [VM] * 7 + [SM], [sds((rows,...]
  transfers between devices with their start and end apart: 2 -> 2, of which waited for: 2 -> 2; matrix products, arithmetic and copies ran while one was open for 1% -> 0% of each run, Pallas kernels for 28% -> 27%
where the time goes in v3:
time: 288 us
  Pallas kernels  244 us (85%)
  waiting for transfers between devices  28.1 us (10%)
  between operations  14.1 us (5%)
    pallas_call x1, Pallas kernels, plane_shards(): kernel(last_body, 'last', [VM] + [ANY] * 4 + [VM] * 7 + [SM], [sds((rows,...  59.7 us
    pallas_call x1, Pallas kernels, plane_shards(): kernel(enter_body, 'enter', [VM] * 9 + [SM, SM, VM], [sds((8, rows, width...  58.1 us
    pallas_call x1, Pallas kernels, plane_shards(): kernel(ffn_body, 'ffn', [VM, ANY, ANY, VM, VM, VM], [sds((8, rows, width)...  44.9 us
    pallas_call x1, Pallas kernels, plane_shards(): kernel(branch_body, 'branch', [VM] * 4, [sds((128, 1024), bf16), sds((row...  31.1 us
    pallas_call x1, Pallas kernels, plane_shards(): kernel(attended_back_body, 'attended_back', [VM] * 3, [sds((64, 2048), bf...  28.5 us
    reduce_scatter x1, waiting for transfers between devices, plane_shards(): lax.psum_scatter(gwg.reshape(1024, 1024), 'col', scatter_dimension=0, til...  15.6 us
    all_gather x1, waiting for transfers between devices, plane_shards(): lax.all_gather(wgp.reshape(256, 1024), 'col', axis=0, tiled=True, axis_in...  12.5 us
    pallas_call x1, Pallas kernels, plane_shards(): kernel(attend_back_body, 'attend_back', [VM] * 8, [sds((192, 2048), bf16)...  11.4 us
  transfers between devices with their start and end apart: 2, of which 2 were waited for; matrix products, arithmetic and copies ran while one was open for 0% of the time, Pallas kernels for 27%

profile of v3, /device:TPU:0, one launch (start us, length us, event | category | flops | bytes accessed | tf_op | source)
XLA Modules:
  0.0 288.1 jit_solution(3498530994883067099)
XLA Ops:
  7.2 0.0 all-gather.2.cloned.1.call-start
  7.2 58.1 %enter.1 = (bf16[8,128,1024]{2,1,0:T(8,128)(2,1)}, bf16[384,1024]{1,0:T(8,128)(2,1)}, bf16[4,32,1024]{2,1,0:T(8,128)(2,1)}, bf16[8,32,1024]{2,1,0:T(8,128)(2,1)}...) custom-call(bf16[128,1024]{1,0:T(8,128)(2,1)} %x.3, ...), custom_call_target="tpu_custom_call" | custom-call | tf_op jit(solution)/shard_map/enter/pallas_call | solution.py:1567
  65.4 0.0 all-gather.2.cloned.1.call-update
  65.4 0.0 reduce-scatter.2.cloned.1.call-start
  65.4 7.6 %attend.1 = (f32[64,2560]{1,0:T(8,128)}, f32[8,2560]{1,0:T(8,128)}, bf16[64,2560]{1,0:T(8,128)(2,1)}, bf16[128,2560]{1,0:T(8,128)(2,1)}, bf16[2048,128]{1,0:T(8,128)(2,1)}) custom-call(f32[2,16]{1,0:T(2,128)} %bias_all.1, bf16[192,2048]{1,0:T(8,128)(2,1)} %get-tuple-element.50.qkvt, f32[8,2048]{1,0:T(8,128)} %get-tuple-element.51.labels), custom_call_target="tpu_custom_call" | custom-call | flops 2000000000 | bytes 6666666 | tf_op jit(solution)/shard_map/attend/pallas_call | solution.py:1617
  73.1 31.1 %branch.1 = (bf16[128,1024]{1,0:T(8,128)(2,1)}, f32[128,1024]{1,0:T(8,128)}, bf16[128,1024]{1,0:T(8,128)(2,1)}) custom-call(bf16[64,2560]{1,0:T(8,128)(2,1)} %get-tuple-element.54.low, bf16[128,1024]{1,0:T(8,128)(2,1)} %bitcast.18, bf16[128,1024]{1,0:T(8,128)(2,1)} %x.3, f32[8,1024]{1,0:T(8,128)} %get-tuple-element.56.gains), custom_call_target="tpu_custom_call" | custom-call | tf_op jit(solution)/shard_map/branch/pallas_call | solution.py:1632
  104.2 12.5 %all-gather.2.cloned.1.call-done = bf16[1024,1024]{1,0:T(8,128)(2,1)} async-done(((bf16[256,1024]{1,0:T(8,128)(2,1)}), bf16[1024,1024]{1,0:T(8,128)(2,1)}) %all-gather.2.cloned.1.call-update) | async-done | bytes 2097168 | tf_op jit(solution)/shard_map/all_gather | solution.py:1611
  116.7 44.9 %ffn.1 = (bf16[8,128,1024]{2,1,0:T(8,128)(2,1)}, bf16[4,128,1024]{2,1,0:T(8,128)(2,1)}, bf16[8,128,1024]{2,1,0:T(8,128)(2,1)}, f32[128,1024]{1,0:T(8,128)}, bf16...) custom-call(bf16[128,1024]{1,0:T(8,128)(2,1)} %get-tuple-element.57.s2, bf16[8,128,1024]{2,1,0:T(8,128)(2,1)} %get-tuple-element.58.cotp_in, ...), custom_call_target="tpu_custom_call" | custom-call | flops 10000000000 | bytes 33333332 | tf_op jit(solution)/shard_map/ffn/pallas_call | solution.py:1646
  161.6 0.0 reduce-scatter.2.cloned.1.call-update
  161.6 28.5 %attended_back.1 = (bf16[64,2048]{1,0:T(8,128)(2,1)}, bf16[128,1024]{1,0:T(8,128)(2,1)}) custom-call(bf16[128,1024]{1,0:T(8,128)(2,1)} %get-tuple-element.61.low, bf16[128,1024]{1,0:T(8,128)(2,1)} %bitcast.19, bf16[128,1024]{1,0:T(8,128)(2,1)} %get-tuple-element.62.atp), custom_call_target="tpu_custom_call" | custom-call | tf_op jit(solution)/shard_map/attended_back/pallas_call | solution.py:1686
  190.1 11.4 %attend_back.1 = (bf16[192,2048]{1,0:T(8,128)(2,1)}, f32[8,128]{1,0:T(8,128)}) custom-call(bf16[192,2048]{1,0:T(8,128)(2,1)} %get-tuple-element.50.qkvt, bf16[128,2560]{1,0:T(8,128)(2,1)} %get-tuple-element.52.qa, bf16[2048,128]{1,0:T(8,128)(2,1)} %get-tuple-element.53.ka, f32[8,2048]{1,0:T(8,128)} %get-tuple-element.51.labels, f32[32,1]{1,0:T(8,128)} %constant.2.clone.freq, ...), custom_call_target="tpu_custom_call" | custom-call | flops 5000000000 | bytes 16666666 | tf_op jit(solution)/shard_map/attend_back/pallas_call | solution.py:1699
  201.4 15.6 %reduce-scatter.2.cloned.1.call-done = bf16[256,1024]{1,0:T(8,128)(2,1)} async-done(((bf16[1024,1024]{1,0:T(8,128)(2,1)}), bf16[256,1024]{1,0:T(8,128)(2,1)}) %reduce-scatter.2.cloned.1.call-update) | async-done | bytes 524304 | tf_op jit(solution)/shard_map/reduce_scatter | solution.py:1682
  217.0 59.7 %last.1 = (bf16[128,1024]{1,0:T(8,128)(2,1)}, bf16[8,32,384]{2,1,0:T(8,128)(2,1)}, bf16[4,32,1024]{2,1,0:T(8,128)(2,1)}, bf16[8,32,1024]{2,1,0:T(8,128)(2,1)}, f...) custom-call(bf16[192,2048]{1,0:T(8,128)(2,1)} %get-tuple-element.66.dproj, bf16[384,1024]{1,0:T(8,128)(2,1)} %get-tuple-element.67.wt_in, ...), custom_call_target="tpu_custom_call" | custom-call | tf_op jit(solution)/shard_map/last/pallas_call | solution.py:1716
  276.7 3.2 %finish.1 = (bf16[128,1024]{1,0:T(8,128)(2,1)}, bf16[128,1024]{1,0:T(8,128)(2,1)}, f32[32,3072]{1,0:T(8,128)}, f32[32,1024]{1,0:T(8,128)}, f32[32,8192]{1,0:T(8,...) custom-call(bf16[128,1024]{1,0:T(8,128)(2,1)} %get-tuple-element.76.grad_tokens_in, ...), custom_call_target="tpu_custom_call" | custom-call | tf_op jit(solution)/shard_map/finish/pallas_call | solution.py:1757
  280.0 1.3 slice_bitcast_fusion
Async XLA Ops:
  7.2 109.5 %all-gather.2.cloned.1.call-start = ((), (), s32[]{:S(2)}) async-start(), calls=%async_computation.1 | async-start | bytes 2621440 | tf_op jit(solution)/shard_map/all_gather | solution.py:1611
  65.4 151.7 %reduce-scatter.2.cloned.1.call-start = ((), (), s32[]{:S(2)}) async-start(), calls=%async_computation.2 | async-start | bytes 2621440 | tf_op jit(solution)/shard_map/reduce_scatter | solution.py:1682
Sparse Core Ops, SparseCore 0:
  65.5 51.1 all-gather.1
  161.7 55.2 reduce-scatter.1

commit v4 on v3

--- a/solution.py
+++ b/solution.py
@@ -512,7 +512,7 @@
         if place is not None:
             self.place = place
         self.core = self.col % 2
-        self.copies, self.sent = [], []
+        self.copies, self.sent = {}, []
 
     def near(self, chip, number):
         copy = push(
@@ -523,7 +523,7 @@
             self.peer(self.row, self.col, 1),
         )
         copy.start()
-        self.copies.append(copy)
+        self.copies[number] = copy
 
     def far(self, bits):
         self.copies[bits].wait_recv()
@@ -558,8 +558,58 @@
         return total
 
     def close(self):
-        for copy in self.copies + self.sent:
+        for copy in list(self.copies.values()) + self.sent:
             copy.wait_send()
+
+
+class RoundScatter(Scatter):
+    def __init__(self, part, inbox, outbox, second, send, recv, passed, sems):
+        super().__init__(part, inbox, outbox, second, send, recv)
+        self.passed, self.sems = passed, sems
+
+    def sum_for(self, bits):
+        self.copies[bits].wait_recv()
+        chip = flip(self.place // 2, bits)
+        return self.part[2 * chip + self.core].astype(f32) + self.inbox[bits].astype(f32)
+
+    def far_first(self):
+        self.outbox[2] = self.sum_for(3).astype(bf16)
+        across = in_plane(self.row, self.col, 4)
+        self.passing = push(
+            self.outbox.at[2], self.passed, self.sems.at[0], self.sems.at[1], across
+        )
+        self.passing.start()
+        self.outbox[1] = self.sum_for(2).astype(bf16)
+        self.sent.append(
+            push(self.outbox.at[1], self.second.at[1], self.send.at[5], self.recv.at[5], across)
+        )
+        self.sent[0].start()
+
+    def far_second(self):
+        total = self.sum_for(1)
+        self.passing.wait_recv()
+        self.outbox[0] = (total + self.passed[...].astype(f32)).astype(bf16)
+        self.sent.append(
+            push(
+                self.outbox.at[0],
+                self.second.at[0],
+                self.send.at[4],
+                self.recv.at[4],
+                in_plane(self.row, self.col, 2),
+            )
+        )
+        self.sent[1].start()
+
+    def finish(self):
+        self.copies[0].wait_recv()
+        total = self.part[self.place].astype(f32) + self.inbox[0].astype(f32)
+        for copy in self.sent:
+            copy.wait_recv()
+        return total + (self.second[0].astype(f32) + self.second[1].astype(f32))
+
+    def close(self):
+        super().close()
+        self.passing.wait_send()
 
 
 class LineScatter(Scatter):
@@ -575,6 +625,10 @@
         chip = flip(self.place // 2, bits)
         return self.part[2 * chip + self.core].astype(f32) + self.inbox[bits].astype(f32)
 
+    def sum_again(self, bits):
+        chip = flip(self.place // 2, bits)
+        return self.part[2 * chip + self.core].astype(f32) + self.inbox[bits].astype(f32)
+
     def to(self, bits):
         return push(
             self.outbox.at[bits - 1],
@@ -584,42 +638,45 @@
             in_line(self.row, self.col, 2 * bits),
         )
 
-    def far_all(self):
-        self.outbox[2] = self.sum_for(3).astype(bf16)
-        self.across = self.to(3)
-        self.passing = push(
-            self.outbox.at[2],
-            self.passed,
-            self.sems.at[0],
-            self.sems.at[1],
-            in_line(self.row, self.col, 2),
-        )
-
-        @pl.when(self.end)
-        def _():
-            self.passing.start()
-            self.second[2] = jnp.zeros(self.second.shape[1:], bf16)
-
-        @pl.when(self.inner)
-        def _():
-            self.across.start()
-
-        total = self.sum_for(2)
-        self.sent = [self.to(2), self.to(1)]
-
-        @pl.when(self.end)
-        def _():
-            self.outbox[1] = total.astype(bf16)
-            self.sent[0].start()
-
-        self.outbox[0] = self.sum_for(1).astype(bf16)
-        self.sent[1].start()
-
+    def far(self, bits):
+        self.outbox[bits - 1] = self.sum_for(bits).astype(bf16)
+        if bits == 1:
+            self.sent.append(self.to(1))
+            self.sent[-1].start()
+        if bits == 2:
+            self.added = self.to(2)
+            self.sent.append(self.added)
+
+            @pl.when(self.end)
+            def _():
+                self.added.start()
+
+        if bits == 3:
+            self.across = self.to(3)
+            self.passing = push(
+                self.outbox.at[2],
+                self.passed,
+                self.sems.at[0],
+                self.sems.at[1],
+                in_line(self.row, self.col, 2),
+            )
+
+            @pl.when(self.end)
+            def _():
+                self.passing.start()
+                self.second[2] = jnp.zeros(self.second.shape[1:], bf16)
+
+            @pl.when(self.inner)
+            def _():
+                self.across.start()
+
+    def far_second(self):
         @pl.when(self.inner)
         def _():
             self.passing.wait_recv()
-            self.outbox[1] = (total + self.passed[...].astype(f32)).astype(bf16)
-            self.sent[0].start()
+            total = self.sum_again(2) + self.passed[...].astype(f32)
+            self.outbox[1] = total.astype(bf16)
+            self.added.start()
 
     def finish(self):
         @pl.when(self.inner)
@@ -661,10 +718,10 @@
 
 
 def enter_body(
-    x, wq, wo, wg, cot, ga, gf, variate, time, lengths, deal, freq,
-    xp_out, wt_out, wop, wgp, cotp_out, s1_out, qkvt, gains, labels,
-    xp, cotp, s1, keep, wqs, wline, wqp, wgs, cotr, cots, tile, tl, tiles, wt, box, cs, sn, times,
-    sx, rx, sq, rq, sv, rv, st, rt, su, ru, sw, rw, sg, rg, sc, rc, sa, ra, sz, rz,
+    x, wq, wo, wg, ga, gf, variate, time, lengths, freq,
+    xp_out, wt_out, wop, wgp, s1_out, qkvt, gains, labels,
+    xp, s1, keep, wqs, wline, wqp, wgs, tile, tl, tiles, wt, box, cs, sn, times,
+    sx, rx, sq, rq, sv, rv, st, rt, su, ru, sw, rw, sg, rg, sz, rz,
 ):
     row, col, z, place = places()
     quarter = col % QUAD
@@ -695,17 +752,10 @@
     for bits in (1, 2, 3):
         first.append(push(tile, tl.at[z], st.at[bits], rt.at[bits], on_line(row, col, bits)))
         first[-1].start()
-    pieces = []
-    for bits in range(1, 16):
-        there = (row, flip(col, bits))
-        pieces.append(push(cot.at[there[1]], cotr.at[col], sc.at[bits], rc.at[bits], there))
-        pieces[-1].start()
     rows_in = LineGather(xp, sx, rx)
-    rows_in.start(x)
     xp[member] = x[...]
     wline[member] = wqs[member]
     tl[z] = tile[...]
-    cotr[col] = cot[col]
     for p in range(MEMBERS):
         for half in range(2):
             for plane in range(PLANES):
@@ -713,36 +763,41 @@
                 at = half * 512 + plane * 128
                 start = half * 4096 + unit * 128
                 wgs[p, :, at : at + 128] = wg[:, start : start + 128]
+    blocks = []
+    for bits in range(1, 8):
+        there = in_plane(row, col, bits)
+        blocks.append(
+            push(wgs.at[flip(place, bits)], wgp.at[place], sg.at[bits], rg.at[bits], there)
+        )
+        blocks[-1].start()
+    wgp[place] = wgs[place]
     for copy in first:
         copy.wait_recv()
+    rows_in.start(x)
     column = row * 2 + y
+    beside, across = (row, flip(col, 2)), (flip(row, 1), col)
+    ways = [
+        push(wline, wqp.at[column], sv.at[1], rv.at[1], beside),
+        push(wline, wqp.at[column], sv.at[2], rv.at[2], across),
+    ]
+    for copy in ways:
+        copy.start()
+    wqp[column] = wline[...]
     second = []
-    for bits in (1, 2, 3):
-        there = (flip(row, bits // 2), flip(col, bits % 2 * 2))
-        second.append(push(wline, wqp.at[column], sv.at[bits], rv.at[bits], there))
-        second[-1].start()
-    wqp[column] = wline[...]
     for bits in range(1, 8):
         there = in_plane(row, col, bits)
         second.append(push(tl, tiles.at[place], su.at[bits], ru.at[bits], there))
         second[-1].start()
     tiles[place] = tl[...]
-    blocks = []
-    for bits in range(1, 8):
-        there = in_plane(row, col, bits)
-        blocks.append(
-            push(wgs.at[flip(place, bits)], wgp.at[place], sg.at[bits], rg.at[bits], there)
-        )
-        blocks[-1].start()
-    wgp[place] = wgs[place]
-    for copy in pieces:
+    ways[0].wait_recv()
+    slot = wqp.at[flip(column, 1)]
+    ways.append(push(slot, slot, sv.at[3], rv.at[3], across))
+    ways[2].start()
+    for copy in second:
         copy.wait_recv()
-    for j in range(16):
-        cots[j * 8 : j * 8 + 8, :] = cotr[jnp.clip(deal[j], 0, 15)]
-    cot_in = Gather(cotp, sa, ra)
-    cot_in.start(cots)
-    cotp[place] = cots[...]
-    for copy in second:
+    rows_in.forward(4)
+    rows_in.forward(2)
+    for copy in ways[1:]:
         copy.wait_recv()
     for k in range(8):
         lanes = slice(k * 128, k * 128 + 128)
@@ -801,22 +856,18 @@
         qkvt[:, lanes] = box[y, :, block(chip, 256)]
 
     for k, bits in enumerate((0, 4, 2, 6)):
-        if bits:
-            rows_in.forward(bits)
-        if bits == 4:
-            cot_in.forward(2)
-            cot_in.forward(4)
-            cot_in.forward(6)
+        if bits == 6:
+            rows_in.forward(6)
         rows_in.arrived(bits)
         chip = flip(z, bits // 2)
         project(chip)
         exchange(chip, k)
         if bits == 2:
             target = col // 2 % 2 * 2 + col // 4 % 2
-            slot = col // 8 * 2 + col % 2
+            slot = row * 2 + col % 2
             for plane in range(PLANES):
-                there = (row, plane * QUAD + target)
-                mine = jnp.logical_and(z == plane, quarter == target)
+                there = (col // 8, plane * QUAD + target)
+                mine = jnp.logical_and(row * 16 + col == there[0] * 16 + there[1], z == plane)
 
                 @pl.when(jnp.logical_not(mine))
                 def _():
@@ -828,24 +879,21 @@
 
     kept.append(fetch(xp, xp_out, keep.at[0]))
     kept.append(fetch(s1, s1_out, keep.at[1]))
-    for bits in (0, 2, 4, 6):
-        cot_in.arrived(bits)
-    kept.append(fetch(cotp, cotp_out, keep.at[3]))
     for copy in blocks:
         copy.wait_recv()
     for j in range(4):
-        source = j // 2 * 8 + core * 4 + y * 2 + j % 2
-        mine = col == source
+        source = (j // 2, row * 8 + core * 4 + y * 2 + j % 2)
+        mine = jnp.logical_and(row == source[0], col == source[1])
 
         @pl.when(jnp.logical_not(mine))
         def _():
-            push(wo, wop.at[j], sw.at[j], rw.at[j], (row, source)).wait_recv()
+            push(wo, wop.at[j], sw.at[j], rw.at[j], source).wait_recv()
 
     target = col // 2 % 2 * 2 + col // 4 % 2
-    slot = col // 8 * 2 + col % 2
+    slot = row * 2 + col % 2
     for plane in range(PLANES):
-        there = (row, plane * QUAD + target)
-        mine = jnp.logical_and(z == plane, quarter == target)
+        there = (col // 8, plane * QUAD + target)
+        mine = jnp.logical_and(row * 16 + col == there[0] * 16 + there[1], z == plane)
 
         @pl.when(jnp.logical_not(mine))
         def _():
@@ -854,8 +902,7 @@
     for copy in turned:
         copy.wait()
     rows_in.close()
-    cot_in.close()
-    for copy in first + second + pieces + blocks:
+    for copy in first + second + blocks + ways:
         copy.wait_send()
     for copy in kept:
         copy.wait()
@@ -1036,31 +1083,39 @@
 
 
 def branch_body(
-    low, wop, x, gains,
-    atp, hidden, s2,
-    atn, part, sz, rz, inbox, outbox, second, ss, rs,
+    low, wop, x, gains, cot, deal,
+    atp, hidden, s2, cotp_out,
+    cotp, cotr, cots, keep, atn, part, sz, rz, sc, rc, sa, ra, inbox, outbox, second, ss, rs,
 ):
     row, col, z, place = places()
     quarter = col % QUAD
-    meet(plane_near(row, col) + column_all(row, col))
-    rows, lanes = block(z % 2, 64), block(row, 512)
+    dealt = [(row, flip(col, bits)) for bits in range(1, 16)]
+    others = [(flip(row, 1), flip(col, bits)) for bits in (0, 2, 4, 8, 12)]
+    meet(dealt + others)
+    rows, lanes = block(z // 2, 64), block(row, 512)
     for plane in range(PLANES):
-        mine = jnp.logical_and(row == z // 2, z == plane)
+        mine = jnp.logical_and(row == z % 2, z == plane)
 
         @pl.when(jnp.logical_not(mine))
         def _():
             push(
                 low.at[:, plane * 512 : plane * 512 + 512], atp.at[rows, lanes],
-                sz.at[plane], rz.at[row * 2 + z % 2], (z // 2, plane * QUAD + quarter),
+                sz.at[plane], rz.at[row * 2 + z // 2], (z % 2, plane * QUAD + quarter),
             ).start()
 
         @pl.when(mine)
         def _():
             atp[rows, lanes] = low[:, plane * 512 : plane * 512 + 512]
 
+    pieces = []
+    for bits in range(1, 16):
+        there = dealt[bits - 1]
+        pieces.append(push(cot.at[there[1]], cotr.at[col], sc.at[bits], rc.at[bits], there))
+        pieces[-1].start()
+    cotr[col] = cot[col]
     for j in range(4):
-        source = (j // 2, (2 * row + j % 2) * QUAD + quarter)
-        mine = jnp.logical_and(row == j // 2, z == 2 * row + j % 2)
+        source = (j // 2, (row + 2 * (j % 2)) * QUAD + quarter)
+        mine = jnp.logical_and(row == j // 2, z == row + 2 * (j % 2))
 
         @pl.when(jnp.logical_not(mine))
         def _():
@@ -1069,13 +1124,13 @@
             ).wait_recv()
 
     for plane in range(PLANES):
-        mine = jnp.logical_and(row == z // 2, z == plane)
+        mine = jnp.logical_and(row == z % 2, z == plane)
 
         @pl.when(jnp.logical_not(mine))
         def _():
             push(
                 low.at[:, plane * 512 : plane * 512 + 512], atp.at[rows, lanes],
-                sz.at[plane], rz.at[row * 2 + z % 2], (z // 2, plane * QUAD + quarter),
+                sz.at[plane], rz.at[row * 2 + z // 2], (z % 2, plane * QUAD + quarter),
             ).wait_send()
 
     atn[...] = jnp.transpose(atp[...])
@@ -1090,10 +1145,23 @@
         chip = flip(place // 2, bits)
         part[2 * chip + core] = mm(atn[block(2 * chip + core, 128), :], wop[...]).astype(bf16)
     total.far_all()
+    for copy in pieces:
+        copy.wait_recv()
+    for j in range(16):
+        cots[j * 8 : j * 8 + 8, :] = cotr[jnp.clip(deal[j], 0, 15)]
+    cot_in = Gather(cotp, sa, ra)
+    cot_in.start(cots)
+    cotp[place] = cots[...]
     state = x[...].astype(f32) + total.finish()
     hidden[...] = state
     s2[...] = (state * norm_scale(state) * gains[1:2, :]).astype(bf16)
+    cot_in.finish()
+    kept = fetch(cotp, cotp_out, keep.at[0])
+    for copy in pieces:
+        copy.wait_send()
     total.close()
+    cot_in.close()
+    kept.wait()
 
 
 def ffn_body(
@@ -1270,7 +1338,7 @@
             continue
         group = row if k == 1 else 1 - row
         for head in range(2):
-            plane = 2 * row + head
+            plane = row + 2 * head
             source = dat.at[head * 64 : head * 64 + 64, block(group, 512)]
             if k == 1:
 
@@ -1296,17 +1364,17 @@
         total = total + mm(atp[:, q * 128 : q * 128 + 128], dbp[q])
     gwo[...] = total.astype(bf16)
     for plane in range(PLANES):
-        mine = jnp.logical_and(row == z // 2, z == plane)
+        mine = jnp.logical_and(row == z % 2, z == plane)
 
         @pl.when(jnp.logical_not(mine))
         def _():
             push(
                 dat.at[0:64, 0:512], grad.at[:, plane * 512 : plane * 512 + 512], sz.at[0],
-                rz.at[plane], (z // 2, plane * QUAD + quarter),
+                rz.at[plane], (z % 2, plane * QUAD + quarter),
             ).wait_recv()
 
     for head in range(2):
-        plane = 2 * row + head
+        plane = row + 2 * head
 
         @pl.when(z != plane)
         def _():
@@ -1326,9 +1394,9 @@
 def last_body(
     dproj, wt_in, s1_in, xp_in, out_in, gains, d_hidden, hidden, gwo, gwg, gain_two, bias_tile, deal,
     grad_tokens, gqin, goin, gwg_in, sums, out,
-    wt, s1, xp, out_part, pieces, slots, keep, dpt, dpn, part, gq, gqcol, gqsum, pack, packs, packed,
+    wt, s1, xp, out_part, pieces, slots, keep, dpt, dpn, part, gq, gqcol, gqout, gqsum, pack, packs, packed,
     passed, sz, rz, inbox, outbox, second, ss, rs, sp,
-    sq, rq, sv, rv, st, rt, su, ru, sw, rw, sg, rg, sc, rc, inbox2, outbox2, second2, ss2, rs2,
+    sq, rq, sv, rv, st, rt, su, ru, sw, rw, sg, rg, sc, rc, passed2, sp2, inbox2, outbox2, second2, ss2, rs2,
 ):
     row, col, z, place = places()
     quarter = col % QUAD
@@ -1342,21 +1410,21 @@
         fetch(wt_in, wt, keep.at[2]),
     ]
     meet([anyone(row, col, bits) for bits in range(1, 32)])
-    copies = []
-    for plane in range(PLANES):
-        ours = pl.ds(pl.multiple_of(plane * 512 + y * 256, 256), 256)
-        theirs = pl.ds(pl.multiple_of(plane * 512 + (1 - y) * 256, 256), 256)
-        lanes = slice(plane * 256, plane * 256 + 256)
-        copy = push(
-            dproj.at[:, theirs], dpt.at[y, :, lanes], sz.at[plane], rz.at[plane], (row, flip(col, 2))
-        )
-        copy.start()
-        copies.append(copy)
-        dpt[y, :, lanes] = dproj[:, ours]
+    copies = {}
+    for bits in (3, 2, 1, 0):
+        chip = flip(z, bits)
+        ours = pl.ds(pl.multiple_of(chip * 512 + y * 256, 256), 256)
+        theirs = pl.ds(pl.multiple_of(chip * 512 + (1 - y) * 256, 256), 256)
+        copies[bits] = push(
+            dproj.at[:, theirs], dpt.at[y, :, block(chip, 256)], sz.at[bits], rz.at[bits],
+            (row, flip(col, 2)),
+        )
+        copies[bits].start()
+        dpt[y, :, block(chip, 256)] = dproj[:, ours]
     owner = core * 4 + y * 2
     for j in range(4):
-        there = (row, j // 2 * 8 + owner + j % 2)
-        mine = col == there[1]
+        there = (j // 2, row * 8 + owner + j % 2)
+        mine = jnp.logical_and(row == there[0], col == there[1])
 
         @pl.when(jnp.logical_not(mine))
         def _():
@@ -1367,9 +1435,9 @@
             goin[z] = gwo[j]
 
     loads[0].wait()
-    output = Scatter(out_part, inbox2, outbox2, second2, ss2, rs2)
+    output = RoundScatter(out_part, inbox2, outbox2, second2, ss2, rs2, passed2, sp2)
     output.near_all()
-    output.far_all()
+    output.far_first()
     spread = []
     for bits in range(1, 8):
         there = in_plane(row, col, bits)
@@ -1379,41 +1447,40 @@
     gwg_in[place] = gwg[place]
     for copy in loads[1:]:
         copy.wait()
-    for copy in copies:
-        copy.wait_recv()
-    for plane in range(PLANES):
-        lanes = slice(plane * 256, plane * 256 + 256)
+    total = LineScatter(part, inbox, outbox, second, ss, rs, passed, sp)
+    term = jnp.zeros((1, 1024), f32)
+    for bits in (3, 2, 1, 0):
+        chip = flip(z, bits)
+        lanes = block(chip, 256)
+        copies[bits].wait_recv()
         for kind in range(3):
             both = jnp.concatenate(
                 [dpt[head, kind * 64 : kind * 64 + 64, lanes] for head in range(2)], axis=0
             )
             dpn[lanes, kind * 128 : kind * 128 + 128] = jnp.transpose(both)
-    total = LineScatter(part, inbox, outbox, second, ss, rs, passed, sp)
-    term = jnp.zeros((1, 1024), f32)
-    for own in range(2):
-        for bits in (3, 2, 1, 0):
-            number = 2 * flip(z, bits) + (core if own else 1 - core)
-            values = xp[number].astype(f32)
-            d_scaled = mm(dpn[block(number, 128), :], wt[...])
-            term = term + jnp.sum(d_scaled * (values * norm_scale(values)), axis=0, keepdims=True)
-            part[number] = d_scaled.astype(bf16)
-        if own == 0:
-            for bits in range(4):
-                total.near(flip(z, bits), bits)
-    total.far_all()
+        d_scaled = mm(dpn[lanes, :], wt[...])
+        values = jnp.concatenate([xp[2 * chip], xp[2 * chip + 1]], axis=0).astype(f32)
+        term = term + jnp.sum(d_scaled * (values * norm_scale(values)), axis=0, keepdims=True)
+        part[2 * chip] = d_scaled[0:128].astype(bf16)
+        part[2 * chip + 1] = d_scaled[128:256].astype(bf16)
+        total.near(chip, bits)
+        if bits < 3:
+            total.far(bits + 1)
+    output.far_second()
     for f in range(8):
+        if f == 4:
+            total.far_second()
         lhs = jnp.concatenate([s1[t, :, f * 128 : f * 128 + 128] for t in range(MEMBERS)], axis=0)
         chunk = mm_tn(lhs, dpn[...]).astype(bf16)
         for j in range(4):
             gq[f // PLANES * 2 + j // 2, f % PLANES * 2 + j % 2] = chunk[j * 32 : j * 32 + 32, :]
-    columns = []
-    for bits in (3, 2, 1):
-        there = (flip(row, bits // 2), flip(col, bits % 2 * 2))
-        copy = push(
-            gq.at[flip(column, bits)], gqcol.at[bits - 1], sv.at[bits], rv.at[bits], there
-        )
+    beside, across = (row, flip(col, 2)), (flip(row, 1), col)
+    columns = [
+        push(gq.at[flip(column, 3)], gqcol.at[1], sv.at[3], rv.at[3], across),
+        push(gq.at[flip(column, 2)], gqcol.at[0], sv.at[2], rv.at[2], across),
+    ]
+    for copy in columns:
         copy.start()
-        columns.append(copy)
     for k in range(8):
         pack[k] = bias_tile[...]
         pack[k, 0:1, :] = term[:, k * 128 : k * 128 + 128]
@@ -1441,6 +1508,12 @@
         copy.start()
         spread.append(copy)
     out[col] = slots[col]
+    columns[0].wait_recv()
+    nearby = flip(column, 1)
+    for m in range(MEMBERS):
+        gqout[m] = (gq[nearby, m].astype(f32) + gqcol[1, m].astype(f32)).astype(bf16)
+    columns.append(push(gqout, gqcol.at[2], sv.at[1], rv.at[1], beside))
+    columns[2].start()
     for copy in first:
         copy.wait_recv()
     summed = packs[0]
@@ -1454,12 +1527,11 @@
         copy.start()
         spread.append(copy)
     sums[z] = packed[z]
-    for copy in columns:
+    for copy in columns[1:]:
         copy.wait_recv()
     for m in range(MEMBERS):
         gqsum[m] = (
-            (gq[column, m].astype(f32) + gqcol[0, m].astype(f32))
-            + (gqcol[1, m].astype(f32) + gqcol[2, m].astype(f32))
+            (gq[column, m].astype(f32) + gqcol[0, m].astype(f32)) + gqcol[2, m].astype(f32)
         ).astype(bf16)
     for bits in range(7, 0, -1):
         there = in_line(row, col, bits)
@@ -1477,23 +1549,24 @@
         copy.wait_recv()
     senders = col // 2 % 2 * 2 + col // 4 % 2
     for plane in range(PLANES):
-        mine = jnp.logical_and(quarter == senders, z == plane)
+        mine = jnp.logical_and(row * 16 + col == (col // 8) * 16 + plane * QUAD + senders, z == plane)
 
         @pl.when(jnp.logical_not(mine))
         def _():
             push(
-                gwo.at[0], goin.at[plane], sw.at[0], rw.at[plane], (row, plane * QUAD + senders)
+                gwo.at[0], goin.at[plane], sw.at[0], rw.at[plane],
+                (col // 8, plane * QUAD + senders),
             ).wait_recv()
 
     for j in range(4):
-        there = (row, j // 2 * 8 + owner + j % 2)
-        mine = col == there[1]
+        there = (j // 2, row * 8 + owner + j % 2)
+        mine = jnp.logical_and(row == there[0], col == there[1])
 
         @pl.when(jnp.logical_not(mine))
         def _():
             push(gwo.at[j], goin.at[z], sw.at[j], rw.at[z], there).wait_send()
 
-    for copy in copies + columns + first + spread:
+    for copy in list(copies.values()) + columns + first + spread:
         copy.wait_send()
     total.close()
     output.close()
@@ -1564,16 +1637,15 @@
     freq = jnp.asarray(np.exp(-math.log(10000.0) * np.arange(32) / 32).astype(np.float32)[:, None])
     target = deal[0, 0]
 
-    xp, wt, wop, wgp, cotp, s1, qkvt, gains, labels = kernel(
+    xp, wt, wop, wgp, s1, qkvt, gains, labels = kernel(
         enter_body,
         "enter",
-        [VM] * 9 + [SM, SM, VM],
+        [VM] * 8 + [SM, VM],
         [
             sds((8, rows, width), bf16),
             sds((384, 1024), bf16),
             sds((4, 32, 1024), bf16),
             sds((8, 32, 1024), bf16),
-            sds((8, rows, width), bf16),
             sds((8, rows, width), bf16),
             sds((192, 2048), bf16),
             sds((8, 1024), f32),
@@ -1582,14 +1654,11 @@
         [
             pltpu.VMEM((8, rows, width), bf16),
             pltpu.VMEM((8, rows, width), bf16),
-            pltpu.VMEM((8, rows, width), bf16),
             dma(4),
             pltpu.VMEM((8, 32, 384), bf16),
             pltpu.VMEM((8, 32, 384), bf16),
             pltpu.VMEM((4, 8, 32, 384), bf16),
             pltpu.VMEM((8, 32, 1024), bf16),
-            pltpu.VMEM((16, 8, width), bf16),
-            pltpu.VMEM((rows, width), bf16),
             pltpu.VMEM((8, 128), f32),
             pltpu.VMEM((4, 8, 128), f32),
             pltpu.VMEM((8, 4, 8, 128), f32),
@@ -1600,12 +1669,12 @@
             pltpu.VMEM((8, 1024), f32),
         ]
         + [dma(8), dma(8), dma(8), dma(8), dma(4), dma(4), dma(4), dma(4), dma(8), dma(8)]
-        + [dma(4), dma(4), dma(8), dma(8), dma(16), dma(16), dma(8), dma(8), dma(4), dma(4)],
+        + [dma(4), dma(4), dma(8), dma(8), dma(4), dma(4)],
         number=1,
-        places_out=[ANY, ANY, VM, VM, ANY, ANY, VM, VM, VM],
+        places_out=[ANY, ANY, VM, VM, ANY, VM, VM, VM],
     )(
-        tokens, w_qkv, w_out, w_gate_up, cotangent.reshape(16, 8, width), gain_attn[None],
-        gain_ffn[None], variate_ids[None], time_ids[None], lengths, target, freq,
+        tokens, w_qkv, w_out, w_gate_up, gain_attn[None], gain_ffn[None], variate_ids[None],
+        time_ids[None], lengths, freq,
     )
 
     gate_up = lax.all_gather(
@@ -1629,19 +1698,29 @@
         cost=2 * 10**9,
     )(var_bias, qkvt, labels)
 
-    atp, hidden, s2 = kernel(
+    atp, hidden, s2, cotp = kernel(
         branch_body,
         "branch",
-        [VM] * 4,
-        [sds((128, 1024), bf16), sds((rows, width), f32), sds((rows, width), bf16)],
+        [VM] * 5 + [SM],
         [
+            sds((128, 1024), bf16),
+            sds((rows, width), f32),
+            sds((rows, width), bf16),
+            sds((8, rows, width), bf16),
+        ],
+        [
+            pltpu.VMEM((8, rows, width), bf16),
+            pltpu.VMEM((16, 8, width), bf16),
+            pltpu.VMEM((rows, width), bf16),
+            dma(1),
             pltpu.VMEM((1024, 128), bf16),
             pltpu.VMEM((8, rows, width), bf16),
-            dma(4), dma(4),
+            dma(4), dma(4), dma(16), dma(16), dma(8), dma(8),
         ]
         + scatter_scratch(rows, width),
         number=2,
-    )(low, wop, tokens, gains)
+        places_out=[VM, VM, VM, ANY],
+    )(low, wop, tokens, gains, cotangent.reshape(16, 8, width), target)
 
     out_part, down_in, gwg, d_hidden, d_branch, gain_two = kernel(
         ffn_body,
@@ -1739,6 +1818,7 @@
             pltpu.VMEM((4, 8, 32, 384), bf16),
             pltpu.VMEM((3, 8, 32, 384), bf16),
             pltpu.VMEM((8, 32, 384), bf16),
+            pltpu.VMEM((8, 32, 384), bf16),
             pltpu.VMEM((8, 8, 128), f32),
             pltpu.VMEM((8, 4, 8, 128), f32),
             pltpu.VMEM((4, 8, 128), f32),
@@ -1748,6 +1828,7 @@
         + scatter_scratch(rows, width)
         + [dma(2), dma(8), dma(8), dma(4), dma(4), dma(8), dma(8), dma(4), dma(4)]
         + [dma(4), dma(4), dma(8), dma(8), dma(16), dma(16)]
+        + [pltpu.VMEM((rows, width), bf16), dma(2)]
         + scatter_scratch(rows, width),
         number=5,
     )(

time: 288 us -> 269 us (0.934)
  waiting for transfers between devices: 28.1 us -> 11.1 us
    all_gather x1, waiting for transfers between devices: 12.5 us -> 0.21 us  [plane_shards(): lax.all_gather(wgp.reshape(256, 1024), 'col', axis=0, tiled=True, axis_in...]
    pallas_call x1, Pallas kernels: 59.7 us -> 49.2 us  [plane_shards(): kernel(last_body, 'last', [VM] + [ANY] * 4 + [VM] * 7 + [SM], [sds((rows,...]
    reduce_scatter x1, waiting for transfers between devices: 15.6 us -> 10.8 us  [plane_shards(): lax.psum_scatter(gwg.reshape(1024, 1024), 'col', scatter_dimension=0, til...]
    pallas_call x1, Pallas kernels: 28.5 us -> 32.5 us  [plane_shards(): kernel(attended_back_body, 'attended_back', [VM] * 3, [sds((64, 2048), bf...]
  transfers between devices with their start and end apart: 2 -> 2, of which waited for: 2 -> 2; matrix products, arithmetic and copies ran while one was open for 0% -> 0% of each run, Pallas kernels for 27% -> 37%
where the time goes in v4:
time: 269 us; the launch traced here: 268 us
  Pallas kernels  242 us (90%)
  between operations  14.1 us (5%)
  waiting for transfers between devices  11.1 us (4%)
    pallas_call x1, Pallas kernels, plane_shards(): kernel(last_body, 'last', [VM] + [ANY] * 4 + [VM] * 7 + [SM], [sds((rows,...  49.2 us
    pallas_call x1, Pallas kernels, plane_shards(): kernel(branch_body, 'branch', [VM] * 5 + [SM], [sds((128, 1024), bf16), s...  48.3 us
    pallas_call x1, Pallas kernels, plane_shards(): kernel(ffn_body, 'ffn', [VM, ANY, ANY, VM, VM, VM], [sds((8, rows, width)...  47.4 us
    pallas_call x1, Pallas kernels, plane_shards(): kernel(enter_body, 'enter', [VM] * 8 + [SM, VM], [sds((8, rows, width), b...  41.5 us
    pallas_call x1, Pallas kernels, plane_shards(): kernel(attended_back_body, 'attended_back', [VM] * 3, [sds((64, 2048), bf...  32.5 us
    pallas_call x1, Pallas kernels, plane_shards(): kernel(attend_back_body, 'attend_back', [VM] * 8, [sds((192, 2048), bf16)...  11.7 us
    reduce_scatter x1, waiting for transfers between devices, plane_shards(): lax.psum_scatter(gwg.reshape(1024, 1024), 'col', scatter_dimension=0, til...  10.8 us
    pallas_call x1, Pallas kernels, plane_shards(): kernel(attend_body, 'attend', [SM, VM, VM], [sds((64, wide), f32), sds((8...  7.93 us
  transfers between devices with their start and end apart: 2, of which 2 were waited for; matrix products, arithmetic and copies ran while one was open for 0% of the time, Pallas kernels for 37%

profile of v4, /device:TPU:0, one launch (start us, length us, event | category | flops | bytes accessed | tf_op | source)
XLA Modules:
  0.0 268.3 jit_solution(527294007230379362)
XLA Ops:
  7.2 0.0 all-gather.2.cloned.1.call-start
  7.2 41.5 %enter.1 = (bf16[8,128,1024]{2,1,0:T(8,128)(2,1)}, bf16[384,1024]{1,0:T(8,128)(2,1)}, bf16[4,32,1024]{2,1,0:T(8,128)(2,1)}, bf16[8,32,1024]{2,1,0:T(8,128)(2,1)}...) custom-call(bf16[128,1024]{1,0:T(8,128)(2,1)} %x.3, ...), custom_call_target="tpu_custom_call" | custom-call | tf_op jit(solution)/shard_map/enter/pallas_call | solution.py:1640
  48.8 0.0 all-gather.2.cloned.1.call-update
  48.8 0.0 reduce-scatter.2.cloned.1.call-start
  48.9 7.9 %attend.1 = (f32[64,2560]{1,0:T(8,128)}, f32[8,2560]{1,0:T(8,128)}, bf16[64,2560]{1,0:T(8,128)(2,1)}, bf16[128,2560]{1,0:T(8,128)(2,1)}, bf16[2048,128]{1,0:T(8,128)(2,1)}) custom-call(f32[2,16]{1,0:T(2,128)} %bias_all.1, bf16[192,2048]{1,0:T(8,128)(2,1)} %get-tuple-element.50.qkvt, f32[8,2048]{1,0:T(8,128)} %get-tuple-element.51.labels), custom_call_target="tpu_custom_call" | custom-call | flops 2000000000 | bytes 6666666 | tf_op jit(solution)/shard_map/attend/pallas_call | solution.py:1686
  56.8 48.3 %branch.1 = (bf16[128,1024]{1,0:T(8,128)(2,1)}, f32[128,1024]{1,0:T(8,128)}, bf16[128,1024]{1,0:T(8,128)(2,1)}, bf16[8,128,1024]{2,1,0:T(8,128)(2,1)}) custom-call(bf16[64,2560]{1,0:T(8,128)(2,1)} %get-tuple-element.54.low, bf16[128,1024]{1,0:T(8,128)(2,1)} %bitcast.18, bf16[128,1024]{1,0:T(8,128)(2,1)} %x.3, f32[8,1024]{1,0:T(8,128)} %get-tuple-element.56.gains, ...), custom_call_target="tpu_custom_call" | custom-call | tf_op jit(solution)/shard_map/branch/pallas_call | solution.py:1701
  105.1 0.2 all-gather.2.cloned.1.call-done
  105.3 47.4 %ffn.1 = (bf16[8,128,1024]{2,1,0:T(8,128)(2,1)}, bf16[4,128,1024]{2,1,0:T(8,128)(2,1)}, bf16[8,128,1024]{2,1,0:T(8,128)(2,1)}, f32[128,1024]{1,0:T(8,128)}, bf16...) custom-call(bf16[128,1024]{1,0:T(8,128)(2,1)} %get-tuple-element.57.s2, bf16[8,128,1024]{2,1,0:T(8,128)(2,1)} %get-tuple-element.58.cotp_in, ...), custom_call_target="tpu_custom_call" | custom-call | flops 10000000000 | bytes 33333332 | tf_op jit(solution)/shard_map/ffn/pallas_call | solution.py:1725
  152.7 0.0 reduce-scatter.2.cloned.1.call-update
  152.7 32.5 %attended_back.1 = (bf16[64,2048]{1,0:T(8,128)(2,1)}, bf16[128,1024]{1,0:T(8,128)(2,1)}) custom-call(bf16[128,1024]{1,0:T(8,128)(2,1)} %get-tuple-element.61.low, bf16[128,1024]{1,0:T(8,128)(2,1)} %bitcast.19, bf16[128,1024]{1,0:T(8,128)(2,1)} %get-tuple-element.62.atp), custom_call_target="tpu_custom_call" | custom-call | tf_op jit(solution)/shard_map/attended_back/pallas_call | solution.py:1765
  185.2 11.7 %attend_back.1 = (bf16[192,2048]{1,0:T(8,128)(2,1)}, f32[8,128]{1,0:T(8,128)}) custom-call(bf16[192,2048]{1,0:T(8,128)(2,1)} %get-tuple-element.50.qkvt, bf16[128,2560]{1,0:T(8,128)(2,1)} %get-tuple-element.52.qa, bf16[2048,128]{1,0:T(8,128)(2,1)} %get-tuple-element.53.ka, f32[8,2048]{1,0:T(8,128)} %get-tuple-element.51.labels, f32[32,1]{1,0:T(8,128)} %constant.2.clone.freq, ...), custom_call_target="tpu_custom_call" | custom-call | flops 5000000000 | bytes 16666666 | tf_op jit(solution)/shard_map/attend_back/pallas_call | solution.py:1778
  196.9 10.8 %reduce-scatter.2.cloned.1.call-done = bf16[256,1024]{1,0:T(8,128)(2,1)} async-done(((bf16[1024,1024]{1,0:T(8,128)(2,1)}), bf16[256,1024]{1,0:T(8,128)(2,1)}) %reduce-scatter.2.cloned.1.call-update) | async-done | bytes 524304 | tf_op jit(solution)/shard_map/reduce_scatter | solution.py:1761
  207.7 49.2 %last.1 = (bf16[128,1024]{1,0:T(8,128)(2,1)}, bf16[8,32,384]{2,1,0:T(8,128)(2,1)}, bf16[4,32,1024]{2,1,0:T(8,128)(2,1)}, bf16[8,32,1024]{2,1,0:T(8,128)(2,1)}, f...) custom-call(bf16[192,2048]{1,0:T(8,128)(2,1)} %get-tuple-element.66.dproj, bf16[384,1024]{1,0:T(8,128)(2,1)} %get-tuple-element.67.wt_in, ...), custom_call_target="tpu_custom_call" | custom-call | tf_op jit(solution)/shard_map/last/pallas_call | solution.py:1795
  256.9 3.2 %finish.1 = (bf16[128,1024]{1,0:T(8,128)(2,1)}, bf16[128,1024]{1,0:T(8,128)(2,1)}, f32[32,3072]{1,0:T(8,128)}, f32[32,1024]{1,0:T(8,128)}, f32[32,8192]{1,0:T(8,...) custom-call(bf16[128,1024]{1,0:T(8,128)(2,1)} %get-tuple-element.76.grad_tokens_in, ...), custom_call_target="tpu_custom_call" | custom-call | tf_op jit(solution)/shard_map/finish/pallas_call | solution.py:1838
  260.2 1.3 slice_bitcast_fusion
Async XLA Ops:
  7.2 98.1 %all-gather.2.cloned.1.call-start = ((), (), s32[]{:S(2)}) async-start(), calls=%async_computation.1 | async-start | bytes 2621440 | tf_op jit(solution)/shard_map/all_gather | solution.py:1680
  48.8 158.9 %reduce-scatter.2.cloned.1.call-start = ((), (), s32[]{:S(2)}) async-start(), calls=%async_computation.2 | async-start | bytes 2621440 | tf_op jit(solution)/shard_map/reduce_scatter | solution.py:1761
Sparse Core Ops, SparseCore 0:
  48.9 56.3 all-gather.1
  152.8 54.8 reduce-scatter.1

commit v5 on v4

--- a/solution.py
+++ b/solution.py
@@ -718,10 +718,10 @@
 
 
 def enter_body(
-    x, wq, wo, wg, ga, gf, variate, time, lengths, freq,
-    xp_out, wt_out, wop, wgp, s1_out, qkvt, gains, labels,
-    xp, s1, keep, wqs, wline, wqp, wgs, tile, tl, tiles, wt, box, cs, sn, times,
-    sx, rx, sq, rq, sv, rv, st, rt, su, ru, sw, rw, sg, rg, sz, rz,
+    x, wq, wo, wg, cot, ga, gf, variate, time, lengths, deal, freq,
+    xp_out, wt_out, wop, wgp, s1_out, qkvt, gains, labels, cots,
+    cotr, xp, s1, keep, wqs, wline, wqp, wgs, tile, tl, tiles, wt, box, cs, sn, times,
+    sx, rx, sq, rq, sv, rv, st, rt, su, ru, sw, rw, sg, rg, sz, rz, sc, rc,
 ):
     row, col, z, place = places()
     quarter = col % QUAD
@@ -840,6 +840,12 @@
             at = 256 + head * 64
             box[head, 128:192, rows] = out[at : at + 64].astype(bf16)
 
+    pieces = []
+    for bits in range(1, 16):
+        there = (row, flip(col, bits))
+        pieces.append(push(cot.at[there[1]], cotr.at[col], sc.at[bits], rc.at[bits], there))
+        pieces[-1].start()
+    cotr[col] = cot[col]
     turned = []
 
     def exchange(chip, number):
@@ -899,10 +905,14 @@
         def _():
             push(wo, wop.at[slot], sw.at[plane], rw.at[slot], there).wait_send()
 
+    for copy in pieces:
+        copy.wait_recv()
+    for j in range(16):
+        cots[j * 8 : j * 8 + 8, :] = cotr[jnp.clip(deal[j], 0, 15)]
     for copy in turned:
         copy.wait()
     rows_in.close()
-    for copy in first + second + blocks + ways:
+    for copy in first + second + blocks + ways + pieces:
         copy.wait_send()
     for copy in kept:
         copy.wait()
@@ -1083,15 +1093,13 @@
 
 
 def branch_body(
-    low, wop, x, gains, cot, deal,
+    low, wop, x, gains, cots,
     atp, hidden, s2, cotp_out,
-    cotp, cotr, cots, keep, atn, part, sz, rz, sc, rc, sa, ra, inbox, outbox, second, ss, rs,
+    cotp, keep, atn, part, sz, rz, sa, ra, inbox, outbox, second, ss, rs,
 ):
     row, col, z, place = places()
     quarter = col % QUAD
-    dealt = [(row, flip(col, bits)) for bits in range(1, 16)]
-    others = [(flip(row, 1), flip(col, bits)) for bits in (0, 2, 4, 8, 12)]
-    meet(dealt + others)
+    meet(plane_near(row, col) + column_all(row, col))
     rows, lanes = block(z // 2, 64), block(row, 512)
     for plane in range(PLANES):
         mine = jnp.logical_and(row == z % 2, z == plane)
@@ -1107,12 +1115,9 @@
         def _():
             atp[rows, lanes] = low[:, plane * 512 : plane * 512 + 512]
 
-    pieces = []
-    for bits in range(1, 16):
-        there = dealt[bits - 1]
-        pieces.append(push(cot.at[there[1]], cotr.at[col], sc.at[bits], rc.at[bits], there))
-        pieces[-1].start()
-    cotr[col] = cot[col]
+    cot_in = Gather(cotp, sa, ra)
+    cot_in.start(cots)
+    cotp[place] = cots[...]
     for j in range(4):
         source = (j // 2, (row + 2 * (j % 2)) * QUAD + quarter)
         mine = jnp.logical_and(row == j // 2, z == row + 2 * (j % 2))
@@ -1145,20 +1150,11 @@
         chip = flip(place // 2, bits)
         part[2 * chip + core] = mm(atn[block(2 * chip + core, 128), :], wop[...]).astype(bf16)
     total.far_all()
-    for copy in pieces:
-        copy.wait_recv()
-    for j in range(16):
-        cots[j * 8 : j * 8 + 8, :] = cotr[jnp.clip(deal[j], 0, 15)]
-    cot_in = Gather(cotp, sa, ra)
-    cot_in.start(cots)
-    cotp[place] = cots[...]
+    cot_in.finish()
+    kept = fetch(cotp, cotp_out, keep.at[0])
     state = x[...].astype(f32) + total.finish()
     hidden[...] = state
     s2[...] = (state * norm_scale(state) * gains[1:2, :]).astype(bf16)
-    cot_in.finish()
-    kept = fetch(cotp, cotp_out, keep.at[0])
-    for copy in pieces:
-        copy.wait_send()
     total.close()
     cot_in.close()
     kept.wait()
@@ -1637,10 +1633,10 @@
     freq = jnp.asarray(np.exp(-math.log(10000.0) * np.arange(32) / 32).astype(np.float32)[:, None])
     target = deal[0, 0]
 
-    xp, wt, wop, wgp, s1, qkvt, gains, labels = kernel(
+    xp, wt, wop, wgp, s1, qkvt, gains, labels, cot = kernel(
         enter_body,
         "enter",
-        [VM] * 8 + [SM, VM],
+        [VM] * 9 + [SM, SM, VM],
         [
             sds((8, rows, width), bf16),
             sds((384, 1024), bf16),
@@ -1650,8 +1646,10 @@
             sds((192, 2048), bf16),
             sds((8, 1024), f32),
             sds((8, 2048), f32),
+            sds((rows, width), bf16),
         ],
         [
+            pltpu.VMEM((16, 8, width), bf16),
             pltpu.VMEM((8, rows, width), bf16),
             pltpu.VMEM((8, rows, width), bf16),
             dma(4),
@@ -1669,12 +1667,12 @@
             pltpu.VMEM((8, 1024), f32),
         ]
         + [dma(8), dma(8), dma(8), dma(8), dma(4), dma(4), dma(4), dma(4), dma(8), dma(8)]
-        + [dma(4), dma(4), dma(8), dma(8), dma(4), dma(4)],
+        + [dma(4), dma(4), dma(8), dma(8), dma(4), dma(4), dma(16), dma(16)],
         number=1,
-        places_out=[ANY, ANY, VM, VM, ANY, VM, VM, VM],
+        places_out=[ANY, ANY, VM, VM, ANY, VM, VM, VM, VM],
     )(
-        tokens, w_qkv, w_out, w_gate_up, gain_attn[None], gain_ffn[None], variate_ids[None],
-        time_ids[None], lengths, freq,
+        tokens, w_qkv, w_out, w_gate_up, cotangent.reshape(16, 8, width), gain_attn[None],
+        gain_ffn[None], variate_ids[None], time_ids[None], lengths, target, freq,
     )
 
     gate_up = lax.all_gather(
@@ -1701,7 +1699,7 @@
     atp, hidden, s2, cotp = kernel(
         branch_body,
         "branch",
-        [VM] * 5 + [SM],
+        [VM] * 5,
         [
             sds((128, 1024), bf16),
             sds((rows, width), f32),
@@ -1710,17 +1708,15 @@
         ],
         [
             pltpu.VMEM((8, rows, width), bf16),
-            pltpu.VMEM((16, 8, width), bf16),
-            pltpu.VMEM((rows, width), bf16),
             dma(1),
             pltpu.VMEM((1024, 128), bf16),
             pltpu.VMEM((8, rows, width), bf16),
-            dma(4), dma(4), dma(16), dma(16), dma(8), dma(8),
+            dma(4), dma(4), dma(8), dma(8),
         ]
         + scatter_scratch(rows, width),
         number=2,
         places_out=[VM, VM, VM, ANY],
-    )(low, wop, tokens, gains, cotangent.reshape(16, 8, width), target)
+    )(low, wop, tokens, gains, cot)
 
     out_part, down_in, gwg, d_hidden, d_branch, gain_two = kernel(
         ffn_body,

time: 269 us -> 264 us (0.981)
  Pallas kernels: 242 us -> 226 us
  waiting for transfers between devices: 11.1 us -> 21.9 us
    pallas_call x2, Pallas kernels: 89.8 us -> 79.4 us  [the longest x1 44.5 us: plane_shards(): kernel(enter_body, 'enter', [VM] * 9 + [SM, SM, VM], [sds((8, rows, width...]
    all_gather x1, waiting for transfers between devices: 0.21 us -> 9.63 us  [plane_shards(): lax.all_gather(wgp.reshape(256, 1024), 'col', axis=0, tiled=True, axis_in...]
  transfers between devices with their start and end apart: 2 -> 2, of which waited for: 2 -> 2; matrix products, arithmetic and copies ran while one was open for 0% -> 0% of each run, Pallas kernels for 37% -> 32%
where the time goes in v5:
time: 264 us
  Pallas kernels  226 us (86%)
  waiting for transfers between devices  21.9 us (8%)
  between operations  14.1 us (5%)
    pallas_call x1, Pallas kernels, plane_shards(): kernel(last_body, 'last', [VM] + [ANY] * 4 + [VM] * 7 + [SM], [sds((rows,...  49.4 us
    pallas_call x1, Pallas kernels, plane_shards(): kernel(ffn_body, 'ffn', [VM, ANY, ANY, VM, VM, VM], [sds((8, rows, width)...  44.9 us
    pallas_call x1, Pallas kernels, plane_shards(): kernel(enter_body, 'enter', [VM] * 9 + [SM, SM, VM], [sds((8, rows, width...  44.5 us
    pallas_call x1, Pallas kernels, plane_shards(): kernel(branch_body, 'branch', [VM] * 5, [sds((128, 1024), bf16), sds((row...  34.9 us
    pallas_call x1, Pallas kernels, plane_shards(): kernel(attended_back_body, 'attended_back', [VM] * 3, [sds((64, 2048), bf...  30.5 us
    reduce_scatter x1, waiting for transfers between devices, plane_shards(): lax.psum_scatter(gwg.reshape(1024, 1024), 'col', scatter_dimension=0, til...  12.2 us
    pallas_call x1, Pallas kernels, plane_shards(): kernel(attend_back_body, 'attend_back', [VM] * 8, [sds((192, 2048), bf16)...  11.4 us
    all_gather x1, waiting for transfers between devices, plane_shards(): lax.all_gather(wgp.reshape(256, 1024), 'col', axis=0, tiled=True, axis_in...  9.63 us
  transfers between devices with their start and end apart: 2, of which 2 were waited for; matrix products, arithmetic and copies ran while one was open for 0% of the time, Pallas kernels for 32%

profile of v5, /device:TPU:0, one launch (start us, length us, event | category | flops | bytes accessed | tf_op | source)
XLA Modules:
  0.0 263.8 jit_solution(13953274708469058937)
XLA Ops:
  7.2 0.0 all-gather.2.cloned.1.call-start
  7.2 44.5 %enter.1 = (bf16[8,128,1024]{2,1,0:T(8,128)(2,1)}, bf16[384,1024]{1,0:T(8,128)(2,1)}, bf16[4,32,1024]{2,1,0:T(8,128)(2,1)}, bf16[8,32,1024]{2,1,0:T(8,128)(2,1)}...) custom-call(bf16[128,1024]{1,0:T(8,128)(2,1)} %x.3, ...), custom_call_target="tpu_custom_call" | custom-call | tf_op jit(solution)/shard_map/enter/pallas_call | solution.py:1636
  51.8 0.0 all-gather.2.cloned.1.call-update
  51.8 0.0 reduce-scatter.2.cloned.1.call-start
  51.8 7.6 %attend.1 = (f32[64,2560]{1,0:T(8,128)}, f32[8,2560]{1,0:T(8,128)}, bf16[64,2560]{1,0:T(8,128)(2,1)}, bf16[128,2560]{1,0:T(8,128)(2,1)}, bf16[2048,128]{1,0:T(8,128)(2,1)}) custom-call(f32[2,16]{1,0:T(2,128)} %bias_all.1, bf16[192,2048]{1,0:T(8,128)(2,1)} %get-tuple-element.51.qkvt, f32[8,2048]{1,0:T(8,128)} %get-tuple-element.52.labels), custom_call_target="tpu_custom_call" | custom-call | flops 2000000000 | bytes 6666666 | tf_op jit(solution)/shard_map/attend/pallas_call | solution.py:1684
  59.5 34.9 %branch.1 = (bf16[128,1024]{1,0:T(8,128)(2,1)}, f32[128,1024]{1,0:T(8,128)}, bf16[128,1024]{1,0:T(8,128)(2,1)}, bf16[8,128,1024]{2,1,0:T(8,128)(2,1)}) custom-call(bf16[64,2560]{1,0:T(8,128)(2,1)} %get-tuple-element.55.low, bf16[128,1024]{1,0:T(8,128)(2,1)} %bitcast.18, bf16[128,1024]{1,0:T(8,128)(2,1)} %x.3, f32[8,1024]{1,0:T(8,128)} %get-tuple-element.57.gains, ...), custom_call_target="tpu_custom_call" | custom-call | tf_op jit(solution)/shard_map/branch/pallas_call | solution.py:1699
  94.4 9.6 %all-gather.2.cloned.1.call-done = bf16[1024,1024]{1,0:T(8,128)(2,1)} async-done(((bf16[256,1024]{1,0:T(8,128)(2,1)}), bf16[1024,1024]{1,0:T(8,128)(2,1)}) %all-gather.2.cloned.1.call-update) | async-done | bytes 2097168 | tf_op jit(solution)/shard_map/all_gather | solution.py:1678
  104.0 44.9 %ffn.1 = (bf16[8,128,1024]{2,1,0:T(8,128)(2,1)}, bf16[4,128,1024]{2,1,0:T(8,128)(2,1)}, bf16[8,128,1024]{2,1,0:T(8,128)(2,1)}, f32[128,1024]{1,0:T(8,128)}, bf16...) custom-call(bf16[128,1024]{1,0:T(8,128)(2,1)} %get-tuple-element.59.s2, bf16[8,128,1024]{2,1,0:T(8,128)(2,1)} %get-tuple-element.60.cotp_in, ...), custom_call_target="tpu_custom_call" | custom-call | flops 10000000000 | bytes 33333332 | tf_op jit(solution)/shard_map/ffn/pallas_call | solution.py:1721
  148.9 0.0 reduce-scatter.2.cloned.1.call-update
  148.9 30.5 %attended_back.1 = (bf16[64,2048]{1,0:T(8,128)(2,1)}, bf16[128,1024]{1,0:T(8,128)(2,1)}) custom-call(bf16[128,1024]{1,0:T(8,128)(2,1)} %get-tuple-element.63.low, bf16[128,1024]{1,0:T(8,128)(2,1)} %bitcast.19, bf16[128,1024]{1,0:T(8,128)(2,1)} %get-tuple-element.64.atp), custom_call_target="tpu_custom_call" | custom-call | tf_op jit(solution)/shard_map/attended_back/pallas_call | solution.py:1761
  179.4 11.4 %attend_back.1 = (bf16[192,2048]{1,0:T(8,128)(2,1)}, f32[8,128]{1,0:T(8,128)}) custom-call(bf16[192,2048]{1,0:T(8,128)(2,1)} %get-tuple-element.51.qkvt, bf16[128,2560]{1,0:T(8,128)(2,1)} %get-tuple-element.53.qa, bf16[2048,128]{1,0:T(8,128)(2,1)} %get-tuple-element.54.ka, f32[8,2048]{1,0:T(8,128)} %get-tuple-element.52.labels, f32[32,1]{1,0:T(8,128)} %constant.2.clone.freq, ...), custom_call_target="tpu_custom_call" | custom-call | flops 5000000000 | bytes 16666666 | tf_op jit(solution)/shard_map/attend_back/pallas_call | solution.py:1774
  190.8 12.2 %reduce-scatter.2.cloned.1.call-done = bf16[256,1024]{1,0:T(8,128)(2,1)} async-done(((bf16[1024,1024]{1,0:T(8,128)(2,1)}), bf16[256,1024]{1,0:T(8,128)(2,1)}) %reduce-scatter.2.cloned.1.call-update) | async-done | bytes 524304 | tf_op jit(solution)/shard_map/reduce_scatter | solution.py:1757
  203.0 49.4 %last.1 = (bf16[128,1024]{1,0:T(8,128)(2,1)}, bf16[8,32,384]{2,1,0:T(8,128)(2,1)}, bf16[4,32,1024]{2,1,0:T(8,128)(2,1)}, bf16[8,32,1024]{2,1,0:T(8,128)(2,1)}, f...) custom-call(bf16[192,2048]{1,0:T(8,128)(2,1)} %get-tuple-element.68.dproj, bf16[384,1024]{1,0:T(8,128)(2,1)} %get-tuple-element.69.wt_in, ...), custom_call_target="tpu_custom_call" | custom-call | tf_op jit(solution)/shard_map/last/pallas_call | solution.py:1791
  252.4 3.2 %finish.1 = (bf16[128,1024]{1,0:T(8,128)(2,1)}, bf16[128,1024]{1,0:T(8,128)(2,1)}, f32[32,3072]{1,0:T(8,128)}, f32[32,1024]{1,0:T(8,128)}, f32[32,8192]{1,0:T(8,...) custom-call(bf16[128,1024]{1,0:T(8,128)(2,1)} %get-tuple-element.78.grad_tokens_in, ...), custom_call_target="tpu_custom_call" | custom-call | tf_op jit(solution)/shard_map/finish/pallas_call | solution.py:1834
  255.7 1.3 slice_bitcast_fusion
Async XLA Ops:
  7.2 96.8 %all-gather.2.cloned.1.call-start = ((), (), s32[]{:S(2)}) async-start(), calls=%async_computation.1 | async-start | bytes 2621440 | tf_op jit(solution)/shard_map/all_gather | solution.py:1678
  51.8 151.2 %reduce-scatter.2.cloned.1.call-start = ((), (), s32[]{:S(2)}) async-start(), calls=%async_computation.2 | async-start | bytes 2621440 | tf_op jit(solution)/shard_map/reduce_scatter | solution.py:1757
Sparse Core Ops, SparseCore 0:
  51.9 52.0 all-gather.1
  149.0 53.8 reduce-scatter.1

commit v6 on v5

--- a/solution.py
+++ b/solution.py
@@ -384,7 +384,7 @@
     )
 
 
-def meet(devices):
+def greet(devices):
     barrier = pltpu.get_barrier_semaphore()
     for device in devices:
         pl.semaphore_signal(
@@ -393,7 +393,11 @@
             device_id={"row": device[0], "col": device[1]},
             device_id_type=pl.DeviceIdType.MESH,
         )
-    pl.semaphore_wait(barrier, len(devices))
+    return len(devices)
+
+
+def wait_for(number):
+    pl.semaphore_wait(pltpu.get_barrier_semaphore(), number)
 
 
 NEAR = (2, 4, 6, 1)
@@ -562,56 +566,6 @@
             copy.wait_send()
 
 
-class RoundScatter(Scatter):
-    def __init__(self, part, inbox, outbox, second, send, recv, passed, sems):
-        super().__init__(part, inbox, outbox, second, send, recv)
-        self.passed, self.sems = passed, sems
-
-    def sum_for(self, bits):
-        self.copies[bits].wait_recv()
-        chip = flip(self.place // 2, bits)
-        return self.part[2 * chip + self.core].astype(f32) + self.inbox[bits].astype(f32)
-
-    def far_first(self):
-        self.outbox[2] = self.sum_for(3).astype(bf16)
-        across = in_plane(self.row, self.col, 4)
-        self.passing = push(
-            self.outbox.at[2], self.passed, self.sems.at[0], self.sems.at[1], across
-        )
-        self.passing.start()
-        self.outbox[1] = self.sum_for(2).astype(bf16)
-        self.sent.append(
-            push(self.outbox.at[1], self.second.at[1], self.send.at[5], self.recv.at[5], across)
-        )
-        self.sent[0].start()
-
-    def far_second(self):
-        total = self.sum_for(1)
-        self.passing.wait_recv()
-        self.outbox[0] = (total + self.passed[...].astype(f32)).astype(bf16)
-        self.sent.append(
-            push(
-                self.outbox.at[0],
-                self.second.at[0],
-                self.send.at[4],
-                self.recv.at[4],
-                in_plane(self.row, self.col, 2),
-            )
-        )
-        self.sent[1].start()
-
-    def finish(self):
-        self.copies[0].wait_recv()
-        total = self.part[self.place].astype(f32) + self.inbox[0].astype(f32)
-        for copy in self.sent:
-            copy.wait_recv()
-        return total + (self.second[0].astype(f32) + self.second[1].astype(f32))
-
-    def close(self):
-        super().close()
-        self.passing.wait_send()
-
-
 class LineScatter(Scatter):
     def __init__(self, part, inbox, outbox, second, send, recv, passed, sems):
         row, col, z, _ = places()
@@ -727,6 +681,7 @@
     quarter = col % QUAD
     y, core = col // 2 % 2, col % 2
     member = z * 2 + core
+    present = greet([anyone(row, col, bits) for bits in range(1, 32)])
     lane = lax.broadcasted_iota(jnp.int32, (1, 128), 1)
     for line, gain in ((0, ga), (1, gf)):
         wide = gain[...].astype(f32)
@@ -743,7 +698,17 @@
         for part in range(3):
             at = part * 1024 + p * 128
             wqs[p, :, part * 128 : part * 128 + 128] = wq[:, at : at + 128]
-    meet([anyone(row, col, bits) for bits in range(1, 32)])
+    for p in range(MEMBERS):
+        for half in range(2):
+            for plane in range(PLANES):
+                unit = (p // QUAD) * 16 + plane * QUAD + p % QUAD
+                at = half * 512 + plane * 128
+                start = half * 4096 + unit * 128
+                wgs[p, :, at : at + 128] = wg[:, start : start + 128]
+    xp[member] = x[...]
+    wline[member] = wqs[member]
+    tl[z] = tile[...]
+    wait_for(present)
     first = []
     for bits in range(1, 8):
         there = in_line(row, col, bits)
@@ -753,16 +718,6 @@
         first.append(push(tile, tl.at[z], st.at[bits], rt.at[bits], on_line(row, col, bits)))
         first[-1].start()
     rows_in = LineGather(xp, sx, rx)
-    xp[member] = x[...]
-    wline[member] = wqs[member]
-    tl[z] = tile[...]
-    for p in range(MEMBERS):
-        for half in range(2):
-            for plane in range(PLANES):
-                unit = (p // QUAD) * 16 + plane * QUAD + p % QUAD
-                at = half * 512 + plane * 128
-                start = half * 4096 + unit * 128
-                wgs[p, :, at : at + 128] = wg[:, start : start + 128]
     blocks = []
     for bits in range(1, 8):
         there = in_plane(row, col, bits)
@@ -1099,8 +1054,10 @@
 ):
     row, col, z, place = places()
     quarter = col % QUAD
-    meet(plane_near(row, col) + column_all(row, col))
+    present = greet(plane_near(row, col) + column_all(row, col))
     rows, lanes = block(z // 2, 64), block(row, 512)
+    cotp[place] = cots[...]
+    wait_for(present)
     for plane in range(PLANES):
         mine = jnp.logical_and(row == z % 2, z == plane)
 
@@ -1117,7 +1074,6 @@
 
     cot_in = Gather(cotp, sa, ra)
     cot_in.start(cots)
-    cotp[place] = cots[...]
     for j in range(4):
         source = (j // 2, (row + 2 * (j % 2)) * QUAD + quarter)
         mine = jnp.logical_and(row == j // 2, z == row + 2 * (j % 2))
@@ -1168,33 +1124,34 @@
 ):
     row, col, z, place = places()
     loads = [fetch(wg_in, wg, keep.at[0]), fetch(cotp_in, cotp, keep.at[1])]
-    meet(plane_near(row, col) + line_all(row, col))
-    rows_in = Gather(s2p, sa, ra)
-    rows_in.start(s2)
+    present = greet(plane_near(row, col) + line_all(row, col))
     s2p[place] = s2[...]
-    inner = jnp.logical_or(z == 1, z == 2)
-    end = jnp.logical_not(inner)
-    downs = {
-        bits: push(
-            w_down, wd.at[block(z, 128), :], sw.at[bits], rw.at[bits], on_line(row, col, bits)
-        )
-        for bits in (2, 1, 3)
-    }
-    passed = wd.at[block(flip(z, 2), 128), :]
-    downs[0] = push(passed, passed, sw.at[0], rw.at[3], on_line(row, col, 1))
-    downs[2].start()
-
-    @pl.when(inner)
-    def _():
-        downs[3].start()
-
-    downs[1].start()
     wd[block(z, 128), :] = w_down[...]
     loads[0].wait()
     for plane in range(PLANES):
         for r in range(2):
             at = (r * PLANES + plane) * 128
             wgs[at : at + 128, :] = wg[plane * 2 + r]
+    wait_for(present)
+    rows_in = Gather(s2p, sa, ra)
+    rows_in.start(s2)
+    inner = jnp.logical_or(z == 1, z == 2)
+    end = jnp.logical_not(inner)
+    downs = {
+        bits: push(
+            w_down, wd.at[block(z, 128), :], sw.at[bits], rw.at[bits], on_line(row, col, bits)
+        )
+        for bits in (2, 1, 3)
+    }
+    passed = wd.at[block(flip(z, 2), 128), :]
+    downs[0] = push(passed, passed, sw.at[0], rw.at[3], on_line(row, col, 1))
+    downs[2].start()
+
+    @pl.when(inner)
+    def _():
+        downs[3].start()
+
+    downs[1].start()
     for k in range(4):
         chip = flip(place // 2, k)
         if k:
@@ -1313,16 +1270,21 @@
 
 
 def attended_back_body(
-    low, wop, atp,
-    grad, gwo,
-    dbp, dat, sg, rg, sz, rz,
+    low, wop, atp, out_in, hidden,
+    grad, gwo, rows_out,
+    out_part, keep, dbp, dat, sg, rg, sz, rz, inbox, outbox, second, ss, rs,
 ):
     row, col, z, place = places()
-    meet(plane_near(row, col) + column_all(row, col))
+    load = fetch(out_in, out_part, keep.at[0])
+    present = greet(plane_near(row, col) + column_all(row, col))
+    dbp[place] = low[...]
+    wait_for(present)
     quarter = col % QUAD
     rows_in = Gather(dbp, sg, rg)
     rows_in.start(low)
-    dbp[place] = low[...]
+    load.wait()
+    output = Scatter(out_part, inbox, outbox, second, ss, rs)
+    output.near_all()
     for k in range(4):
         chip = flip(place // 2, k)
         if k:
@@ -1355,10 +1317,13 @@
                     (group, plane * QUAD + quarter),
                 ).start()
 
+    output.far_all()
     total = mm(atp[:, 0:128], dbp[0])
     for q in range(1, MEMBERS):
         total = total + mm(atp[:, q * 128 : q * 128 + 128], dbp[q])
     gwo[...] = total.astype(bf16)
+    rows_out[...] = (hidden[...] + output.finish()).astype(bf16)
+    output.close()
     for plane in range(PLANES):
         mine = jnp.logical_and(row == z % 2, z == plane)
 
@@ -1388,11 +1353,11 @@
 
 
 def last_body(
-    dproj, wt_in, s1_in, xp_in, out_in, gains, d_hidden, hidden, gwo, gwg, gain_two, bias_tile, deal,
+    dproj, wt_in, s1_in, xp_in, gains, d_hidden, rows_out, gwo, gwg, gain_two, bias_tile, deal,
     grad_tokens, gqin, goin, gwg_in, sums, out,
-    wt, s1, xp, out_part, pieces, slots, keep, dpt, dpn, part, gq, gqcol, gqout, gqsum, pack, packs, packed,
+    wt, s1, xp, pieces, slots, keep, dpt, dpn, part, gq, gqcol, gqsum, pack, packs, packed,
     passed, sz, rz, inbox, outbox, second, ss, rs, sp,
-    sq, rq, sv, rv, st, rt, su, ru, sw, rw, sg, rg, sc, rc, passed2, sp2, inbox2, outbox2, second2, ss2, rs2,
+    sq, rq, sv, rv, st, rt, su, ru, sw, rw, sg, rg, sc, rc,
 ):
     row, col, z, place = places()
     quarter = col % QUAD
@@ -1400,12 +1365,21 @@
     member = z * 2 + core
     column = row * 2 + y
     loads = [
-        fetch(out_in, out_part, keep.at[3]),
         fetch(s1_in, s1, keep.at[0]),
         fetch(xp_in, xp, keep.at[1]),
         fetch(wt_in, wt, keep.at[2]),
     ]
-    meet([anyone(row, col, bits) for bits in range(1, 32)])
+    present = greet([anyone(row, col, bits) for bits in range(1, 32)])
+    for j in range(16):
+        pieces[j] = rows_out[j * 8 : j * 8 + 8, :]
+    for d in range(16):
+        number = 0
+        for j in range(1, 16):
+            number = jnp.where(deal[j] == d, j, number)
+        slots[d] = pieces[number]
+    gwg_in[place] = gwg[place]
+    out[col] = slots[col]
+    wait_for(present)
     copies = {}
     for bits in (3, 2, 1, 0):
         chip = flip(z, bits)
@@ -1430,18 +1404,13 @@
         def _():
             goin[z] = gwo[j]
 
-    loads[0].wait()
-    output = RoundScatter(out_part, inbox2, outbox2, second2, ss2, rs2, passed2, sp2)
-    output.near_all()
-    output.far_first()
     spread = []
-    for bits in range(1, 8):
-        there = in_plane(row, col, bits)
-        copy = push(gwg.at[flip(place, bits)], gwg_in.at[place], sg.at[bits], rg.at[bits], there)
+    for bits in range(1, 16):
+        there = (row, flip(col, bits))
+        copy = push(slots.at[there[1]], out.at[col], sc.at[bits], rc.at[bits], there)
         copy.start()
         spread.append(copy)
-    gwg_in[place] = gwg[place]
-    for copy in loads[1:]:
+    for copy in loads:
         copy.wait()
     total = LineScatter(part, inbox, outbox, second, ss, rs, passed, sp)
     term = jnp.zeros((1, 1024), f32)
@@ -1462,7 +1431,11 @@
         total.near(chip, bits)
         if bits < 3:
             total.far(bits + 1)
-    output.far_second()
+    for bits in range(1, 8):
+        there = in_plane(row, col, bits)
+        copy = push(gwg.at[flip(place, bits)], gwg_in.at[place], sg.at[bits], rg.at[bits], there)
+        copy.start()
+        spread.append(copy)
     for f in range(8):
         if f == 4:
             total.far_second()
@@ -1470,13 +1443,12 @@
         chunk = mm_tn(lhs, dpn[...]).astype(bf16)
         for j in range(4):
             gq[f // PLANES * 2 + j // 2, f % PLANES * 2 + j % 2] = chunk[j * 32 : j * 32 + 32, :]
-    beside, across = (row, flip(col, 2)), (flip(row, 1), col)
-    columns = [
-        push(gq.at[flip(column, 3)], gqcol.at[1], sv.at[3], rv.at[3], across),
-        push(gq.at[flip(column, 2)], gqcol.at[0], sv.at[2], rv.at[2], across),
-    ]
-    for copy in columns:
+    columns = []
+    for bits in (3, 2, 1):
+        there = (flip(row, bits // 2), flip(col, bits % 2 * 2))
+        copy = push(gq.at[flip(column, bits)], gqcol.at[bits - 1], sv.at[bits], rv.at[bits], there)
         copy.start()
+        columns.append(copy)
     for k in range(8):
         pack[k] = bias_tile[...]
         pack[k, 0:1, :] = term[:, k * 128 : k * 128 + 128]
@@ -1490,26 +1462,6 @@
         copy.start()
         first.append(copy)
     packs[place] = pack[pl.ds(row * PLANES, PLANES)]
-    rows_out = (hidden[...] + output.finish()).astype(bf16)
-    for j in range(16):
-        pieces[j] = rows_out[j * 8 : j * 8 + 8, :]
-    for d in range(16):
-        number = 0
-        for j in range(1, 16):
-            number = jnp.where(deal[j] == d, j, number)
-        slots[d] = pieces[number]
-    for bits in range(1, 16):
-        there = (row, flip(col, bits))
-        copy = push(slots.at[there[1]], out.at[col], sc.at[bits], rc.at[bits], there)
-        copy.start()
-        spread.append(copy)
-    out[col] = slots[col]
-    columns[0].wait_recv()
-    nearby = flip(column, 1)
-    for m in range(MEMBERS):
-        gqout[m] = (gq[nearby, m].astype(f32) + gqcol[1, m].astype(f32)).astype(bf16)
-    columns.append(push(gqout, gqcol.at[2], sv.at[1], rv.at[1], beside))
-    columns[2].start()
     for copy in first:
         copy.wait_recv()
     summed = packs[0]
@@ -1523,11 +1475,12 @@
         copy.start()
         spread.append(copy)
     sums[z] = packed[z]
-    for copy in columns[1:]:
+    for copy in columns:
         copy.wait_recv()
     for m in range(MEMBERS):
         gqsum[m] = (
-            (gq[column, m].astype(f32) + gqcol[0, m].astype(f32)) + gqcol[2, m].astype(f32)
+            (gq[column, m].astype(f32) + gqcol[0, m].astype(f32))
+            + (gqcol[1, m].astype(f32) + gqcol[2, m].astype(f32))
         ).astype(bf16)
     for bits in range(7, 0, -1):
         there = in_line(row, col, bits)
@@ -1565,12 +1518,11 @@
     for copy in list(copies.values()) + columns + first + spread:
         copy.wait_send()
     total.close()
-    output.close()
 
 
 def finish_body(
     grad_tokens_in, gqin, goin, out_in, gwg, gwd, tiles,
-    out, grad_tokens, grad_q, grad_o, grad_gu, grad_d, grad_gains, grad_bias,
+    out, grad_tokens, grad_q, grad_o, grad_gu, grad_d, grad_one, grad_two, grad_bias,
 ):
     grad_tokens[...] = grad_tokens_in[...]
     out[...] = out_in[...]
@@ -1596,7 +1548,8 @@
     chosen = jnp.zeros((2, 32), f32)
     for k in range(4):
         chosen = chosen + jnp.where(quarter == k, total[0:2, k * 32 : k * 32 + 32], 0.0)
-    grad_gains[...] = chosen
+    grad_one[...] = chosen[0]
+    grad_two[...] = chosen[1]
     grad_bias[...] = total[2:4, 0:16]
 
 
@@ -1758,18 +1711,21 @@
         gwg.reshape(1024, 1024), "col", scatter_dimension=0, tiled=True, axis_index_groups=lines
     )
 
-    grad, gwo = kernel(
+    grad, gwo, rows_out = kernel(
         attended_back_body,
         "attended_back",
-        [VM] * 3,
-        [sds((64, 2048), bf16), sds((128, 1024), bf16)],
+        [VM, VM, VM, ANY, VM],
+        [sds((64, 2048), bf16), sds((128, 1024), bf16), sds((rows, width), bf16)],
         [
+            pltpu.VMEM((8, rows, width), bf16),
+            dma(1),
             pltpu.VMEM((8, rows, width), bf16),
             pltpu.VMEM((128, 1024), bf16),
             dma(8), dma(8), dma(4), dma(4),
-        ],
+        ]
+        + scatter_scratch(rows, width),
         number=4,
-    )(d_branch, wop, atp)
+    )(d_branch, wop, atp, out_part, hidden)
 
     dproj, bias_tile = kernel(
         attend_back_body,
@@ -1791,7 +1747,7 @@
     grad_tokens, gqin, goin, gwg_in, sums, out = kernel(
         last_body,
         "last",
-        [VM] + [ANY] * 4 + [VM] * 7 + [SM],
+        [VM] + [ANY] * 3 + [VM] * 7 + [SM],
         [
             sds((rows, width), bf16),
             sds((8, 32, 384), bf16),
@@ -1804,16 +1760,14 @@
             pltpu.VMEM((384, 1024), bf16),
             pltpu.VMEM((8, rows, width), bf16),
             pltpu.VMEM((8, rows, width), bf16),
-            pltpu.VMEM((8, rows, width), bf16),
             pltpu.VMEM((16, 8, width), bf16),
             pltpu.VMEM((16, 8, width), bf16),
-            dma(4),
+            dma(3),
             pltpu.VMEM((2, 192, 1024), bf16),
             pltpu.VMEM((1024, 384), bf16),
             pltpu.VMEM((8, rows, width), bf16),
             pltpu.VMEM((4, 8, 32, 384), bf16),
             pltpu.VMEM((3, 8, 32, 384), bf16),
-            pltpu.VMEM((8, 32, 384), bf16),
             pltpu.VMEM((8, 32, 384), bf16),
             pltpu.VMEM((8, 8, 128), f32),
             pltpu.VMEM((8, 4, 8, 128), f32),
@@ -1823,15 +1777,13 @@
         ]
         + scatter_scratch(rows, width)
         + [dma(2), dma(8), dma(8), dma(4), dma(4), dma(8), dma(8), dma(4), dma(4)]
-        + [dma(4), dma(4), dma(8), dma(8), dma(16), dma(16)]
-        + [pltpu.VMEM((rows, width), bf16), dma(2)]
-        + scatter_scratch(rows, width),
+        + [dma(4), dma(4), dma(8), dma(8), dma(16), dma(16)],
         number=5,
     )(
-        dproj, wt, s1, xp, out_part, gains, d_hidden, hidden, gwo.reshape(4, 32, 1024),
+        dproj, wt, s1, xp, gains, d_hidden, rows_out, gwo.reshape(4, 32, 1024),
         gate_up_sum.reshape(8, 32, 1024), gain_two, bias_tile, target,
     )
-    out, grad_tokens, grad_q, grad_o, grad_gate_up, grad_down, gain_grads, bias_grads = kernel(
+    out, grad_tokens, grad_q, grad_o, grad_gate_up, grad_down, gain_one, gain_two_grad, bias_grads = kernel(
         finish_body,
         "finish",
         [VM] * 7,
@@ -1842,7 +1794,8 @@
             sds((32, 1024), f32),
             sds((32, 8192), f32),
             sds((rows, width), f32),
-            sds((2, 32), f32),
+            sds((32,), f32),
+            sds((32,), f32),
             sds((2, 16), f32),
         ],
         [],
@@ -1857,8 +1810,8 @@
         grad_o,
         grad_gate_up,
         grad_down,
-        gain_grads[0],
-        gain_grads[1],
+        gain_one,
+        gain_two_grad,
         bias_grads,
     )
 

time: 264 us -> 262 us (level)
  waiting for transfers between devices: 21.9 us -> 11.7 us
  Pallas kernels: 226 us -> 236 us
    reduce_scatter x1, waiting for transfers between devices: 12.2 us -> 2.26 us  [plane_shards(): lax.psum_scatter(gwg.reshape(1024, 1024), 'col', scatter_dimension=0, til...]
    pallas_call x2, Pallas kernels: 79.9 us -> 88.7 us  [the longest x1 48.5 us: plane_shards(): kernel(last_body, 'last', [VM] + [ANY] * 3 + [VM] * 7 + [SM], [sds((rows,...]
  transfers between devices with their start and end apart: 2 -> 2, of which waited for: 2 -> 2; matrix products, arithmetic and copies ran while one was open for 0% -> 0% of each run, Pallas kernels for 32% -> 36%
where the time goes in v6:
time: 262 us
  Pallas kernels  236 us (90%)
  between operations  14.1 us (5%)
  waiting for transfers between devices  11.7 us (4%)
    pallas_call x1, Pallas kernels, plane_shards(): kernel(last_body, 'last', [VM] + [ANY] * 3 + [VM] * 7 + [SM], [sds((rows,...  48.5 us
    pallas_call x1, Pallas kernels, plane_shards(): kernel(ffn_body, 'ffn', [VM, ANY, ANY, VM, VM, VM], [sds((8, rows, width)...  44.8 us
    pallas_call x1, Pallas kernels, plane_shards(): kernel(enter_body, 'enter', [VM] * 9 + [SM, SM, VM], [sds((8, rows, width...  44.5 us
    pallas_call x1, Pallas kernels, plane_shards(): kernel(attended_back_body, 'attended_back', [VM, VM, VM, ANY, VM], [sds((...  40.2 us
    pallas_call x1, Pallas kernels, plane_shards(): kernel(branch_body, 'branch', [VM] * 5, [sds((128, 1024), bf16), sds((row...  34.9 us
    pallas_call x1, Pallas kernels, plane_shards(): kernel(attend_back_body, 'attend_back', [VM] * 8, [sds((192, 2048), bf16)...  11.6 us
    all_gather x1, waiting for transfers between devices, plane_shards(): lax.all_gather(wgp.reshape(256, 1024), 'col', axis=0, tiled=True, axis_in...  9.37 us
    pallas_call x1, Pallas kernels, plane_shards(): kernel(attend_body, 'attend', [SM, VM, VM], [sds((64, wide), f32), sds((8...  7.94 us
  transfers between devices with their start and end apart: 2, of which 2 were waited for; matrix products, arithmetic and copies ran while one was open for 0% of the time, Pallas kernels for 36%

profile of v6, /device:TPU:0, one launch (start us, length us, event | category | flops | bytes accessed | tf_op | source)
XLA Modules:
  0.0 261.6 jit_solution(13370501784856639496)
XLA Ops:
  7.2 0.0 all-gather.2.cloned.1.call-start
  7.2 44.5 %enter.1 = (bf16[8,128,1024]{2,1,0:T(8,128)(2,1)}, bf16[384,1024]{1,0:T(8,128)(2,1)}, bf16[4,32,1024]{2,1,0:T(8,128)(2,1)}, bf16[8,32,1024]{2,1,0:T(8,128)(2,1)}...) custom-call(bf16[128,1024]{1,0:T(8,128)(2,1)} %x.3, ...), custom_call_target="tpu_custom_call" | custom-call | tf_op jit(solution)/shard_map/enter/pallas_call | solution.py:1589
  51.8 0.0 all-gather.2.cloned.1.call-update
  51.8 0.0 reduce-scatter.2.cloned.1.call-start
  51.9 7.9 %attend.1 = (f32[64,2560]{1,0:T(8,128)}, f32[8,2560]{1,0:T(8,128)}, bf16[64,2560]{1,0:T(8,128)(2,1)}, bf16[128,2560]{1,0:T(8,128)(2,1)}, bf16[2048,128]{1,0:T(8,128)(2,1)}) custom-call(f32[2,16]{1,0:T(2,128)} %bias_all.1, bf16[192,2048]{1,0:T(8,128)(2,1)} %get-tuple-element.44.qkvt, f32[8,2048]{1,0:T(8,128)} %get-tuple-element.45.labels), custom_call_target="tpu_custom_call" | custom-call | flops 2000000000 | bytes 6666666 | tf_op jit(solution)/shard_map/attend/pallas_call | solution.py:1637
  59.8 34.9 %branch.1 = (bf16[128,1024]{1,0:T(8,128)(2,1)}, f32[128,1024]{1,0:T(8,128)}, bf16[128,1024]{1,0:T(8,128)(2,1)}, bf16[8,128,1024]{2,1,0:T(8,128)(2,1)}) custom-call(bf16[64,2560]{1,0:T(8,128)(2,1)} %get-tuple-element.48.low, bf16[128,1024]{1,0:T(8,128)(2,1)} %bitcast.14, bf16[128,1024]{1,0:T(8,128)(2,1)} %x.3, f32[8,1024]{1,0:T(8,128)} %get-tuple-element.50.gains, ...), custom_call_target="tpu_custom_call" | custom-call | tf_op jit(solution)/shard_map/branch/pallas_call | solution.py:1652
  94.7 9.4 %all-gather.2.cloned.1.call-done = bf16[1024,1024]{1,0:T(8,128)(2,1)} async-done(((bf16[256,1024]{1,0:T(8,128)(2,1)}), bf16[1024,1024]{1,0:T(8,128)(2,1)}) %all-gather.2.cloned.1.call-update) | async-done | bytes 2097168 | tf_op jit(solution)/shard_map/all_gather | solution.py:1631
  104.1 44.8 %ffn.1 = (bf16[8,128,1024]{2,1,0:T(8,128)(2,1)}, bf16[4,128,1024]{2,1,0:T(8,128)(2,1)}, bf16[8,128,1024]{2,1,0:T(8,128)(2,1)}, f32[128,1024]{1,0:T(8,128)}, bf16...) custom-call(bf16[128,1024]{1,0:T(8,128)(2,1)} %get-tuple-element.52.s2, bf16[8,128,1024]{2,1,0:T(8,128)(2,1)} %get-tuple-element.53.cotp_in, ...), custom_call_target="tpu_custom_call" | custom-call | flops 10000000000 | bytes 33333332 | tf_op jit(solution)/shard_map/ffn/pallas_call | solution.py:1674
  148.9 0.0 reduce-scatter.2.cloned.1.call-update
  148.9 40.2 %attended_back.1 = (bf16[64,2048]{1,0:T(8,128)(2,1)}, bf16[128,1024]{1,0:T(8,128)(2,1)}, bf16[128,1024]{1,0:T(8,128)(2,1)}) custom-call(bf16[128,1024]{1,0:T(8,128)(2,1)} %get-tuple-element.56.low, bf16[128,1024]{1,0:T(8,128)(2,1)} %bitcast.15, bf16[128,1024]{1,0:T(8,128)(2,1)} %get-tuple-element.57.atp, bf16[8,128,1024]{2,1,0:T(8,128)(2,1)} %get-tuple-element.58.out_in, ...), custom_call_target="tpu_custom_call" | custom-call | tf_op jit(solution)/shard_map/attended_back/pallas_call | solution.py:1714
  189.2 11.6 %attend_back.1 = (bf16[192,2048]{1,0:T(8,128)(2,1)}, f32[8,128]{1,0:T(8,128)}) custom-call(bf16[192,2048]{1,0:T(8,128)(2,1)} %get-tuple-element.44.qkvt, bf16[128,2560]{1,0:T(8,128)(2,1)} %get-tuple-element.46.qa, bf16[2048,128]{1,0:T(8,128)(2,1)} %get-tuple-element.47.ka, f32[8,2048]{1,0:T(8,128)} %get-tuple-element.45.labels, f32[32,1]{1,0:T(8,128)} %constant.2.clone.freq, ...), custom_call_target="tpu_custom_call" | custom-call | flops 5000000000 | bytes 16666666 | tf_op jit(solution)/shard_map/attend_back/pallas_call | solution.py:1730
  200.8 2.3 reduce-scatter.2.cloned.1.call-done
  203.0 48.5 %last.1 = (bf16[128,1024]{1,0:T(8,128)(2,1)}, bf16[8,32,384]{2,1,0:T(8,128)(2,1)}, bf16[4,32,1024]{2,1,0:T(8,128)(2,1)}, bf16[8,32,1024]{2,1,0:T(8,128)(2,1)}, f...) custom-call(bf16[192,2048]{1,0:T(8,128)(2,1)} %get-tuple-element.62.dproj, bf16[384,1024]{1,0:T(8,128)(2,1)} %get-tuple-element.63.wt_in, ...), custom_call_target="tpu_custom_call" | custom-call | tf_op jit(solution)/shard_map/last/pallas_call | solution.py:1747
  251.5 3.3 %finish.1 = (bf16[128,1024]{1,0:T(8,128)(2,1)}, bf16[128,1024]{1,0:T(8,128)(2,1)}, f32[32,3072]{1,0:T(8,128)}, f32[32,1024]{1,0:T(8,128)}, f32[32,8192]{1,0:T(8,...) custom-call(bf16[128,1024]{1,0:T(8,128)(2,1)} %get-tuple-element.72.grad_tokens_in, ...), custom_call_target="tpu_custom_call" | custom-call | tf_op jit(solution)/shard_map/finish/pallas_call | solution.py:1786
Async XLA Ops:
  7.2 96.9 %all-gather.2.cloned.1.call-start = ((), (), s32[]{:S(2)}) async-start(), calls=%async_computation.1 | async-start | bytes 2621440 | tf_op jit(solution)/shard_map/all_gather | solution.py:1631
  51.8 151.2 %reduce-scatter.2.cloned.1.call-start = ((), (), s32[]{:S(2)}) async-start(), calls=%async_computation.2 | async-start | bytes 2621440 | tf_op jit(solution)/shard_map/reduce_scatter | solution.py:1710
Sparse Core Ops, SparseCore 0:
  51.9 52.1 all-gather.1
  149.0 53.9 reduce-scatter.1

commit v7 on v6

--- a/solution.py
+++ b/solution.py
@@ -750,10 +750,6 @@
     ways[2].start()
     for copy in second:
         copy.wait_recv()
-    rows_in.forward(4)
-    rows_in.forward(2)
-    for copy in ways[1:]:
-        copy.wait_recv()
     for k in range(8):
         lanes = slice(k * 128, k * 128 + 128)
         r, plane = k // PLANES, k % PLANES
@@ -761,25 +757,37 @@
             tiles[r * QUAD + 2, plane] + tiles[r * QUAD + 3, plane]
         )
         times[:, lanes] = tiles[row * QUAD + y * 2 + k % 2, k // 2]
-        wt[:, lanes] = jnp.transpose(
-            jnp.concatenate(
-                [wqp[r * 2 + j // 2, plane * 2 + j % 2] for j in range(4)], axis=0
-            )
-        )
     for k in range(16):
         labels[:, k * 128 : k * 128 + 128] = tiles[row * QUAD + k % QUAD, k // QUAD]
     phases = times[3:4, :] * freq[...]
     cs[...] = jnp.cos(phases)
     sn[...] = jnp.sin(phases)
     gain = gains[0:1, :]
-    kept = [fetch(wt, wt_out, keep.at[2])]
-
-    def project(chip):
-        rows = block(chip, 256)
+
+    def scale(chip):
         values = jnp.concatenate([xp[2 * chip], xp[2 * chip + 1]], axis=0).astype(f32)
         scaled = (values * norm_scale(values) * gain).astype(bf16)
         s1[2 * chip] = scaled[0:128]
         s1[2 * chip + 1] = scaled[128:256]
+
+    rows_in.arrived(0)
+    scale(z)
+    rows_in.forward(4)
+    rows_in.forward(2)
+    for copy in ways[1:]:
+        copy.wait_recv()
+    for k in range(8):
+        r, plane = k // PLANES, k % PLANES
+        wt[:, k * 128 : k * 128 + 128] = jnp.transpose(
+            jnp.concatenate(
+                [wqp[r * 2 + j // 2, plane * 2 + j % 2] for j in range(4)], axis=0
+            )
+        )
+    kept = [fetch(wt, wt_out, keep.at[2])]
+
+    def project(chip):
+        rows = block(chip, 256)
+        scaled = jnp.concatenate([s1[2 * chip], s1[2 * chip + 1]], axis=0)
         out = mm_nt(wt[...], scaled)
         cos_part, sin_part = cs[:, rows], sn[:, rows]
         for head in range(2):
@@ -819,8 +827,10 @@
     for k, bits in enumerate((0, 4, 2, 6)):
         if bits == 6:
             rows_in.forward(6)
-        rows_in.arrived(bits)
         chip = flip(z, bits // 2)
+        if bits:
+            rows_in.arrived(bits)
+            scale(chip)
         project(chip)
         exchange(chip, k)
         if bits == 2:
@@ -879,15 +889,29 @@
     return high, middle, (value - high - middle).astype(bf16).astype(f32)
 
 
-def window_queries(qa, lanes, first, limit):
-    place = first + lax.broadcasted_iota(jnp.int32, (16, WINDOW), 1)
-    line = lax.broadcasted_iota(jnp.int32, (16, WINDOW), 0)
+def window_queries(qa, lanes, first, limit, width):
+    place = first + lax.broadcasted_iota(jnp.int32, (16, width), 1)
+    line = lax.broadcasted_iota(jnp.int32, (16, width), 0)
     extra = jnp.where(
         jnp.logical_and(line == 12, place >= limit), -1e30, qa[64:80, lanes].astype(f32)
     )
     return jnp.concatenate(
-        [qa[0:64, lanes], extra.astype(bf16), jnp.zeros((AUG - 80, WINDOW), bf16)], axis=0
-    )
+        [qa[0:64, lanes], extra.astype(bf16), jnp.zeros((AUG - 80, width), bf16)], axis=0
+    )
+
+
+def over_windows(start, length, window):
+    wide = (length + 1) // 4
+
+    def step(j, unused):
+        window((start + 4 * j) * 128, WINDOW)
+        return unused
+
+    lax.fori_loop(0, wide, step, 0)
+
+    @pl.when(4 * wide < length)
+    def _():
+        window((start + 4 * wide) * 128, WINDOW // 2)
 
 
 def head_of():
@@ -944,10 +968,9 @@
         length = info[number]
         limit = (start + length) * 128
 
-        def window(j, unused):
-            first = (start + 4 * j) * 128
-            lanes = pl.ds(pl.multiple_of(first, 128), WINDOW)
-            queries = window_queries(qa, lanes, first, limit)
+        def window(first, width):
+            lanes = pl.ds(pl.multiple_of(first, 128), width)
+            queries = window_queries(qa, lanes, first, limit, width)
 
             def keys(first_key, count, running):
                 total, numerator = running
@@ -958,15 +981,14 @@
                 return total, numerator
 
             total, numerator = over_keys(
-                start, length, keys, (jnp.zeros((1, WINDOW), f32), jnp.zeros((64, WINDOW), f32))
+                start, length, keys, (jnp.zeros((1, width), f32), jnp.zeros((64, width), f32))
             )
             attended = numerator / total
             att[:, lanes] = attended
-            den[:, lanes] = jnp.broadcast_to(total, (8, WINDOW))
+            den[:, lanes] = jnp.broadcast_to(total, (8, width))
             low[:, lanes] = attended.astype(bf16)
-            return unused
-
-        lax.fori_loop(0, (length + 3) // 4, window, 0)
+
+        over_windows(start, length, window)
         return start + length
 
     lax.fori_loop(0, NSEQ, sequence, 0)
@@ -997,10 +1019,9 @@
         length = info[number]
         limit = (start + length) * 128
 
-        def window(j, unused):
-            first = (start + 4 * j) * 128
-            lanes = pl.ds(pl.multiple_of(first, 128), WINDOW)
-            queries = window_queries(qa, lanes, first, limit)
+        def window(first, width):
+            lanes = pl.ds(pl.multiple_of(first, 128), width)
+            queries = window_queries(qa, lanes, first, limit, width)
             upstream = dn[:, lanes]
             centre = cw[0:1, lanes]
 
@@ -1013,10 +1034,9 @@
                 dv[:, rows] += mm_nt(upstream, weights.astype(bf16))
                 return running + mm(qkvt[64:128, rows], rounded)
 
-            dq[:, lanes] = over_keys(start, length, keys, jnp.zeros((64, WINDOW), f32))
-            return unused
-
-        lax.fori_loop(0, (length + 3) // 4, window, 0)
+            dq[:, lanes] = over_keys(start, length, keys, jnp.zeros((64, width), f32))
+
+        over_windows(start, length, window)
         return start + length
 
     lax.fori_loop(0, NSEQ, sequence, 0)
@@ -1157,7 +1177,7 @@
         if k:
             rows_in.forward(2 * k)
         rows_in.arrived(2 * k)
-        if k == 1:
+        if k == 2:
             downs[2].wait_recv()
 
             @pl.when(inner)
@@ -1216,7 +1236,14 @@
         total.near(chip, k)
         if k > 1:
             total.far(k - 1)
-        if k == 1:
+    for k in range(4):
+        chip = flip(place // 2, k)
+        tile = mm(inner_s[block(chip, 256), :], wd[...]).astype(bf16)
+        out_part[2 * chip] = tile[0:128]
+        out_part[2 * chip + 1] = tile[128:256]
+        if k == 0:
+            total.far(3)
+        if k == 0:
 
             @pl.when(inner)
             def _():
@@ -1225,14 +1252,6 @@
                     gwd[flip(z, 2)].astype(f32) + relayed[...].astype(f32)
                 ).astype(bf16)
                 grads[2].start()
-
-    for k in range(4):
-        chip = flip(place // 2, k)
-        tile = mm(inner_s[block(chip, 256), :], wd[...]).astype(bf16)
-        out_part[2 * chip] = tile[0:128]
-        out_part[2 * chip + 1] = tile[128:256]
-        if k == 0:
-            total.far(3)
     kept = [fetch(out_part, out_keep, keep.at[10])]
     for f in range(8):
         cols = slice(f * 128, f * 128 + 128)
@@ -1437,8 +1456,6 @@
         copy.start()
         spread.append(copy)
     for f in range(8):
-        if f == 4:
-            total.far_second()
         lhs = jnp.concatenate([s1[t, :, f * 128 : f * 128 + 128] for t in range(MEMBERS)], axis=0)
         chunk = mm_tn(lhs, dpn[...]).astype(bf16)
         for j in range(4):
@@ -1462,6 +1479,7 @@
         copy.start()
         first.append(copy)
     packs[place] = pack[pl.ds(row * PLANES, PLANES)]
+    total.far_second()
     for copy in first:
         copy.wait_recv()
     summed = packs[0]

time: 262 us -> 257 us (0.981)
  Pallas kernels: 236 us -> 232 us
  transfers between devices with their start and end apart: 2 -> 2, of which waited for: 2 -> 2; matrix products, arithmetic and copies ran while one was open for 0% -> 0% of each run, Pallas kernels for 36% -> 35%
where the time goes in v7:
time: 257 us; the launch traced here: 259 us
  Pallas kernels  232 us (90%)
  between operations  14.1 us (5%)
  waiting for transfers between devices  12.8 us (5%)
    pallas_call x1, Pallas kernels, plane_shards(): kernel(last_body, 'last', [VM] + [ANY] * 3 + [VM] * 7 + [SM], [sds((rows,...  48.5 us
    pallas_call x1, Pallas kernels, plane_shards(): kernel(enter_body, 'enter', [VM] * 9 + [SM, SM, VM], [sds((8, rows, width...  45.1 us
    pallas_call x1, Pallas kernels, plane_shards(): kernel(ffn_body, 'ffn', [VM, ANY, ANY, VM, VM, VM], [sds((8, rows, width)...  43.6 us
    pallas_call x1, Pallas kernels, plane_shards(): kernel(attended_back_body, 'attended_back', [VM, VM, VM, ANY, VM], [sds((...  39 us
    pallas_call x1, Pallas kernels, plane_shards(): kernel(branch_body, 'branch', [VM] * 5, [sds((128, 1024), bf16), sds((row...  34.3 us
    pallas_call x1, Pallas kernels, plane_shards(): kernel(attend_back_body, 'attend_back', [VM] * 8, [sds((192, 2048), bf16)...  10.8 us
    all_gather x1, waiting for transfers between devices, plane_shards(): lax.all_gather(wgp.reshape(256, 1024), 'col', axis=0, tiled=True, axis_in...  9.91 us
    pallas_call x1, Pallas kernels, plane_shards(): kernel(attend_body, 'attend', [SM, VM, VM], [sds((64, wide), f32), sds((8...  7.49 us
  transfers between devices with their start and end apart: 2, of which 2 were waited for; matrix products, arithmetic and copies ran while one was open for 0% of the time, Pallas kernels for 35%

profile of v7, /device:TPU:0, one launch (start us, length us, event | category | flops | bytes accessed | tf_op | source)
XLA Modules:
  0.0 259.0 jit_solution(10861415051769284743)
XLA Ops:
  7.2 0.0 all-gather.2.cloned.1.call-start
  7.2 45.1 %enter.1 = (bf16[8,128,1024]{2,1,0:T(8,128)(2,1)}, bf16[384,1024]{1,0:T(8,128)(2,1)}, bf16[4,32,1024]{2,1,0:T(8,128)(2,1)}, bf16[8,32,1024]{2,1,0:T(8,128)(2,1)}...) custom-call(bf16[128,1024]{1,0:T(8,128)(2,1)} %x.3, ...), custom_call_target="tpu_custom_call" | custom-call | tf_op jit(solution)/shard_map/enter/pallas_call | solution.py:1607
  52.3 0.0 all-gather.2.cloned.1.call-update
  52.3 0.0 reduce-scatter.2.cloned.1.call-start
  52.4 7.5 %attend.1 = (f32[64,2560]{1,0:T(8,128)}, f32[8,2560]{1,0:T(8,128)}, bf16[64,2560]{1,0:T(8,128)(2,1)}, bf16[128,2560]{1,0:T(8,128)(2,1)}, bf16[2048,128]{1,0:T(8,128)(2,1)}) custom-call(f32[2,16]{1,0:T(2,128)} %bias_all.1, bf16[192,2048]{1,0:T(8,128)(2,1)} %get-tuple-element.44.qkvt, f32[8,2048]{1,0:T(8,128)} %get-tuple-element.45.labels), custom_call_target="tpu_custom_call" | custom-call | flops 2000000000 | bytes 6666666 | tf_op jit(solution)/shard_map/attend/pallas_call | solution.py:1655
  59.9 34.3 %branch.1 = (bf16[128,1024]{1,0:T(8,128)(2,1)}, f32[128,1024]{1,0:T(8,128)}, bf16[128,1024]{1,0:T(8,128)(2,1)}, bf16[8,128,1024]{2,1,0:T(8,128)(2,1)}) custom-call(bf16[64,2560]{1,0:T(8,128)(2,1)} %get-tuple-element.48.low, bf16[128,1024]{1,0:T(8,128)(2,1)} %bitcast.14, bf16[128,1024]{1,0:T(8,128)(2,1)} %x.3, f32[8,1024]{1,0:T(8,128)} %get-tuple-element.50.gains, ...), custom_call_target="tpu_custom_call" | custom-call | tf_op jit(solution)/shard_map/branch/pallas_call | solution.py:1670
  94.2 9.9 %all-gather.2.cloned.1.call-done = bf16[1024,1024]{1,0:T(8,128)(2,1)} async-done(((bf16[256,1024]{1,0:T(8,128)(2,1)}), bf16[1024,1024]{1,0:T(8,128)(2,1)}) %all-gather.2.cloned.1.call-update) | async-done | bytes 2097168 | tf_op jit(solution)/shard_map/all_gather | solution.py:1649
  104.1 43.6 %ffn.1 = (bf16[8,128,1024]{2,1,0:T(8,128)(2,1)}, bf16[4,128,1024]{2,1,0:T(8,128)(2,1)}, bf16[8,128,1024]{2,1,0:T(8,128)(2,1)}, f32[128,1024]{1,0:T(8,128)}, bf16...) custom-call(bf16[128,1024]{1,0:T(8,128)(2,1)} %get-tuple-element.52.s2, bf16[8,128,1024]{2,1,0:T(8,128)(2,1)} %get-tuple-element.53.cotp_in, ...), custom_call_target="tpu_custom_call" | custom-call | flops 10000000000 | bytes 33333332 | tf_op jit(solution)/shard_map/ffn/pallas_call | solution.py:1692
  147.7 0.0 reduce-scatter.2.cloned.1.call-update
  147.8 39.0 %attended_back.1 = (bf16[64,2048]{1,0:T(8,128)(2,1)}, bf16[128,1024]{1,0:T(8,128)(2,1)}, bf16[128,1024]{1,0:T(8,128)(2,1)}) custom-call(bf16[128,1024]{1,0:T(8,128)(2,1)} %get-tuple-element.56.low, bf16[128,1024]{1,0:T(8,128)(2,1)} %bitcast.15, bf16[128,1024]{1,0:T(8,128)(2,1)} %get-tuple-element.57.atp, bf16[8,128,1024]{2,1,0:T(8,128)(2,1)} %get-tuple-element.58.out_in, ...), custom_call_target="tpu_custom_call" | custom-call | tf_op jit(solution)/shard_map/attended_back/pallas_call | solution.py:1732
  186.8 10.8 %attend_back.1 = (bf16[192,2048]{1,0:T(8,128)(2,1)}, f32[8,128]{1,0:T(8,128)}) custom-call(bf16[192,2048]{1,0:T(8,128)(2,1)} %get-tuple-element.44.qkvt, bf16[128,2560]{1,0:T(8,128)(2,1)} %get-tuple-element.46.qa, bf16[2048,128]{1,0:T(8,128)(2,1)} %get-tuple-element.47.ka, f32[8,2048]{1,0:T(8,128)} %get-tuple-element.45.labels, f32[32,1]{1,0:T(8,128)} %constant.2.clone.freq, ...), custom_call_target="tpu_custom_call" | custom-call | flops 5000000000 | bytes 16666666 | tf_op jit(solution)/shard_map/attend_back/pallas_call | solution.py:1748
  197.5 2.8 %reduce-scatter.2.cloned.1.call-done = bf16[256,1024]{1,0:T(8,128)(2,1)} async-done(((bf16[1024,1024]{1,0:T(8,128)(2,1)}), bf16[256,1024]{1,0:T(8,128)(2,1)}) %reduce-scatter.2.cloned.1.call-update) | async-done | bytes 524304 | tf_op jit(solution)/shard_map/reduce_scatter | solution.py:1728
  200.4 48.5 %last.1 = (bf16[128,1024]{1,0:T(8,128)(2,1)}, bf16[8,32,384]{2,1,0:T(8,128)(2,1)}, bf16[4,32,1024]{2,1,0:T(8,128)(2,1)}, bf16[8,32,1024]{2,1,0:T(8,128)(2,1)}, f...) custom-call(bf16[192,2048]{1,0:T(8,128)(2,1)} %get-tuple-element.62.dproj, bf16[384,1024]{1,0:T(8,128)(2,1)} %get-tuple-element.63.wt_in, ...), custom_call_target="tpu_custom_call" | custom-call | tf_op jit(solution)/shard_map/last/pallas_call | solution.py:1765
  248.9 3.3 %finish.1 = (bf16[128,1024]{1,0:T(8,128)(2,1)}, bf16[128,1024]{1,0:T(8,128)(2,1)}, f32[32,3072]{1,0:T(8,128)}, f32[32,1024]{1,0:T(8,128)}, f32[32,8192]{1,0:T(8,...) custom-call(bf16[128,1024]{1,0:T(8,128)(2,1)} %get-tuple-element.72.grad_tokens_in, ...), custom_call_target="tpu_custom_call" | custom-call | tf_op jit(solution)/shard_map/finish/pallas_call | solution.py:1804
Async XLA Ops:
  7.2 97.0 %all-gather.2.cloned.1.call-start = ((), (), s32[]{:S(2)}) async-start(), calls=%async_computation.1 | async-start | bytes 2621440 | tf_op jit(solution)/shard_map/all_gather | solution.py:1649
  52.3 148.0 %reduce-scatter.2.cloned.1.call-start = ((), (), s32[]{:S(2)}) async-start(), calls=%async_computation.2 | async-start | bytes 2621440 | tf_op jit(solution)/shard_map/reduce_scatter | solution.py:1728
Sparse Core Ops, SparseCore 0:
  52.5 51.6 all-gather.1
  147.9 52.4 reduce-scatter.1
